TPU v7x, 512 devices: a whole 4x4x16 slice. The times are simulated.
512 devices in a mesh: gz: 64 (over z, x), gy: 8 (over y, core).
Axes of the slice: x: 4, y: 4, z: 16, core: 2. Of those that a mesh axis runs over, the one named last changes fastest.
Arguments:
- fields: float32 [4, 256, 128, 512], P(None, 'gz', 'gy'), may hold values from -4 to 4
- velocity: float32 [2, 256, 128, 512], P(None, 'gz', 'gy'), may hold values from -3 to 3
- face_rate: float32 [256, 128, 512], P('gz', 'gy'), may hold values from 1 to 4
- xy_rate: float32 [4], replicated, may hold values from 0.05 to 0.2
- z_scale: float32 [4], replicated, may hold values from 128 to 512
Outputs:
- advanced: float32 [4, 256, 128, 512], P(None, 'gz', 'gy')
All inputs are finite; a program needn't handle non-finite values.
Results may differ from a plain program's by a relative error of at most 0.0003.
Values sent between devices are 32-bit elements; how exact they have to be, the bound alone decides.
No kernel may reach another device: no remote copies, remote signals or barrier semaphores. Data moves between devices by JAX's collectives and lax.ppermute only.
A program may use at most 64 MiB of HBM per device.

v0:
```python
import jax
import jax.numpy as jnp
from jax import lax
from jax.sharding import PartitionSpec as P

STEPS = 2


def with_halo(block, sides, width):
    for axis, dim in sides:
        count = lax.axis_size(axis)
        forward = [(i, i + 1) for i in range(count - 1)]
        forward.append((count - 1, 0))
        backward = [(target, source) for source, target in forward]
        low = lax.ppermute(
            lax.slice_in_dim(block, block.shape[dim] - width, None, axis=dim), axis, forward
        )
        high = lax.ppermute(lax.slice_in_dim(block, 0, width, axis=dim), axis, backward)
        block = jnp.concatenate([low, block, high], axis=dim)
    return block


def shifted(block, axis, distance):
    devices = range(lax.axis_size(axis))
    route = [(i - distance, i) for i in devices if i - distance in devices]
    return lax.ppermute(block, axis, route)


def tendency(extended, along_x, along_y, spread):
    middle = extended[:, :, 1:-1]
    north = extended[:, :, 2:]
    south = extended[:, :, :-2]
    eastern = jnp.roll(middle, -1, 3)
    western = jnp.roll(middle, 1, 3)
    return spread * (eastern + western + north + south - 4.0 * middle) - 0.5 * (
        along_x * (eastern - western) + along_y * (north - south)
    )


def reduce_step(current, beneath, overhead):
    couple_down = current[0]
    couple_up = current[1]
    pivot = 1.0 - couple_down * beneath[1] - couple_up * overhead[0]
    return jnp.stack(
        [
            -couple_down * beneath[0] / pivot,
            -couple_up * overhead[1] / pivot,
            (current[2] - couple_down * beneath[2] - couple_up * overhead[2]) / pivot,
        ]
    )


def sweep_interior(source, beneath):
    inner_count = source.shape[1] - 1
    nothing = jnp.zeros_like(source[:, 0])
    factor = nothing
    particular = nothing
    below_part = nothing
    above_part = nothing
    stored = []
    for layer_index in range(inner_count):
        face_below = beneath[:, layer_index]
        face_above = beneath[:, layer_index + 1]
        pivot = 1.0 + face_below + face_above + face_below * factor
        particular = (source[:, layer_index] + face_below * particular) / pivot
        below_part = (
            (face_below if layer_index == 0 else nothing) + face_below * below_part
        ) / pivot
        above_part = (
            (face_above if layer_index == inner_count - 1 else nothing) + face_below * above_part
        ) / pivot
        factor = -face_above / pivot
        stored.append((factor, particular, below_part, above_part))
    carried = (nothing, nothing, nothing)
    outcome = []
    for layer_index in reversed(range(inner_count)):
        factor, particular, below_part, above_part = stored[layer_index]
        carried = (
            particular - factor * carried[0],
            below_part - factor * carried[1],
            above_part - factor * carried[2],
        )
        outcome.insert(0, carried)
    return tuple((jnp.stack([record[position] for record in outcome], 1) for position in range(3)))


def on_device(fields, velocity, face_rate, xy_rate, z_scale):
    spread = xy_rate[:, None, None, None]
    present = fields
    for step_index in range(STEPS):
        along_x = velocity[0][None]
        along_y = velocity[1][None]
        extended = with_halo(present, (("gy", 2),), 1)
        sectioned = present + tendency(extended, along_x, along_y, spread)
        extended = with_halo(sectioned, (("gy", 2),), 1)
        explicit = 0.5 * present + 0.5 * (sectioned + tendency(extended, along_x, along_y, spread))
        beneath = z_scale[:, None, None, None] * face_rate[None]
        inner_base, inner_below, inner_above = sweep_interior(explicit, beneath)
        neighbour = shifted(
            jnp.stack([inner_base[:, 0], inner_below[:, 0], inner_above[:, 0], beneath[:, 0]]),
            "gz",
            -1,
        )
        last_below = beneath[:, -1]
        next_flux = neighbour[3]
        pivot = (
            1.0
            + last_below
            + next_flux
            - last_below * inner_above[:, -1]
            - next_flux * neighbour[1]
        )
        system = jnp.stack(
            [
                -last_below * inner_below[:, -1] / pivot,
                -next_flux * neighbour[2] / pivot,
                (explicit[:, -1] + last_below * inner_base[:, -1] + next_flux * neighbour[0])
                / pivot,
            ]
        )
        distance = 1
        while distance < lax.axis_size("gz"):
            from_below = shifted(system, "gz", distance)
            from_above = shifted(system, "gz", -distance)
            system = reduce_step(system, from_below, from_above)
            distance = distance * 2
        separators = system[2]
        separators_below = shifted(separators, "gz", 1)
        inner = (
            inner_base + inner_below * separators_below[:, None] + inner_above * separators[:, None]
        )
        present = jnp.concatenate([inner, separators[:, None]], 1)
    return present


def solution(mesh):
    in_specs = (P(None, "gz", "gy", None), P(None, "gz", "gy", None), P("gz", "gy", None), P(), P())
    out_specs = P(None, "gz", "gy", None)
    return jax.shard_map(
        on_device, mesh=mesh, in_specs=in_specs, out_specs=out_specs, check_vma=False
    )
```

profile of v0, /device:TPU:40, one launch (start us, length us, event | category | flops | bytes accessed | tf_op | source)
XLA Modules:
  0.0 412.9 jit_solution(17089744884990644193)
XLA Ops:
  12.9 4.2 %collective-permute-start.4 = (f32[4,4,16,512]{3,2,1,0:T(8,128)S(1)}, f32[4,4,16,512]{3,2,1,0:T(8,128)S(1)}, u32[]{:S(2)}, u32[]{:S(2)}) collective-permute-start(f32[4,4,16,512]{3,2,1,0:T(8,128)S(1)} %pad_maximum_fusion.2), channel_id=1, source_target_pairs={{8,0},{16,8},{24,16},{32,24},{40,32},{48,40},{56,48},{64,56},{72,6... | collective-permute-start | bytes 1572872 | tf_op jit(solution)/shard_map/ppermute | solution.py:26
  17.1 10.6 %collective-permute-done.4 = f32[4,4,16,512]{3,2,1,0:T(8,128)S(1)} collective-permute-done((f32[4,4,16,512]{3,2,1,0:T(8,128)S(1)}, f32[4,4,16,512]{3,2,1,0:T(8,128)S(1)}, u32[]{:S(2)}, u32[]{:S(2)}) %collective-permute-start.4) | collective-permute-done | bytes 524320 | tf_op jit(solution)/shard_map/ppermute | solution.py:26
  27.8 6.3 %collective-permute-start.6 = (f32[3,4,16,512]{3,2,1,0:T(8,128)S(1)}, f32[3,4,16,512]{3,2,1,0:T(8,128)S(1)}, u32[]{:S(2)}, u32[]{:S(2)}) collective-permute-start(f32[3,4,16,512]{3,2,1,0:T(8,128)S(1)} %pad_maximum_fusion.27), channel_id=1, source_target_pairs={{8,0},{16,8},{24,16},{32,24},{40,32},{48,40},{56,48},{64,56},{72,6... | collective-permute-start | bytes 1179656 | tf_op jit(solution)/shard_map/ppermute | solution.py:26
  36.1 4.8 %collective-permute-done.6 = f32[3,4,16,512]{3,2,1,0:T(8,128)S(1)} collective-permute-done((f32[3,4,16,512]{3,2,1,0:T(8,128)S(1)}, f32[3,4,16,512]{3,2,1,0:T(8,128)S(1)}, u32[]{:S(2)}, u32[]{:S(2)}) %collective-permute-start.6) | collective-permute-done | bytes 393248 | tf_op jit(solution)/shard_map/ppermute | solution.py:26
  40.9 6.2 %collective-permute-done.5 = f32[3,4,16,512]{3,2,1,0:T(8,128)S(1)} collective-permute-done((f32[3,4,16,512]{3,2,1,0:T(8,128)S(1)}, f32[3,4,16,512]{3,2,1,0:T(8,128)S(1)}, u32[]{:S(2)}, u32[]{:S(2)}) %collective-permute-start.5) | collective-permute-done | bytes 393248 | tf_op jit(solution)/shard_map/ppermute | solution.py:26
  49.2 5.4 %collective-permute-start.7 = (f32[3,4,16,512]{3,2,1,0:T(8,128)S(1)}, f32[3,4,16,512]{3,2,1,0:T(8,128)S(1)}, u32[]{:S(2)}, u32[]{:S(2)}) collective-permute-start(f32[3,4,16,512]{3,2,1,0:T(8,128)S(1)} %pad_maximum_fusion.28), channel_id=1, source_target_pairs={{0,16},{8,24},{16,32},{24,40},{32,48},{40,56},{48,64},{56,72},{64,... | collective-permute-start | bytes 1179656 | tf_op jit(solution)/shard_map/ppermute | solution.py:26
  54.6 12.5 %collective-permute-done.8 = f32[3,4,16,512]{3,2,1,0:T(8,128)S(1)} collective-permute-done((f32[3,4,16,512]{3,2,1,0:T(8,128)S(1)}, f32[3,4,16,512]{3,2,1,0:T(8,128)S(1)}, u32[]{:S(2)}, u32[]{:S(2)}) %collective-permute-start.8) | collective-permute-done | bytes 393248 | tf_op jit(solution)/shard_map/ppermute | solution.py:26
  69.3 3.9 collective-permute-start.9
  73.2 4.9 %collective-permute-done.10 = f32[3,4,16,512]{3,2,1,0:T(8,128)S(1)} collective-permute-done((f32[3,4,16,512]{3,2,1,0:T(8,128)S(1)}, f32[3,4,16,512]{3,2,1,0:T(8,128)S(1)}, u32[]{:S(2)}, u32[]{:S(2)}) %collective-permute-start.10) | collective-permute-done | bytes 393248 | tf_op jit(solution)/shard_map/ppermute | solution.py:26
  81.3 9.7 %collective-permute-start.11 = (f32[3,4,16,512]{3,2,1,0:T(8,128)S(1)}, f32[3,4,16,512]{3,2,1,0:T(8,128)S(1)}, u32[]{:S(2)}, u32[]{:S(2)}) collective-permute-start(f32[3,4,16,512]{3,2,1,0:T(8,128)S(1)} %pad_maximum_fusion.30), channel_id=1, source_target_pairs={{0,64},{8,72},{16,80},{24,88},{32,96},{40,104},{48,112},{56,120},{... | collective-permute-start | bytes 1179656 | tf_op jit(solution)/shard_map/ppermute | solution.py:26
  91.0 10.6 %collective-permute-done.12 = f32[3,4,16,512]{3,2,1,0:T(8,128)S(1)} collective-permute-done((f32[3,4,16,512]{3,2,1,0:T(8,128)S(1)}, f32[3,4,16,512]{3,2,1,0:T(8,128)S(1)}, u32[]{:S(2)}, u32[]{:S(2)}) %collective-permute-start.12) | collective-permute-done | bytes 393248 | tf_op jit(solution)/shard_map/ppermute | solution.py:26
  101.6 3.9 collective-permute-done.11
  107.0 9.2 %collective-permute-start.13 = (f32[3,4,16,512]{3,2,1,0:T(8,128)S(1)}, f32[3,4,16,512]{3,2,1,0:T(8,128)S(1)}, u32[]{:S(2)}, u32[]{:S(2)}) collective-permute-start(f32[3,4,16,512]{3,2,1,0:T(8,128)S(1)} %pad_maximum_fusion.31), channel_id=1, source_target_pairs={{0,128},{8,136},{16,144},{24,152},{32,160},{40,168},{48,176},{56,1... | collective-permute-start | bytes 1179656 | tf_op jit(solution)/shard_map/ppermute | solution.py:26
  116.2 25.5 %collective-permute-done.14 = f32[3,4,16,512]{3,2,1,0:T(8,128)S(1)} collective-permute-done((f32[3,4,16,512]{3,2,1,0:T(8,128)S(1)}, f32[3,4,16,512]{3,2,1,0:T(8,128)S(1)}, u32[]{:S(2)}, u32[]{:S(2)}) %collective-permute-start.14) | collective-permute-done | bytes 393248 | tf_op jit(solution)/shard_map/ppermute | solution.py:26
  143.1 21.1 %collective-permute-start.15 = (f32[3,4,16,512]{3,2,1,0:T(8,128)S(1)}, f32[3,4,16,512]{3,2,1,0:T(8,128)S(1)}, u32[]{:S(2)}, u32[]{:S(2)}) collective-permute-start(f32[3,4,16,512]{3,2,1,0:T(8,128)S(1)} %pad_maximum_fusion.32), channel_id=1, source_target_pairs={{0,256},{8,264},{16,272},{24,280},{32,288},{40,296},{48,304},{56,3... | collective-permute-start | bytes 1179656 | tf_op jit(solution)/shard_map/ppermute | solution.py:26
  164.2 16.0 %collective-permute-done.16 = f32[3,4,16,512]{3,2,1,0:T(8,128)S(1)} collective-permute-done((f32[3,4,16,512]{3,2,1,0:T(8,128)S(1)}, f32[3,4,16,512]{3,2,1,0:T(8,128)S(1)}, u32[]{:S(2)}, u32[]{:S(2)}) %collective-permute-start.16) | collective-permute-done | bytes 393248 | tf_op jit(solution)/shard_map/ppermute | solution.py:26
  181.0 4.2 %collective-permute-start.17 = (f32[4,16,512]{2,1,0:T(8,128)S(1)}, f32[4,16,512]{2,1,0:T(8,128)S(1)}, u32[]{:S(2)}, u32[]{:S(2)}) collective-permute-start(f32[4,16,512]{2,1,0:T(8,128)S(1)} %fusion.172), channel_id=1, source_target_pairs={{0,8},{8,16},{16,24},{24,32},{32,40},{40,48},{48,56},{56,64},{64,7... | collective-permute-start | bytes 393224 | tf_op jit(solution)/shard_map/ppermute | solution.py:26
  185.8 23.4 %collective-permute-done.17 = f32[4,16,512]{2,1,0:T(8,128)S(1)} collective-permute-done((f32[4,16,512]{2,1,0:T(8,128)S(1)}, f32[4,16,512]{2,1,0:T(8,128)S(1)}, u32[]{:S(2)}, u32[]{:S(2)}) %collective-permute-start.17) | collective-permute-done | bytes 131104 | tf_op jit(solution)/shard_map/ppermute | solution.py:26
  213.7 5.4 %collective-permute-start.20 = (f32[4,4,1,512]{3,2,0,1:T(1,128)S(1)}, f32[4,4,1,512]{3,2,0,1:T(1,128)S(1)}, u32[]{:S(2)}, u32[]{:S(2)}) collective-permute-start(f32[4,4,1,512]{3,2,0,1:T(1,128)S(1)} %get-tuple-element.78), channel_id=1, source_target_pairs={{1,0},{2,1},{3,2},{4,3},{5,4},{6,5},{7,6},{0,7},{9,8},{10,9},{11,1... | collective-permute-start | bytes 98312 | tf_op jit(solution)/shard_map/ppermute | solution.py:18
  228.7 8.5 %collective-permute-done.22 = f32[4,4,16,512]{3,2,1,0:T(8,128)S(1)} collective-permute-done((f32[4,4,16,512]{3,2,1,0:T(8,128)S(1)}, f32[4,4,16,512]{3,2,1,0:T(8,128)S(1)}, u32[]{:S(2)}, u32[]{:S(2)}) %collective-permute-start.22) | collective-permute-done | bytes 524320 | tf_op jit(solution)/shard_map/ppermute | solution.py:26
  237.4 5.1 %collective-permute-start.24 = (f32[3,4,16,512]{3,2,1,0:T(8,128)S(1)}, f32[3,4,16,512]{3,2,1,0:T(8,128)S(1)}, u32[]{:S(2)}, u32[]{:S(2)}) collective-permute-start(f32[3,4,16,512]{3,2,1,0:T(8,128)S(1)} %pad_maximum_fusion.34), channel_id=1, source_target_pairs={{8,0},{16,8},{24,16},{32,24},{40,32},{48,40},{56,48},{64,56},{72,6... | collective-permute-start | bytes 1179656 | tf_op jit(solution)/shard_map/ppermute | solution.py:26
  244.4 6.9 %collective-permute-done.24 = f32[3,4,16,512]{3,2,1,0:T(8,128)S(1)} collective-permute-done((f32[3,4,16,512]{3,2,1,0:T(8,128)S(1)}, f32[3,4,16,512]{3,2,1,0:T(8,128)S(1)}, u32[]{:S(2)}, u32[]{:S(2)}) %collective-permute-start.24) | collective-permute-done | bytes 393248 | tf_op jit(solution)/shard_map/ppermute | solution.py:26
  256.7 5.4 %collective-permute-start.25 = (f32[3,4,16,512]{3,2,1,0:T(8,128)S(1)}, f32[3,4,16,512]{3,2,1,0:T(8,128)S(1)}, u32[]{:S(2)}, u32[]{:S(2)}) collective-permute-start(f32[3,4,16,512]{3,2,1,0:T(8,128)S(1)} %pad_maximum_fusion.35), channel_id=1, source_target_pairs={{0,16},{8,24},{16,32},{24,40},{32,48},{40,56},{48,64},{56,72},{64,... | collective-permute-start | bytes 1179656 | tf_op jit(solution)/shard_map/ppermute | solution.py:26
  262.2 9.0 %collective-permute-done.26 = f32[3,4,16,512]{3,2,1,0:T(8,128)S(1)} collective-permute-done((f32[3,4,16,512]{3,2,1,0:T(8,128)S(1)}, f32[3,4,16,512]{3,2,1,0:T(8,128)S(1)}, u32[]{:S(2)}, u32[]{:S(2)}) %collective-permute-start.26) | collective-permute-done | bytes 393248 | tf_op jit(solution)/shard_map/ppermute | solution.py:26
  273.2 3.9 collective-permute-start.27
  284.3 11.1 %collective-permute-start.29 = (f32[3,4,16,512]{3,2,1,0:T(8,128)S(1)}, f32[3,4,16,512]{3,2,1,0:T(8,128)S(1)}, u32[]{:S(2)}, u32[]{:S(2)}) collective-permute-start(f32[3,4,16,512]{3,2,1,0:T(8,128)S(1)} %pad_maximum_fusion.37), channel_id=1, source_target_pairs={{0,64},{8,72},{16,80},{24,88},{32,96},{40,104},{48,112},{56,120},{... | collective-permute-start | bytes 1179656 | tf_op jit(solution)/shard_map/ppermute | solution.py:26
  295.4 9.2 %collective-permute-done.30 = f32[3,4,16,512]{3,2,1,0:T(8,128)S(1)} collective-permute-done((f32[3,4,16,512]{3,2,1,0:T(8,128)S(1)}, f32[3,4,16,512]{3,2,1,0:T(8,128)S(1)}, u32[]{:S(2)}, u32[]{:S(2)}) %collective-permute-start.30) | collective-permute-done | bytes 393248 | tf_op jit(solution)/shard_map/ppermute | solution.py:26
  306.3 12.7 %collective-permute-start.31 = (f32[3,4,16,512]{3,2,1,0:T(8,128)S(1)}, f32[3,4,16,512]{3,2,1,0:T(8,128)S(1)}, u32[]{:S(2)}, u32[]{:S(2)}) collective-permute-start(f32[3,4,16,512]{3,2,1,0:T(8,128)S(1)} %pad_maximum_fusion.38), channel_id=1, source_target_pairs={{0,128},{8,136},{16,144},{24,152},{32,160},{40,168},{48,176},{56,1... | collective-permute-start | bytes 1179656 | tf_op jit(solution)/shard_map/ppermute | solution.py:26
  319.1 14.0 %collective-permute-done.32 = f32[3,4,16,512]{3,2,1,0:T(8,128)S(1)} collective-permute-done((f32[3,4,16,512]{3,2,1,0:T(8,128)S(1)}, f32[3,4,16,512]{3,2,1,0:T(8,128)S(1)}, u32[]{:S(2)}, u32[]{:S(2)}) %collective-permute-start.32) | collective-permute-done | bytes 393248 | tf_op jit(solution)/shard_map/ppermute | solution.py:26
  336.0 28.3 %collective-permute-start.33 = (f32[3,4,16,512]{3,2,1,0:T(8,128)S(1)}, f32[3,4,16,512]{3,2,1,0:T(8,128)S(1)}, u32[]{:S(2)}, u32[]{:S(2)}) collective-permute-start(f32[3,4,16,512]{3,2,1,0:T(8,128)S(1)} %pad_maximum_fusion.39), channel_id=1, source_target_pairs={{0,256},{8,264},{16,272},{24,280},{32,288},{40,296},{48,304},{56,3... | collective-permute-start | bytes 1179656 | tf_op jit(solution)/shard_map/ppermute | solution.py:26
  364.4 26.8 %collective-permute-done.34 = f32[3,4,16,512]{3,2,1,0:T(8,128)S(1)} collective-permute-done((f32[3,4,16,512]{3,2,1,0:T(8,128)S(1)}, f32[3,4,16,512]{3,2,1,0:T(8,128)S(1)}, u32[]{:S(2)}, u32[]{:S(2)}) %collective-permute-start.34) | collective-permute-done | bytes 393248 | tf_op jit(solution)/shard_map/ppermute | solution.py:26
  396.2 15.7 %collective-permute-done.35 = f32[4,16,512]{2,1,0:T(8,128)S(1)} collective-permute-done((f32[4,16,512]{2,1,0:T(8,128)S(1)}, f32[4,16,512]{2,1,0:T(8,128)S(1)}, u32[]{:S(2)}, u32[]{:S(2)}) %collective-permute-start.35) | collective-permute-done | bytes 131104 | tf_op jit(solution)/shard_map/ppermute | solution.py:26
  (109 shorter events, 67.8 us)
Async XLA Ops:
  1.1 3.7 collective-permute-start
  7.5 4.2 %collective-permute-start.3 = (f32[4,4,1,512]{3,2,0,1:T(1,128)S(1)}, f32[4,4,1,512]{3,2,0,1:T(1,128)S(1)}, u32[]{:S(2)}, u32[]{:S(2)}) collective-permute-start(f32[4,4,1,512]{3,2,0,1:T(1,128)S(1)} %get-tuple-element.92), channel_id=1, source_target_pairs={{0,1},{1,2},{2,3},{3,4},{4,5},{5,6},{6,7},{7,0},{8,9},{9,10},{10,1... | collective-permute-start | bytes 98312 | tf_op jit(solution)/shard_map/ppermute | solution.py:15
  12.9 14.8 %collective-permute-start.4 = (f32[4,4,16,512]{3,2,1,0:T(8,128)S(1)}, f32[4,4,16,512]{3,2,1,0:T(8,128)S(1)}, u32[]{:S(2)}, u32[]{:S(2)}) collective-permute-start(f32[4,4,16,512]{3,2,1,0:T(8,128)S(1)} %pad_maximum_fusion.2), channel_id=1, source_target_pairs={{8,0},{16,8},{24,16},{32,24},{40,32},{48,40},{56,48},{64,56},{72,6... | collective-permute-start | bytes 1572872 | tf_op jit(solution)/shard_map/ppermute | solution.py:26
  27.8 13.0 %collective-permute-start.6 = (f32[3,4,16,512]{3,2,1,0:T(8,128)S(1)}, f32[3,4,16,512]{3,2,1,0:T(8,128)S(1)}, u32[]{:S(2)}, u32[]{:S(2)}) collective-permute-start(f32[3,4,16,512]{3,2,1,0:T(8,128)S(1)} %pad_maximum_fusion.27), channel_id=1, source_target_pairs={{8,0},{16,8},{24,16},{32,24},{40,32},{48,40},{56,48},{64,56},{72,6... | collective-permute-start | bytes 1179656 | tf_op jit(solution)/shard_map/ppermute | solution.py:26
  34.2 12.9 %collective-permute-start.5 = (f32[3,4,16,512]{3,2,1,0:T(8,128)S(1)}, f32[3,4,16,512]{3,2,1,0:T(8,128)S(1)}, u32[]{:S(2)}, u32[]{:S(2)}) collective-permute-start(f32[3,4,16,512]{3,2,1,0:T(8,128)S(1)} %pad_maximum_fusion.27), channel_id=1, source_target_pairs={{0,8},{8,16},{16,24},{24,32},{32,40},{40,48},{48,56},{56,64},{64,7... | collective-permute-start | bytes 1179656 | tf_op jit(solution)/shard_map/ppermute | solution.py:26
  47.3 19.9 %collective-permute-start.8 = (f32[3,4,16,512]{3,2,1,0:T(8,128)S(1)}, f32[3,4,16,512]{3,2,1,0:T(8,128)S(1)}, u32[]{:S(2)}, u32[]{:S(2)}) collective-permute-start(f32[3,4,16,512]{3,2,1,0:T(8,128)S(1)} %pad_maximum_fusion.28), channel_id=1, source_target_pairs={{16,0},{24,8},{32,16},{40,24},{48,32},{56,40},{64,48},{72,56},{80,... | collective-permute-start | bytes 1179656 | tf_op jit(solution)/shard_map/ppermute | solution.py:26
  49.2 18.0 %collective-permute-start.7 = (f32[3,4,16,512]{3,2,1,0:T(8,128)S(1)}, f32[3,4,16,512]{3,2,1,0:T(8,128)S(1)}, u32[]{:S(2)}, u32[]{:S(2)}) collective-permute-start(f32[3,4,16,512]{3,2,1,0:T(8,128)S(1)} %pad_maximum_fusion.28), channel_id=1, source_target_pairs={{0,16},{8,24},{16,32},{24,40},{32,48},{40,56},{48,64},{56,72},{64,... | collective-permute-start | bytes 1179656 | tf_op jit(solution)/shard_map/ppermute | solution.py:26
  67.3 10.8 %collective-permute-start.10 = (f32[3,4,16,512]{3,2,1,0:T(8,128)S(1)}, f32[3,4,16,512]{3,2,1,0:T(8,128)S(1)}, u32[]{:S(2)}, u32[]{:S(2)}) collective-permute-start(f32[3,4,16,512]{3,2,1,0:T(8,128)S(1)} %pad_maximum_fusion.29), channel_id=1, source_target_pairs={{32,0},{40,8},{48,16},{56,24},{64,32},{72,40},{80,48},{88,56},{96,... | collective-permute-start | bytes 1179656 | tf_op jit(solution)/shard_map/ppermute | solution.py:26
  69.3 10.6 %collective-permute-start.9 = (f32[3,4,16,512]{3,2,1,0:T(8,128)S(1)}, f32[3,4,16,512]{3,2,1,0:T(8,128)S(1)}, u32[]{:S(2)}, u32[]{:S(2)}) collective-permute-start(f32[3,4,16,512]{3,2,1,0:T(8,128)S(1)} %pad_maximum_fusion.29), channel_id=1, source_target_pairs={{0,32},{8,40},{16,48},{24,56},{32,64},{40,72},{48,80},{56,88},{64,... | collective-permute-start | bytes 1179656 | tf_op jit(solution)/shard_map/ppermute | solution.py:26
  80.0 21.6 %collective-permute-start.12 = (f32[3,4,16,512]{3,2,1,0:T(8,128)S(1)}, f32[3,4,16,512]{3,2,1,0:T(8,128)S(1)}, u32[]{:S(2)}, u32[]{:S(2)}) collective-permute-start(f32[3,4,16,512]{3,2,1,0:T(8,128)S(1)} %pad_maximum_fusion.30), channel_id=1, source_target_pairs={{64,0},{72,8},{80,16},{88,24},{96,32},{104,40},{112,48},{120,56},{... | collective-permute-start | bytes 1179656 | tf_op jit(solution)/shard_map/ppermute | solution.py:26
  81.3 24.2 %collective-permute-start.11 = (f32[3,4,16,512]{3,2,1,0:T(8,128)S(1)}, f32[3,4,16,512]{3,2,1,0:T(8,128)S(1)}, u32[]{:S(2)}, u32[]{:S(2)}) collective-permute-start(f32[3,4,16,512]{3,2,1,0:T(8,128)S(1)} %pad_maximum_fusion.30), channel_id=1, source_target_pairs={{0,64},{8,72},{16,80},{24,88},{32,96},{40,104},{48,112},{56,120},{... | collective-permute-start | bytes 1179656 | tf_op jit(solution)/shard_map/ppermute | solution.py:26
  105.7 36.0 %collective-permute-start.14 = (f32[3,4,16,512]{3,2,1,0:T(8,128)S(1)}, f32[3,4,16,512]{3,2,1,0:T(8,128)S(1)}, u32[]{:S(2)}, u32[]{:S(2)}) collective-permute-start(f32[3,4,16,512]{3,2,1,0:T(8,128)S(1)} %pad_maximum_fusion.31), channel_id=1, source_target_pairs={{128,0},{136,8},{144,16},{152,24},{160,32},{168,40},{176,48},{184,... | collective-permute-start | bytes 1179656 | tf_op jit(solution)/shard_map/ppermute | solution.py:26
  107.0 34.7 %collective-permute-start.13 = (f32[3,4,16,512]{3,2,1,0:T(8,128)S(1)}, f32[3,4,16,512]{3,2,1,0:T(8,128)S(1)}, u32[]{:S(2)}, u32[]{:S(2)}) collective-permute-start(f32[3,4,16,512]{3,2,1,0:T(8,128)S(1)} %pad_maximum_fusion.31), channel_id=1, source_target_pairs={{0,128},{8,136},{16,144},{24,152},{32,160},{40,168},{48,176},{56,1... | collective-permute-start | bytes 1179656 | tf_op jit(solution)/shard_map/ppermute | solution.py:26
  141.8 38.4 %collective-permute-start.16 = (f32[3,4,16,512]{3,2,1,0:T(8,128)S(1)}, f32[3,4,16,512]{3,2,1,0:T(8,128)S(1)}, u32[]{:S(2)}, u32[]{:S(2)}) collective-permute-start(f32[3,4,16,512]{3,2,1,0:T(8,128)S(1)} %pad_maximum_fusion.32), channel_id=1, source_target_pairs={{256,0},{264,8},{272,16},{280,24},{288,32},{296,40},{304,48},{312,... | collective-permute-start | bytes 1179656 | tf_op jit(solution)/shard_map/ppermute | solution.py:26
  143.1 37.1 %collective-permute-start.15 = (f32[3,4,16,512]{3,2,1,0:T(8,128)S(1)}, f32[3,4,16,512]{3,2,1,0:T(8,128)S(1)}, u32[]{:S(2)}, u32[]{:S(2)}) collective-permute-start(f32[3,4,16,512]{3,2,1,0:T(8,128)S(1)} %pad_maximum_fusion.32), channel_id=1, source_target_pairs={{0,256},{8,264},{16,272},{24,280},{32,288},{40,296},{48,304},{56,3... | collective-permute-start | bytes 1179656 | tf_op jit(solution)/shard_map/ppermute | solution.py:26
  181.0 28.2 %collective-permute-start.17 = (f32[4,16,512]{2,1,0:T(8,128)S(1)}, f32[4,16,512]{2,1,0:T(8,128)S(1)}, u32[]{:S(2)}, u32[]{:S(2)}) collective-permute-start(f32[4,16,512]{2,1,0:T(8,128)S(1)} %fusion.172), channel_id=1, source_target_pairs={{0,8},{8,16},{16,24},{24,32},{32,40},{40,48},{48,56},{56,64},{64,7... | collective-permute-start | bytes 393224 | tf_op jit(solution)/shard_map/ppermute | solution.py:26
  213.7 7.0 %collective-permute-start.20 = (f32[4,4,1,512]{3,2,0,1:T(1,128)S(1)}, f32[4,4,1,512]{3,2,0,1:T(1,128)S(1)}, u32[]{:S(2)}, u32[]{:S(2)}) collective-permute-start(f32[4,4,1,512]{3,2,0,1:T(1,128)S(1)} %get-tuple-element.78), channel_id=1, source_target_pairs={{1,0},{2,1},{3,2},{4,3},{5,4},{6,5},{7,6},{0,7},{9,8},{10,9},{11,1... | collective-permute-start | bytes 98312 | tf_op jit(solution)/shard_map/ppermute | solution.py:18
  219.2 5.4 %collective-permute-start.21 = (f32[4,4,1,512]{3,2,0,1:T(1,128)S(1)}, f32[4,4,1,512]{3,2,0,1:T(1,128)S(1)}, u32[]{:S(2)}, u32[]{:S(2)}) collective-permute-start(f32[4,4,1,512]{3,2,0,1:T(1,128)S(1)} %get-tuple-element.79), channel_id=1, source_target_pairs={{0,1},{1,2},{2,3},{3,4},{4,5},{5,6},{6,7},{7,0},{8,9},{9,10},{10,1... | collective-permute-start | bytes 98312 | tf_op jit(solution)/shard_map/ppermute | solution.py:15
  225.3 11.9 %collective-permute-start.22 = (f32[4,4,16,512]{3,2,1,0:T(8,128)S(1)}, f32[4,4,16,512]{3,2,1,0:T(8,128)S(1)}, u32[]{:S(2)}, u32[]{:S(2)}) collective-permute-start(f32[4,4,16,512]{3,2,1,0:T(8,128)S(1)} %pad_maximum_fusion.1), channel_id=1, source_target_pairs={{8,0},{16,8},{24,16},{32,24},{40,32},{48,40},{56,48},{64,56},{72,6... | collective-permute-start | bytes 1572872 | tf_op jit(solution)/shard_map/ppermute | solution.py:26
  237.4 13.9 %collective-permute-start.24 = (f32[3,4,16,512]{3,2,1,0:T(8,128)S(1)}, f32[3,4,16,512]{3,2,1,0:T(8,128)S(1)}, u32[]{:S(2)}, u32[]{:S(2)}) collective-permute-start(f32[3,4,16,512]{3,2,1,0:T(8,128)S(1)} %pad_maximum_fusion.34), channel_id=1, source_target_pairs={{8,0},{16,8},{24,16},{32,24},{40,32},{48,40},{56,48},{64,56},{72,6... | collective-permute-start | bytes 1179656 | tf_op jit(solution)/shard_map/ppermute | solution.py:26
  242.5 12.2 %collective-permute-start.23 = (f32[3,4,16,512]{3,2,1,0:T(8,128)S(1)}, f32[3,4,16,512]{3,2,1,0:T(8,128)S(1)}, u32[]{:S(2)}, u32[]{:S(2)}) collective-permute-start(f32[3,4,16,512]{3,2,1,0:T(8,128)S(1)} %pad_maximum_fusion.34), channel_id=1, source_target_pairs={{0,8},{8,16},{16,24},{24,32},{32,40},{40,48},{48,56},{56,64},{64,7... | collective-permute-start | bytes 1179656 | tf_op jit(solution)/shard_map/ppermute | solution.py:26
  254.8 16.3 %collective-permute-start.26 = (f32[3,4,16,512]{3,2,1,0:T(8,128)S(1)}, f32[3,4,16,512]{3,2,1,0:T(8,128)S(1)}, u32[]{:S(2)}, u32[]{:S(2)}) collective-permute-start(f32[3,4,16,512]{3,2,1,0:T(8,128)S(1)} %pad_maximum_fusion.35), channel_id=1, source_target_pairs={{16,0},{24,8},{32,16},{40,24},{48,32},{56,40},{64,48},{72,56},{80,... | collective-permute-start | bytes 1179656 | tf_op jit(solution)/shard_map/ppermute | solution.py:26
  256.7 14.4 %collective-permute-start.25 = (f32[3,4,16,512]{3,2,1,0:T(8,128)S(1)}, f32[3,4,16,512]{3,2,1,0:T(8,128)S(1)}, u32[]{:S(2)}, u32[]{:S(2)}) collective-permute-start(f32[3,4,16,512]{3,2,1,0:T(8,128)S(1)} %pad_maximum_fusion.35), channel_id=1, source_target_pairs={{0,16},{8,24},{16,32},{24,40},{32,48},{40,56},{48,64},{56,72},{64,... | collective-permute-start | bytes 1179656 | tf_op jit(solution)/shard_map/ppermute | solution.py:26
  271.3 9.7 %collective-permute-start.28 = (f32[3,4,16,512]{3,2,1,0:T(8,128)S(1)}, f32[3,4,16,512]{3,2,1,0:T(8,128)S(1)}, u32[]{:S(2)}, u32[]{:S(2)}) collective-permute-start(f32[3,4,16,512]{3,2,1,0:T(8,128)S(1)} %pad_maximum_fusion.36), channel_id=1, source_target_pairs={{32,0},{40,8},{48,16},{56,24},{64,32},{72,40},{80,48},{88,56},{96,... | collective-permute-start | bytes 1179656 | tf_op jit(solution)/shard_map/ppermute | solution.py:26
  273.2 9.7 %collective-permute-start.27 = (f32[3,4,16,512]{3,2,1,0:T(8,128)S(1)}, f32[3,4,16,512]{3,2,1,0:T(8,128)S(1)}, u32[]{:S(2)}, u32[]{:S(2)}) collective-permute-start(f32[3,4,16,512]{3,2,1,0:T(8,128)S(1)} %pad_maximum_fusion.36), channel_id=1, source_target_pairs={{0,32},{8,40},{16,48},{24,56},{32,64},{40,72},{48,80},{56,88},{64,... | collective-permute-start | bytes 1179656 | tf_op jit(solution)/shard_map/ppermute | solution.py:26
  283.0 21.6 %collective-permute-start.30 = (f32[3,4,16,512]{3,2,1,0:T(8,128)S(1)}, f32[3,4,16,512]{3,2,1,0:T(8,128)S(1)}, u32[]{:S(2)}, u32[]{:S(2)}) collective-permute-start(f32[3,4,16,512]{3,2,1,0:T(8,128)S(1)} %pad_maximum_fusion.37), channel_id=1, source_target_pairs={{64,0},{72,8},{80,16},{88,24},{96,32},{104,40},{112,48},{120,56},{... | collective-permute-start | bytes 1179656 | tf_op jit(solution)/shard_map/ppermute | solution.py:26
  284.3 20.5 %collective-permute-start.29 = (f32[3,4,16,512]{3,2,1,0:T(8,128)S(1)}, f32[3,4,16,512]{3,2,1,0:T(8,128)S(1)}, u32[]{:S(2)}, u32[]{:S(2)}) collective-permute-start(f32[3,4,16,512]{3,2,1,0:T(8,128)S(1)} %pad_maximum_fusion.37), channel_id=1, source_target_pairs={{0,64},{8,72},{16,80},{24,88},{32,96},{40,104},{48,112},{56,120},{... | collective-permute-start | bytes 1179656 | tf_op jit(solution)/shard_map/ppermute | solution.py:26
  305.0 28.1 %collective-permute-start.32 = (f32[3,4,16,512]{3,2,1,0:T(8,128)S(1)}, f32[3,4,16,512]{3,2,1,0:T(8,128)S(1)}, u32[]{:S(2)}, u32[]{:S(2)}) collective-permute-start(f32[3,4,16,512]{3,2,1,0:T(8,128)S(1)} %pad_maximum_fusion.38), channel_id=1, source_target_pairs={{128,0},{136,8},{144,16},{152,24},{160,32},{168,40},{176,48},{184,... | collective-permute-start | bytes 1179656 | tf_op jit(solution)/shard_map/ppermute | solution.py:26
  306.3 28.2 %collective-permute-start.31 = (f32[3,4,16,512]{3,2,1,0:T(8,128)S(1)}, f32[3,4,16,512]{3,2,1,0:T(8,128)S(1)}, u32[]{:S(2)}, u32[]{:S(2)}) collective-permute-start(f32[3,4,16,512]{3,2,1,0:T(8,128)S(1)} %pad_maximum_fusion.38), channel_id=1, source_target_pairs={{0,128},{8,136},{16,144},{24,152},{32,160},{40,168},{48,176},{56,1... | collective-permute-start | bytes 1179656 | tf_op jit(solution)/shard_map/ppermute | solution.py:26
  334.7 56.5 %collective-permute-start.34 = (f32[3,4,16,512]{3,2,1,0:T(8,128)S(1)}, f32[3,4,16,512]{3,2,1,0:T(8,128)S(1)}, u32[]{:S(2)}, u32[]{:S(2)}) collective-permute-start(f32[3,4,16,512]{3,2,1,0:T(8,128)S(1)} %pad_maximum_fusion.39), channel_id=1, source_target_pairs={{256,0},{264,8},{272,16},{280,24},{288,32},{296,40},{304,48},{312,... | collective-permute-start | bytes 1179656 | tf_op jit(solution)/shard_map/ppermute | solution.py:26
  336.0 56.9 %collective-permute-start.33 = (f32[3,4,16,512]{3,2,1,0:T(8,128)S(1)}, f32[3,4,16,512]{3,2,1,0:T(8,128)S(1)}, u32[]{:S(2)}, u32[]{:S(2)}) collective-permute-start(f32[3,4,16,512]{3,2,1,0:T(8,128)S(1)} %pad_maximum_fusion.39), channel_id=1, source_target_pairs={{0,256},{8,264},{16,272},{24,280},{32,288},{40,296},{48,304},{56,3... | collective-permute-start | bytes 1179656 | tf_op jit(solution)/shard_map/ppermute | solution.py:26
  393.6 18.3 %collective-permute-start.35 = (f32[4,16,512]{2,1,0:T(8,128)S(1)}, f32[4,16,512]{2,1,0:T(8,128)S(1)}, u32[]{:S(2)}, u32[]{:S(2)}) collective-permute-start(f32[4,16,512]{2,1,0:T(8,128)S(1)} %fusion.79), channel_id=1, source_target_pairs={{0,8},{8,16},{16,24},{24,32},{32,40},{40,48},{48,56},{56,64},{64,7... | collective-permute-start | bytes 393224 | tf_op jit(solution)/shard_map/ppermute | solution.py:26
  (9 other events, 17.6 us)
where the time goes:
time: 414 us; the launch traced here: 413 us
  waiting for transfers between devices  235 us (57%)
  starting transfers between devices  163 us (39%)
  other arithmetic  9.25 us (2%)
  local copies, waits for them, and re-layouts  5.3 us (1%)
    ppermute x28, waiting for transfers between devices, shifted(): return lax.ppermute(block, axis, route)  223 us
    ppermute x28, starting transfers between devices, shifted(): return lax.ppermute(block, axis, route)  155 us
  transfers between devices with their start and end apart: 36, of which 30 were waited for; matrix products, arithmetic and copies ran while one was open for 1% of the time, Pallas kernels for 0%

commit v1 on v0

v1 whole, which is shorter than its diff:
```python
import functools

import jax
import jax.numpy as jnp
from jax import lax
from jax.experimental import pallas as pl
from jax.experimental.pallas import tpu as pltpu
from jax.sharding import PartitionSpec as P

FIELDS = 4
LEVELS = 4
ROWS = 16
WIDTH = 512
LANES = 128
BLOCKS = 64
HALF = BLOCKS // 2
COLUMNS = WIDTH // LANES


def tendency(middle, half_x, half_y, spread):
    rows = middle.shape[0]
    eastern = pltpu.roll(middle, WIDTH - 1, 1)
    western = pltpu.roll(middle, 1, 1)
    north = pltpu.roll(middle, rows - 1, 0)
    south = pltpu.roll(middle, 1, 0)
    return spread * (eastern + western + north + south - 4.0 * middle) - (
        half_x * (eastern - western) + half_y * (north - south)
    )


def inner_pivots(rates):
    hold = 1.0 + rates[0]
    inverse = []
    for level in range(LEVELS - 1):
        once = 1.0 / (hold + rates[level + 1])
        inverse.append(once)
        hold = 1.0 + rates[level + 1] * hold * once
    return inverse


def solve_inner(source, rates, inverse):
    first = source[0]
    second = source[1] + rates[1] * inverse[0] * first
    third = (source[2] + rates[2] * inverse[1] * second) * inverse[2]
    second = (second + rates[2] * third) * inverse[1]
    first = (first + rates[1] * second) * inverse[0]
    return first, second, third


def explicit_kernel(chunk, xy_ref, zs_ref, present_ref, south_ref, north_ref, vel_ref, vel_south_ref,
                    vel_north_ref, face_ref, explicit_ref, send_ref, tail_ref, vel_tail_ref):
    tail_ref[:, 0:2, :] = north_ref[...]
    tail_ref[:, 6:8, :] = south_ref[...]
    vel_tail_ref[:, 0:1, :] = vel_north_ref[...]
    vel_tail_ref[:, 7:8, :] = vel_south_ref[...]
    for level in range(LEVELS):
        half_x = 0.5 * jnp.concatenate([vel_ref[level], vel_tail_ref[level]], 0)
        half_y = 0.5 * jnp.concatenate([vel_ref[LEVELS + level], vel_tail_ref[LEVELS + level]], 0)
        for field in range(FIELDS):
            item = field * LEVELS + level
            spread = xy_ref[field]
            middle = jnp.concatenate([present_ref[item], tail_ref[item]], 0)
            sectioned = middle + tendency(middle, half_x, half_y, spread)
            again = sectioned + tendency(sectioned, half_x, half_y, spread)
            explicit_ref[item] = (0.5 * middle + 0.5 * again)[:ROWS]
    for tile in range(ROWS // 8):
        rows = slice(tile * 8, tile * 8 + 8)
        for field in range(FIELDS):
            scale = zs_ref[field]
            rates = [scale * face_ref[level, rows, :] for level in range(LEVELS)]
            source = [explicit_ref[field * LEVELS + level, rows, :] for level in range(LEVELS)]
            first, _, third = solve_inner(source, rates, inner_pivots(rates))
            own = source[3] + rates[3] * third
            under = rates[0] * first
            for column in range(COLUMNS):
                lanes = slice(column * LANES, column * LANES + LANES)
                start = (tile * 8 * COLUMNS + column) * chunk
                send_ref[pl.ds(start + field, 8, stride=COLUMNS * chunk), :] = own[:, lanes]
                send_ref[pl.ds(start + FIELDS + field, 8, stride=COLUMNS * chunk), :] = under[:, lanes]
        if chunk > 8:
            for level in range(LEVELS):
                for column in range(COLUMNS):
                    lanes = slice(column * LANES, column * LANES + LANES)
                    start = (tile * 8 * COLUMNS + column) * chunk
                    send_ref[pl.ds(start + 8 + level, 8, stride=COLUMNS * chunk), :] = face_ref[level, rows, lanes]


def swap(value):
    return pltpu.roll(value, 4, 0)


def lower_half():
    return lax.broadcasted_iota(jnp.int32, (8, LANES), 0) < 4


def factor_kernel(got_ref, zs_ref, weight_ref, gain_ref):
    low = lower_half()
    scale = zs_ref[...]
    couple, own, under = [], [], []
    for step in range(HALF):
        rates = [
            scale
            * jnp.where(
                low,
                jnp.broadcast_to(got_ref[step, 8 + level : 9 + level, :], (8, LANES)),
                jnp.broadcast_to(got_ref[BLOCKS - 1 - step, 8 + level : 9 + level, :], (8, LANES)),
            )
            for level in range(LEVELS)
        ]
        inverse = inner_pivots(rates)
        one = jnp.ones((8, LANES), jnp.float32)
        first, _, third = solve_inner([one, one, one], rates, inverse)
        own.append(1.0 + rates[3] * third)
        under.append(rates[0] * first)
        couple.append(rates[0] * inverse[0] * rates[1] * inverse[1] * rates[2] * inverse[2] * rates[3])
    zero = jnp.zeros((8, LANES), jnp.float32)
    hold = None
    for step in range(HALF):
        last = step == HALF - 1
        below = swap(under[step]) if last else under[step + 1]
        above = zero if step == 0 else under[step - 1]
        mass = own[step] + jnp.where(low, below, above)
        hold = mass + (jnp.where(low, couple[0], zero) if step == 0 else hold * gain)
        inward = jnp.where(low, swap(couple[step]) if last else couple[step + 1], couple[step])
        if last:
            other = swap(hold)
            inverse = 1.0 / (hold * other + inward * (hold + other))
            weight_ref[step] = (other + inward) * inverse
            gain_ref[step] = inward * inverse
        else:
            weight = 1.0 / (hold + inward)
            gain = inward * weight
            weight_ref[step] = weight
            gain_ref[step] = gain


def separator_kernel(got_ref, weight_ref, gain_ref, back_ref):
    low = lower_half()

    def side(block):
        value = got_ref[block, 0:8, :]
        if block + 1 < BLOCKS:
            return value + swap(got_ref[block + 1, 0:8, :])
        return jnp.where(low, value, 0.0)

    value = None
    kept = []
    for step in range(HALF):
        source = jnp.where(low, side(step), swap(side(BLOCKS - 1 - step)))
        value = source if step == 0 else source + gain_ref[step - 1] * value
        kept.append(value)
    value = weight_ref[HALF - 1] * value + gain_ref[HALF - 1] * swap(value)
    back_ref[HALF] = value
    for step in reversed(range(HALF)):
        inner = value
        turned = swap(inner)
        if step > 0:
            value = weight_ref[step - 1] * kept[step - 1] + gain_ref[step - 1] * inner
            back_ref[step] = jnp.where(low, value, turned)
            back_ref[BLOCKS - step] = jnp.where(low, turned, value)
        else:
            back_ref[0] = jnp.where(low, 0.0, turned)


def finish_kernel(edges, zs_ref, explicit_ref, face_ref, back_ref, present_ref, *edge_refs):
    for tile in range(ROWS // 8):
        rows = slice(tile * 8, tile * 8 + 8)
        for field in range(FIELDS):
            scale = zs_ref[field]
            rates = [scale * face_ref[level, rows, :] for level in range(LEVELS)]
            source = [explicit_ref[field * LEVELS + level, rows, :] for level in range(LEVELS - 1)]
            below, top = [], []
            for column in range(COLUMNS):
                start = (tile * 8 * COLUMNS + column) * 8
                below.append(back_ref[pl.ds(start + field, 8, stride=COLUMNS * 8), :])
                top.append(back_ref[pl.ds(start + FIELDS + field, 8, stride=COLUMNS * 8), :])
            below = jnp.concatenate(below, 1)
            top = jnp.concatenate(top, 1)
            source[0] = source[0] + rates[0] * below
            source[2] = source[2] + rates[3] * top
            solved = solve_inner(source, rates, inner_pivots(rates)) + (top,)
            for level in range(LEVELS):
                item = field * LEVELS + level
                present_ref[item, rows, :] = solved[level]
                if edges and tile == 0:
                    edge_refs[0][item] = solved[level][0:2]
                if edges and tile == 1:
                    edge_refs[1][item] = solved[level][6:8]


VMEM = pl.BlockSpec(memory_space=pltpu.VMEM)
SMEM = pl.BlockSpec(memory_space=pltpu.SMEM)


def struct(*shape):
    return jax.ShapeDtypeStruct(shape, jnp.float32)


def explicit_part(chunk, *operands):
    return pl.pallas_call(
        functools.partial(explicit_kernel, chunk),
        out_shape=(struct(FIELDS * LEVELS, ROWS, WIDTH), struct(BLOCKS * chunk, LANES)),
        in_specs=[SMEM, SMEM] + [VMEM] * 7,
        out_specs=(VMEM, VMEM),
        scratch_shapes=[
            pltpu.VMEM((FIELDS * LEVELS, 8, WIDTH), jnp.float32),
            pltpu.VMEM((2 * LEVELS, 8, WIDTH), jnp.float32),
        ],
        name="explicit_part",
    )(*operands)


def factor_part(got, scale):
    return pl.pallas_call(
        factor_kernel,
        out_shape=(struct(HALF, 8, LANES), struct(HALF, 8, LANES)),
        in_specs=[VMEM, VMEM],
        out_specs=(VMEM, VMEM),
        name="factor_part",
    )(got, scale)


def separator_part(got, weight, gain):
    return pl.pallas_call(
        separator_kernel,
        out_shape=struct(BLOCKS, 8, LANES),
        in_specs=[VMEM] * 3,
        out_specs=VMEM,
        name="separator_part",
    )(got, weight, gain)


def finish_part(edges, *operands):
    shapes = [struct(FIELDS * LEVELS, ROWS, WIDTH)]
    if edges:
        shapes += [struct(FIELDS * LEVELS, 2, WIDTH)] * 2
    return pl.pallas_call(
        functools.partial(finish_kernel, edges),
        out_shape=tuple(shapes),
        in_specs=[SMEM] + [VMEM] * 3,
        out_specs=(VMEM,) * len(shapes),
        name="finish_part",
    )(*operands)


def on_device(fields, velocity, face_rate, xy_rate, z_scale):
    count = lax.axis_size("gy")
    up = [(i, (i + 1) % count) for i in range(count)]
    down = [(target, source) for source, target in up]
    present = fields.reshape(FIELDS * LEVELS, ROWS, WIDTH)
    vel = velocity.reshape(2 * LEVELS, ROWS, WIDTH)
    scale = jnp.broadcast_to(jnp.tile(z_scale, 2)[:, None], (8, LANES))

    lowest = jnp.concatenate([present[:, 0:2].reshape(-1, WIDTH), vel[:, 0]], 0)
    highest = jnp.concatenate([present[:, ROWS - 2 :].reshape(-1, WIDTH), vel[:, ROWS - 1]], 0)
    south = lax.ppermute(highest, "gy", up)
    north = lax.ppermute(lowest, "gy", down)
    cut = 2 * FIELDS * LEVELS
    vel_south, vel_north = south[cut:, None], north[cut:, None]
    south = south[:cut].reshape(-1, 2, WIDTH)
    north = north[:cut].reshape(-1, 2, WIDTH)

    def swap_over(chunks):
        return lax.all_to_all(chunks, "gz", 0, 0, tiled=True)

    explicit, send = explicit_part(
        16, xy_rate, z_scale, present, south, north, vel, vel_south, vel_north, face_rate
    )
    got = swap_over(send.reshape(BLOCKS, 16, LANES))
    weight, gain = factor_part(got, scale)
    back = swap_over(separator_part(got, weight, gain))
    present, lowest, highest = finish_part(
        True, z_scale, explicit, face_rate, back.reshape(BLOCKS * 8, LANES)
    )
    south = lax.ppermute(highest, "gy", up)
    north = lax.ppermute(lowest, "gy", down)
    explicit, send = explicit_part(
        8, xy_rate, z_scale, present, south, north, vel, vel_south, vel_north, face_rate
    )
    got = swap_over(send.reshape(BLOCKS, 8, LANES))
    back = swap_over(separator_part(got, weight, gain))
    (present,) = finish_part(False, z_scale, explicit, face_rate, back.reshape(BLOCKS * 8, LANES))
    return present.reshape(fields.shape)


def solution(mesh):
    in_specs = (P(None, "gz", "gy", None), P(None, "gz", "gy", None), P("gz", "gy", None), P(), P())
    out_specs = P(None, "gz", "gy", None)
    return jax.shard_map(
        on_device, mesh=mesh, in_specs=in_specs, out_specs=out_specs, check_vma=False
    )
```

time: 414 us -> 171 us (0.41)
  the two profiles are of different devices: /device:TPU:40 before, /device:TPU:24 now
where the time goes in v1:
time: 171 us; the launch traced here: 170 us
  blocking collectives  85.2 us (50%)
  waiting for transfers between devices  38.9 us (23%)
  starting transfers between devices  20.8 us (12%)
  Pallas kernels  18.9 us (11%)
  local copies, waits for them, and re-layouts  6.22 us (4%)
    all_to_all x3, blocking collectives, swap_over(): return lax.all_to_all(chunks, 'gz', 0, 0, tiled=True)  85.2 us
    all_to_all x1, waiting for transfers between devices, swap_over(): return lax.all_to_all(chunks, 'gz', 0, 0, tiled=True)  33.2 us
    all_to_all x1, starting transfers between devices, swap_over(): return lax.all_to_all(chunks, 'gz', 0, 0, tiled=True)  17.3 us
    pallas_call x2, Pallas kernels, explicit_part(): pl.pallas_call(functools.partial(explicit_kernel, chunk), out_shape=(stru...  8.38 us
    pallas_call x2, Pallas kernels, finish_part(): pl.pallas_call(functools.partial(finish_kernel, edges), out_shape=tuple(s...  4.48 us
    ppermute x2, waiting for transfers between devices, on_device(): south = lax.ppermute(highest, 'gy', up)  4.19 us
    pallas_call x2, Pallas kernels, separator_part(): pl.pallas_call(separator_kernel, out_shape=struct(BLOCKS, 8, LANES), in_s...  3.87 us
    ppermute x2, starting transfers between devices, on_device(): north = lax.ppermute(lowest, 'gy', down)  3.47 us
  transfers between devices with their start and end apart: 5, of which 5 were waited for; matrix products, arithmetic and copies ran while one was open for 1% of the time, Pallas kernels for 0%

profile of v1, /device:TPU:24, one launch (start us, length us, event | category | flops | bytes accessed | tf_op | source)
XLA Modules:
  0.0 170.1 jit_solution(11538009145640194595)
XLA Ops:
  0.0 1.0 fusion.1
  1.0 1.1 fusion
  2.2 0.0 collective-permute-start
  2.3 1.7 %collective-permute-start.1 = (f32[40,512]{1,0:T(8,128)S(1)}, f32[40,512]{1,0:T(8,128)S(1)}, u32[]{:S(2)}, u32[]{:S(2)}) collective-permute-start(f32[40,512]{1,0:T(8,128)S(1)} %pad_maximum_fusion.1), channel_id=1, source_target_pairs={{1,0},{2,1},{3,2},{4,3},{5,4},{6,5},{7,6},{0,7},{9,8},{10,9},{11,1... | collective-permute-start | bytes 245768 | tf_op jit(solution)/shard_map/ppermute | solution.py:257
  4.0 2.0 %collective-permute-done = f32[40,512]{1,0:T(8,128)S(1)} collective-permute-done((f32[40,512]{1,0:T(8,128)S(1)}, f32[40,512]{1,0:T(8,128)S(1)}, u32[]{:S(2)}, u32[]{:S(2)}) %collective-permute-start) | collective-permute-done | bytes 81952 | tf_op jit(solution)/shard_map/ppermute | solution.py:256
  6.0 0.6 broadcast_in_dim.13.vel_south_ref
  6.7 0.7 reshape.38.south_ref
  7.3 1.4 collective-permute-done.1
  8.7 0.6 broadcast_in_dim.14.vel_north_ref
  9.3 0.7 reshape.40.north_ref
  10.0 4.3 %explicit_part.2 = (f32[16,16,512]{2,1,0:T(8,128)}, f32[1024,128]{1,0:T(8,128)}) custom-call(f32[4]{0:T(128)} %xy_ref.3, f32[4]{0:T(128)} %zs_ref.7, f32[16,16,512]{2,1,0:T(8,128)} %bitcast.19, f32[16,2,512]{2,1,0:T(2,128)} %reshape.38.south_ref, f32[16,2,512]{2,1,0:T(2,128)} %reshape.40.north_ref, f32[8,16,512]{2,1,0:T(8,128)} %bitcast.14, ...), custom_call_target="tpu_custom_call" | custom-call | tf_op jit(solution)/shard_map/explicit_part/pallas_call | solution.py:200
  14.3 17.3 %all-to-all-start = ((f32[64,16,128]{2,1,0:T(8,128)}), f32[64,16,128]{2,1,0:T(8,128)S(1)}, u32[]{:S(2)}, u32[]{:S(2)}) async-start(f32[64,16,128]{2,1,0:T(8,128)} %bitcast.20), calls=%async_computation | async-start | bytes 1048576 | tf_op jit(solution)/shard_map/all_to_all | solution.py:264
  31.6 0.0 copy-done.3
  31.6 0.1 broadcast_in_dim.15
  31.7 33.2 %all-to-all-done.got_ref = f32[64,16,128]{2,1,0:T(8,128)S(1)} async-done(((f32[64,16,128]{2,1,0:T(8,128)}), f32[64,16,128]{2,1,0:T(8,128)S(1)}, u32[]{:S(2)}, u32[]{:S(2)}) %all-to-all-start) | async-done | bytes 524320 | tf_op jit(solution)/shard_map/all_to_all | solution.py:264
  64.9 0.7 broadcast_in_dim.16.zs_ref
  65.6 0.1 copy-done
  65.7 2.1 %factor_part.1 = (f32[32,8,128]{2,1,0:T(8,128)}, f32[32,8,128]{2,1,0:T(8,128)}) custom-call(f32[64,16,128]{2,1,0:T(8,128)} %copy-done, f32[8,128]{1,0:T(8,128)} %broadcast_in_dim.16.zs_ref), custom_call_target="tpu_custom_call" | custom-call | tf_op jit(solution)/shard_map/factor_part/pallas_call | solution.py:214
  67.8 2.0 %separator_part.2 = f32[64,8,128]{2,1,0:T(8,128)} custom-call(f32[64,16,128]{2,1,0:T(8,128)} %copy-done, f32[32,8,128]{2,1,0:T(8,128)} %get-tuple-element.16.weight_ref, f32[32,8,128]{2,1,0:T(8,128)} %get-tuple-element.17.gain_ref), custom_call_target="tpu_custom_call" | custom-call | tf_op jit(solution)/shard_map/separator_part/pallas_call | solution.py:224
  69.8 28.1 %all_to_all.20 = f32[64,8,128]{2,1,0:T(8,128)} all-to-all(f32[64,8,128]{2,1,0:T(8,128)} %separator_part.2), channel_id=1, replica_groups=mesh['gz'=64,'gy'=8] {'gz'}, dimensions={0} | all-to-all | bytes 524288 | tf_op jit(solution)/shard_map/all_to_all | solution.py:264
  98.0 2.3 %finish_part.2 = (f32[16,16,512]{2,1,0:T(8,128)}, f32[16,2,512]{2,1,0:T(2,128)}, f32[16,2,512]{2,1,0:T(2,128)}) custom-call(f32[4]{0:T(128)} %zs_ref.7, f32[16,16,512]{2,1,0:T(8,128)} %get-tuple-element.14.explicit_ref, f32[4,16,512]{2,1,0:T(8,128)} %face_ref.7, f32[512,128]{1,0:T(8,128)} %bitcast.16), custom_call_target="tpu_custom_call" | custom-call | tf_op jit(solution)/shard_map/finish_part/pallas_call | solution.py:237
  100.2 0.0 collective-permute-start.2
  100.2 1.7 %collective-permute-start.3 = (f32[16,2,512]{2,1,0:T(2,128)}, f32[16,2,512]{2,1,0:T(2,128)S(1)}, u32[]{:S(2)}, u32[]{:S(2)}) collective-permute-start(f32[16,2,512]{2,1,0:T(2,128)} %get-tuple-element.20), channel_id=1, source_target_pairs={{1,0},{2,1},{3,2},{4,3},{5,4},{6,5},{7,6},{0,7},{9,8},{10,9},{11,1... | collective-permute-start | bytes 196616 | tf_op jit(solution)/shard_map/ppermute | solution.py:276
  102.0 2.2 %collective-permute-done.2.south_ref = f32[16,2,512]{2,1,0:T(2,128)S(1)} collective-permute-done((f32[16,2,512]{2,1,0:T(2,128)}, f32[16,2,512]{2,1,0:T(2,128)S(1)}, u32[]{:S(2)}, u32[]{:S(2)}) %collective-permute-start.2) | collective-permute-done | bytes 65568 | tf_op jit(solution)/shard_map/ppermute | solution.py:275
  104.1 0.1 collective-permute-done.3.north_ref
  104.2 0.5 copy-done.1
  104.7 0.1 copy-done.2
  104.8 4.1 %explicit_part.3 = (f32[16,16,512]{2,1,0:T(8,128)}, f32[512,128]{1,0:T(8,128)}) custom-call(f32[4]{0:T(128)} %xy_ref.3, f32[4]{0:T(128)} %zs_ref.7, f32[16,16,512]{2,1,0:T(8,128)} %get-tuple-element.18.present_ref, f32[16,2,512]{2,1,0:T(2,128)} %copy-done.1, f32[16,2,512]{2,1,0:T(2,128)} %copy-done.2, f32[8,16,512]{2,1,0:T(8,128)} %bitcast.15, ...), custom_call_target="tpu_custom_call" | custom-call | tf_op jit(solution)/shard_map/explicit_part/pallas_call | solution.py:200
  108.9 27.8 %all_to_all.21.got_ref = f32[64,8,128]{2,1,0:T(8,128)} all-to-all(f32[64,8,128]{2,1,0:T(8,128)} %bitcast.21), channel_id=1, replica_groups=mesh['gz'=64,'gy'=8] {'gz'}, dimensions={0} | all-to-all | bytes 524288 | tf_op jit(solution)/shard_map/all_to_all | solution.py:264
  136.7 1.9 %separator_part.3 = f32[64,8,128]{2,1,0:T(8,128)} custom-call(f32[64,8,128]{2,1,0:T(8,128)} %all_to_all.21.got_ref, f32[32,8,128]{2,1,0:T(8,128)} %get-tuple-element.16.weight_ref, f32[32,8,128]{2,1,0:T(8,128)} %get-tuple-element.17.gain_ref), custom_call_target="tpu_custom_call" | custom-call | tf_op jit(solution)/shard_map/separator_part/pallas_call | solution.py:224
  138.6 29.3 %all_to_all.22 = f32[64,8,128]{2,1,0:T(8,128)} all-to-all(f32[64,8,128]{2,1,0:T(8,128)} %separator_part.3), channel_id=1, replica_groups=mesh['gz'=64,'gy'=8] {'gz'}, dimensions={0} | all-to-all | bytes 524288 | tf_op jit(solution)/shard_map/all_to_all | solution.py:264
  167.8 2.2 %finish_part.3 = f32[16,16,512]{2,1,0:T(8,128)} custom-call(f32[4]{0:T(128)} %zs_ref.7, f32[16,16,512]{2,1,0:T(8,128)} %get-tuple-element.21.explicit_ref, f32[4,16,512]{2,1,0:T(8,128)} %face_ref.7, f32[512,128]{1,0:T(8,128)} %bitcast.17), custom_call_target="tpu_custom_call" | custom-call | tf_op jit(solution)/shard_map/finish_part/pallas_call | solution.py:237
  (15 shorter events, 0.1 us)
Async XLA Ops:
  2.2 3.9 %collective-permute-start = (f32[40,512]{1,0:T(8,128)S(1)}, f32[40,512]{1,0:T(8,128)S(1)}, u32[]{:S(2)}, u32[]{:S(2)}) collective-permute-start(f32[40,512]{1,0:T(8,128)S(1)} %pad_maximum_fusion), channel_id=1, source_target_pairs={{0,1},{1,2},{2,3},{3,4},{4,5},{5,6},{6,7},{7,0},{8,9},{9,10},{10,1... | collective-permute-start | bytes 245768 | tf_op jit(solution)/shard_map/ppermute | solution.py:256
  2.3 6.4 %collective-permute-start.1 = (f32[40,512]{1,0:T(8,128)S(1)}, f32[40,512]{1,0:T(8,128)S(1)}, u32[]{:S(2)}, u32[]{:S(2)}) collective-permute-start(f32[40,512]{1,0:T(8,128)S(1)} %pad_maximum_fusion.1), channel_id=1, source_target_pairs={{1,0},{2,1},{3,2},{4,3},{5,4},{6,5},{7,6},{0,7},{9,8},{10,9},{11,1... | collective-permute-start | bytes 245768 | tf_op jit(solution)/shard_map/ppermute | solution.py:257
  14.3 17.3 %copy-start.3 = (f32[4]{0:T(128)S(1)}, f32[4]{0:T(128)}, u32[]{:S(2)}) copy-start(f32[4]{0:T(128)} %zs_ref.7) | copy-start | bytes 52
  14.3 50.6 %all-to-all-start = ((f32[64,16,128]{2,1,0:T(8,128)}), f32[64,16,128]{2,1,0:T(8,128)S(1)}, u32[]{:S(2)}, u32[]{:S(2)}) async-start(f32[64,16,128]{2,1,0:T(8,128)} %bitcast.20), calls=%async_computation | async-start | bytes 1048576 | tf_op jit(solution)/shard_map/all_to_all | solution.py:264
  64.9 0.8 copy-start
  100.2 3.9 %collective-permute-start.2 = (f32[16,2,512]{2,1,0:T(2,128)}, f32[16,2,512]{2,1,0:T(2,128)S(1)}, u32[]{:S(2)}, u32[]{:S(2)}) collective-permute-start(f32[16,2,512]{2,1,0:T(2,128)} %get-tuple-element.19), channel_id=1, source_target_pairs={{0,1},{1,2},{2,3},{3,4},{4,5},{5,6},{6,7},{7,0},{8,9},{9,10},{10,1... | collective-permute-start | bytes 196616 | tf_op jit(solution)/shard_map/ppermute | solution.py:275
  100.2 4.0 %collective-permute-start.3 = (f32[16,2,512]{2,1,0:T(2,128)}, f32[16,2,512]{2,1,0:T(2,128)S(1)}, u32[]{:S(2)}, u32[]{:S(2)}) collective-permute-start(f32[16,2,512]{2,1,0:T(2,128)} %get-tuple-element.20), channel_id=1, source_target_pairs={{1,0},{2,1},{3,2},{4,3},{5,4},{6,5},{7,6},{0,7},{9,8},{10,9},{11,1... | collective-permute-start | bytes 196616 | tf_op jit(solution)/shard_map/ppermute | solution.py:276
  104.1 0.6 copy-start.1
  104.2 0.6 copy-start.2

commit v2 on v1

--- a/solution.py
+++ b/solution.py
@@ -9,6 +9,7 @@
 
 FIELDS = 4
 LEVELS = 4
+ITEMS = FIELDS * LEVELS
 ROWS = 16
 WIDTH = 512
 LANES = 128
@@ -47,12 +48,22 @@
     return first, second, third
 
 
+def pack_kernel(present_ref, vel_ref, low_ref, high_ref):
+    low_ref[0:ITEMS] = present_ref[:, 0:2, :]
+    high_ref[0:ITEMS] = present_ref[:, ROWS - 2 : ROWS, :]
+    for item in range(2 * LEVELS):
+        low_ref[ITEMS + item // 2, item % 2 : item % 2 + 1, :] = vel_ref[item, 0:1, :]
+        high_ref[ITEMS + item // 2, item % 2 : item % 2 + 1, :] = vel_ref[item, ROWS - 1 : ROWS, :]
+
+
 def explicit_kernel(chunk, xy_ref, zs_ref, present_ref, south_ref, north_ref, vel_ref, vel_south_ref,
                     vel_north_ref, face_ref, explicit_ref, send_ref, tail_ref, vel_tail_ref):
-    tail_ref[:, 0:2, :] = north_ref[...]
-    tail_ref[:, 6:8, :] = south_ref[...]
-    vel_tail_ref[:, 0:1, :] = vel_north_ref[...]
-    vel_tail_ref[:, 7:8, :] = vel_south_ref[...]
+    tail_ref[:, 0:2, :] = north_ref[0:ITEMS]
+    tail_ref[:, 6:8, :] = south_ref[0:ITEMS]
+    for item in range(2 * LEVELS):
+        row = slice(item % 2, item % 2 + 1)
+        vel_tail_ref[item, 0:1, :] = vel_north_ref[ITEMS + item // 2, row, :]
+        vel_tail_ref[item, 7:8, :] = vel_south_ref[ITEMS + item // 2, row, :]
     for level in range(LEVELS):
         half_x = 0.5 * jnp.concatenate([vel_ref[level], vel_tail_ref[level]], 0)
         half_y = 0.5 * jnp.concatenate([vel_ref[LEVELS + level], vel_tail_ref[LEVELS + level]], 0)
@@ -93,9 +104,12 @@
     return lax.broadcasted_iota(jnp.int32, (8, LANES), 0) < 4
 
 
-def factor_kernel(got_ref, zs_ref, weight_ref, gain_ref):
+def factor_kernel(zs_ref, got_ref, weight_ref, gain_ref, back_ref):
     low = lower_half()
-    scale = zs_ref[...]
+    field = lax.rem(lax.broadcasted_iota(jnp.int32, (8, LANES), 0), FIELDS)
+    scale = jnp.full((8, LANES), zs_ref[0], jnp.float32)
+    for other in range(1, FIELDS):
+        scale = jnp.where(field == other, zs_ref[other], scale)
     couple, own, under = [], [], []
     for step in range(HALF):
         rates = [
@@ -132,6 +146,7 @@
             gain = inward * weight
             weight_ref[step] = weight
             gain_ref[step] = gain
+    separator_kernel(got_ref, weight_ref, gain_ref, back_ref)
 
 
 def separator_kernel(got_ref, weight_ref, gain_ref, back_ref):
@@ -190,34 +205,49 @@
 
 VMEM = pl.BlockSpec(memory_space=pltpu.VMEM)
 SMEM = pl.BlockSpec(memory_space=pltpu.SMEM)
+PARAMS = pltpu.CompilerParams(vmem_limit_bytes=6 << 20)
 
 
 def struct(*shape):
     return jax.ShapeDtypeStruct(shape, jnp.float32)
 
 
+def pack_part(present, vel):
+    shape = struct(ITEMS + LEVELS, 2, WIDTH)
+    return pl.pallas_call(
+        pack_kernel,
+        out_shape=(shape, shape),
+        in_specs=[VMEM, VMEM],
+        out_specs=(VMEM, VMEM),
+        compiler_params=PARAMS,
+        name="pack_part",
+    )(present, vel)
+
+
 def explicit_part(chunk, *operands):
     return pl.pallas_call(
         functools.partial(explicit_kernel, chunk),
-        out_shape=(struct(FIELDS * LEVELS, ROWS, WIDTH), struct(BLOCKS * chunk, LANES)),
+        out_shape=(struct(ITEMS, ROWS, WIDTH), struct(BLOCKS * chunk, LANES)),
         in_specs=[SMEM, SMEM] + [VMEM] * 7,
         out_specs=(VMEM, VMEM),
         scratch_shapes=[
-            pltpu.VMEM((FIELDS * LEVELS, 8, WIDTH), jnp.float32),
+            pltpu.VMEM((ITEMS, 8, WIDTH), jnp.float32),
             pltpu.VMEM((2 * LEVELS, 8, WIDTH), jnp.float32),
         ],
+        compiler_params=PARAMS,
         name="explicit_part",
     )(*operands)
 
 
-def factor_part(got, scale):
+def factor_part(scale, got):
     return pl.pallas_call(
         factor_kernel,
-        out_shape=(struct(HALF, 8, LANES), struct(HALF, 8, LANES)),
-        in_specs=[VMEM, VMEM],
-        out_specs=(VMEM, VMEM),
+        out_shape=(struct(HALF, 8, LANES), struct(HALF, 8, LANES), struct(BLOCKS, 8, LANES)),
+        in_specs=[SMEM, VMEM],
+        out_specs=(VMEM, VMEM, VMEM),
+        compiler_params=PARAMS,
         name="factor_part",
-    )(got, scale)
+    )(scale, got)
 
 
 def separator_part(got, weight, gain):
@@ -226,19 +256,21 @@
         out_shape=struct(BLOCKS, 8, LANES),
         in_specs=[VMEM] * 3,
         out_specs=VMEM,
+        compiler_params=PARAMS,
         name="separator_part",
     )(got, weight, gain)
 
 
 def finish_part(edges, *operands):
-    shapes = [struct(FIELDS * LEVELS, ROWS, WIDTH)]
+    shapes = [struct(ITEMS, ROWS, WIDTH)]
     if edges:
-        shapes += [struct(FIELDS * LEVELS, 2, WIDTH)] * 2
+        shapes += [struct(ITEMS, 2, WIDTH)] * 2
     return pl.pallas_call(
         functools.partial(finish_kernel, edges),
         out_shape=tuple(shapes),
         in_specs=[SMEM] + [VMEM] * 3,
         out_specs=(VMEM,) * len(shapes),
+        compiler_params=PARAMS,
         name="finish_part",
     )(*operands)
 
@@ -247,18 +279,12 @@
     count = lax.axis_size("gy")
     up = [(i, (i + 1) % count) for i in range(count)]
     down = [(target, source) for source, target in up]
-    present = fields.reshape(FIELDS * LEVELS, ROWS, WIDTH)
+    present = fields.reshape(ITEMS, ROWS, WIDTH)
     vel = velocity.reshape(2 * LEVELS, ROWS, WIDTH)
-    scale = jnp.broadcast_to(jnp.tile(z_scale, 2)[:, None], (8, LANES))
-
-    lowest = jnp.concatenate([present[:, 0:2].reshape(-1, WIDTH), vel[:, 0]], 0)
-    highest = jnp.concatenate([present[:, ROWS - 2 :].reshape(-1, WIDTH), vel[:, ROWS - 1]], 0)
+    lowest, highest = pack_part(present, vel)
     south = lax.ppermute(highest, "gy", up)
     north = lax.ppermute(lowest, "gy", down)
-    cut = 2 * FIELDS * LEVELS
-    vel_south, vel_north = south[cut:, None], north[cut:, None]
-    south = south[:cut].reshape(-1, 2, WIDTH)
-    north = north[:cut].reshape(-1, 2, WIDTH)
+    vel_south, vel_north = south, north
 
     def swap_over(chunks):
         return lax.all_to_all(chunks, "gz", 0, 0, tiled=True)
@@ -267,8 +293,8 @@
         16, xy_rate, z_scale, present, south, north, vel, vel_south, vel_north, face_rate
     )
     got = swap_over(send.reshape(BLOCKS, 16, LANES))
-    weight, gain = factor_part(got, scale)
-    back = swap_over(separator_part(got, weight, gain))
+    weight, gain, back = factor_part(z_scale, got)
+    back = swap_over(back)
     present, lowest, highest = finish_part(
         True, z_scale, explicit, face_rate, back.reshape(BLOCKS * 8, LANES)
     )

time: 171 us -> 155 us (0.906)
  blocking collectives: 85.2 us -> 134 us
  waiting for transfers between devices: 38.9 us -> 6.65 us
  starting transfers between devices: 20.8 us -> 3.5 us
  Pallas kernels: 18.9 us -> 8.8 us
  local copies, waits for them, and re-layouts: 6.22 us -> 2.01 us
    all_to_all x3 -> x4, blocking collectives: 85.2 us -> 134 us  [swap_over(): return lax.all_to_all(chunks, 'gz', 0, 0, tiled=True)]
    all_to_all x1 -> x0, waiting for transfers between devices: 33.2 us -> none  [swap_over(): return lax.all_to_all(chunks, 'gz', 0, 0, tiled=True)]
    all_to_all x1 -> x0, starting transfers between devices: 17.3 us -> none  [swap_over(): return lax.all_to_all(chunks, 'gz', 0, 0, tiled=True)]
    pallas_call x2 -> x1, Pallas kernels: 3.87 us -> 0.15 us  [separator_part(): pl.pallas_call(separator_kernel, out_shape=struct(BLOCKS, 8, LANES), in_s...]
    pallas_call x2, Pallas kernels: 8.38 us -> 5.19 us  [explicit_part(): pl.pallas_call(functools.partial(explicit_kernel, chunk), out_shape=(stru...]
    slice x6 -> x0, local copies, waits for them, and re-layouts: 2.09 us -> none  [the longest x2 2.08 us: on_device(): lowest = jnp.concatenate([present[:, 0:2].reshape(-1, WIDTH), vel[:, 0]], 0)]
    pallas_call x2, Pallas kernels: 4.48 us -> 2.41 us  [finish_part(): pl.pallas_call(functools.partial(finish_kernel, edges), out_shape=tuple(s...]
    broadcast_in_dim x4 -> x0, local copies, waits for them, and re-layouts: 2.03 us -> none  [the longest x2 1.22 us: on_device(): vel_south, vel_north = (south[cut:, None], north[cut:, None])]
  transfers between devices with their start and end apart: 5 -> 4, of which waited for: 5 -> 3; matrix products, arithmetic and copies ran while one was open for 1% -> 0% of each run, Pallas kernels for 0% -> 0%
where the time goes in v2:
time: 155 us
  blocking collectives  134 us (86%)
  Pallas kernels  8.8 us (6%)
  waiting for transfers between devices  6.65 us (4%)
  starting transfers between devices  3.5 us (2%)
  local copies, waits for them, and re-layouts  2.01 us (1%)
    all_to_all x4, blocking collectives, swap_over(): return lax.all_to_all(chunks, 'gz', 0, 0, tiled=True)  134 us
    pallas_call x2, Pallas kernels, explicit_part(): pl.pallas_call(functools.partial(explicit_kernel, chunk), out_shape=(stru...  5.19 us
    ppermute x2, waiting for transfers between devices, on_device(): south = lax.ppermute(highest, 'gy', up)  4.06 us
    ppermute x2, starting transfers between devices, on_device(): north = lax.ppermute(lowest, 'gy', down)  3.47 us
  transfers between devices with their start and end apart: 4, of which 3 were waited for; matrix products, arithmetic and copies ran while one was open for 0% of the time, Pallas kernels for 0%

profile of v2, /device:TPU:24, one launch (start us, length us, event | category | flops | bytes accessed | tf_op | source)
XLA Modules:
  0.0 155.0 jit_solution(1537312955475310966)
XLA Ops:
  0.0 0.0 copy-start
  0.0 0.9 copy-done
  1.0 0.0 copy-start.2
  1.0 1.0 copy-done.2
  2.0 0.0 copy-start.3
  2.0 0.0 copy-start.4
  2.0 0.0 copy-start.5
  2.1 0.0 collective-permute-start
  2.1 1.7 %collective-permute-start.1 = (f32[20,2,512]{2,1,0:T(2,128)S(1)}, f32[20,2,512]{2,1,0:T(2,128)S(1)}, u32[]{:S(2)}, u32[]{:S(2)}) collective-permute-start(f32[20,2,512]{2,1,0:T(2,128)S(1)} %get-tuple-element.18), channel_id=1, source_target_pairs={{1,0},{2,1},{3,2},{4,3},{5,4},{6,5},{7,6},{0,7},{9,8},{10,9},{11,1... | collective-permute-start | bytes 245768 | tf_op jit(solution)/shard_map/ppermute | solution.py:286
  3.8 2.1 %collective-permute-done.south_ref.vel_south_ref = f32[20,2,512]{2,1,0:T(2,128)S(1)} collective-permute-done((f32[20,2,512]{2,1,0:T(2,128)S(1)}, f32[20,2,512]{2,1,0:T(2,128)S(1)}, u32[]{:S(2)}, u32[]{:S(2)}) %collective-permute-start) | collective-permute-done | bytes 81952 | tf_op jit(solution)/shard_map/ppermute | solution.py:285
  5.9 2.6 %collective-permute-done.1.north_ref.vel_north_ref = f32[20,2,512]{2,1,0:T(2,128)S(1)} collective-permute-done((f32[20,2,512]{2,1,0:T(2,128)S(1)}, f32[20,2,512]{2,1,0:T(2,128)S(1)}, u32[]{:S(2)}, u32[]{:S(2)}) %collective-permute-start.1) | collective-permute-done | bytes 81952 | tf_op jit(solution)/shard_map/ppermute | solution.py:286
  8.5 0.0 copy-done.3
  8.5 0.0 copy-done.4
  8.5 0.0 copy-done.5
  8.5 2.6 %explicit_part.2 = (f32[16,16,512]{2,1,0:T(8,128)S(1)}, f32[1024,128]{1,0:T(8,128)S(1)}) custom-call(f32[4]{0:T(128)S(1)} %copy-done.5, f32[4]{0:T(128)S(1)} %copy-done.4, f32[16,16,512]{2,1,0:T(8,128)S(1)} %bitcast.11, f32[20,2,512]{2,1,0:T(2,128)S(1)} %collective-permute-done.south_ref.vel_south_ref, ...), custom_call_target="tpu_custom_call" | custom-call | tf_op jit(solution)/shard_map/explicit_part/pallas_call | solution.py:228
  11.2 49.3 %all_to_all.20.got_ref = f32[64,16,128]{2,1,0:T(8,128)S(1)} all-to-all(f32[64,16,128]{2,1,0:T(8,128)S(1)} %bitcast.14), channel_id=1, replica_groups=mesh['gz'=64,'gy'=8] {'gz'}, dimensions={0} | all-to-all | bytes 1048576 | tf_op jit(solution)/shard_map/all_to_all | solution.py:290
  60.5 1.0 factor_part.1
  61.5 28.8 %all_to_all.21 = f32[64,8,128]{2,1,0:T(8,128)S(1)} all-to-all(f32[64,8,128]{2,1,0:T(8,128)S(1)} %get-tuple-element.21), channel_id=1, replica_groups=mesh['gz'=64,'gy'=8] {'gz'}, dimensions={0} | all-to-all | bytes 524288 | tf_op jit(solution)/shard_map/all_to_all | solution.py:290
  90.3 0.0 copy-start.1
  90.3 0.8 finish_part.2
  91.1 0.0 collective-permute-start.2
  91.1 1.7 %collective-permute-start.3 = (f32[16,2,512]{2,1,0:T(2,128)S(1)}, f32[16,2,512]{2,1,0:T(2,128)S(1)}, u32[]{:S(2)}, u32[]{:S(2)}) collective-permute-start(f32[16,2,512]{2,1,0:T(2,128)S(1)} %get-tuple-element.24), channel_id=1, source_target_pairs={{1,0},{2,1},{3,2},{4,3},{5,4},{6,5},{7,6},{0,7},{9,8},{10,9},{11,1... | collective-permute-start | bytes 196616 | tf_op jit(solution)/shard_map/ppermute | solution.py:302
  92.9 1.9 %collective-permute-done.2.south_ref = f32[16,2,512]{2,1,0:T(2,128)S(1)} collective-permute-done((f32[16,2,512]{2,1,0:T(2,128)S(1)}, f32[16,2,512]{2,1,0:T(2,128)S(1)}, u32[]{:S(2)}, u32[]{:S(2)}) %collective-permute-start.2) | collective-permute-done | bytes 65568 | tf_op jit(solution)/shard_map/ppermute | solution.py:301
  94.8 0.0 collective-permute-done.3.north_ref
  94.8 0.0 copy-done.1
  94.8 2.6 %explicit_part.3 = (f32[16,16,512]{2,1,0:T(8,128)S(1)}, f32[512,128]{1,0:T(8,128)S(1)}) custom-call(f32[4]{0:T(128)S(1)} %copy-done.5, f32[4]{0:T(128)S(1)} %copy-done.4, f32[16,16,512]{2,1,0:T(8,128)S(1)} %get-tuple-element.22.present_ref, f32[16,2,512]{2,1,0:T(2,128)S(1)} %collective-permute-done.2.south_ref, ...), custom_call_target="tpu_custom_call" | custom-call | tf_op jit(solution)/shard_map/explicit_part/pallas_call | solution.py:228
  97.4 27.5 %all_to_all.22.got_ref = f32[64,8,128]{2,1,0:T(8,128)S(1)} all-to-all(f32[64,8,128]{2,1,0:T(8,128)S(1)} %bitcast.15), channel_id=1, replica_groups=mesh['gz'=64,'gy'=8] {'gz'}, dimensions={0} | all-to-all | bytes 524288 | tf_op jit(solution)/shard_map/all_to_all | solution.py:290
  124.9 0.1 separator_part.1
  125.0 28.4 %all_to_all.23 = f32[64,8,128]{2,1,0:T(8,128)S(1)} all-to-all(f32[64,8,128]{2,1,0:T(8,128)S(1)} %separator_part.1), channel_id=1, replica_groups=mesh['gz'=64,'gy'=8] {'gz'}, dimensions={0} | all-to-all | bytes 524288 | tf_op jit(solution)/shard_map/all_to_all | solution.py:290
  153.4 1.6 %finish_part.3 = f32[16,16,512]{2,1,0:T(8,128)} custom-call(f32[4]{0:T(128)S(1)} %copy-done.4, f32[16,16,512]{2,1,0:T(8,128)S(1)} %get-tuple-element.25.explicit_ref, f32[4,16,512]{2,1,0:T(8,128)S(1)} %copy-done.3, f32[512,128]{1,0:T(8,128)S(1)} %bitcast.13), custom_call_target="tpu_custom_call" | custom-call | tf_op jit(solution)/shard_map/finish_part/pallas_call | solution.py:268
  (1 shorter events, 0.0 us)
Async XLA Ops:
  0.0 0.9 copy-start
  1.0 1.0 copy-start.2
  2.0 6.5 %copy-start.3 = (f32[4,16,512]{2,1,0:T(8,128)S(1)}, f32[4,16,512]{2,1,0:T(8,128)}, u32[]{:S(2)}) copy-start(f32[4,16,512]{2,1,0:T(8,128)} %face_ref.7) | copy-start | bytes 393220
  2.0 6.5 %copy-start.4 = (f32[4]{0:T(128)S(1)}, f32[4]{0:T(128)}, u32[]{:S(2)}) copy-start(f32[4]{0:T(128)} %zs_ref.9) | copy-start | bytes 52
  2.0 6.5 %copy-start.5 = (f32[4]{0:T(128)S(1)}, f32[4]{0:T(128)}, u32[]{:S(2)}) copy-start(f32[4]{0:T(128)} %xy_ref.3) | copy-start | bytes 52
  2.1 3.9 %collective-permute-start = (f32[20,2,512]{2,1,0:T(2,128)S(1)}, f32[20,2,512]{2,1,0:T(2,128)S(1)}, u32[]{:S(2)}, u32[]{:S(2)}) collective-permute-start(f32[20,2,512]{2,1,0:T(2,128)S(1)} %get-tuple-element.17), channel_id=1, source_target_pairs={{0,1},{1,2},{2,3},{3,4},{4,5},{5,6},{6,7},{7,0},{8,9},{9,10},{10,1... | collective-permute-start | bytes 245768 | tf_op jit(solution)/shard_map/ppermute | solution.py:285
  2.1 6.4 %collective-permute-start.1 = (f32[20,2,512]{2,1,0:T(2,128)S(1)}, f32[20,2,512]{2,1,0:T(2,128)S(1)}, u32[]{:S(2)}, u32[]{:S(2)}) collective-permute-start(f32[20,2,512]{2,1,0:T(2,128)S(1)} %get-tuple-element.18), channel_id=1, source_target_pairs={{1,0},{2,1},{3,2},{4,3},{5,4},{6,5},{7,6},{0,7},{9,8},{10,9},{11,1... | collective-permute-start | bytes 245768 | tf_op jit(solution)/shard_map/ppermute | solution.py:286
  90.3 4.5 %copy-start.1 = (f32[2,4,16,512]{3,2,1,0:T(8,128)S(1)}, f32[2,4,16,512]{3,2,1,0:T(8,128)}, u32[]{:S(2)}) copy-start(f32[2,4,16,512]{3,2,1,0:T(8,128)} %param.6) | copy-start | bytes 786436
  91.1 3.7 %collective-permute-start.2 = (f32[16,2,512]{2,1,0:T(2,128)S(1)}, f32[16,2,512]{2,1,0:T(2,128)S(1)}, u32[]{:S(2)}, u32[]{:S(2)}) collective-permute-start(f32[16,2,512]{2,1,0:T(2,128)S(1)} %get-tuple-element.23), channel_id=1, source_target_pairs={{0,1},{1,2},{2,3},{3,4},{4,5},{5,6},{6,7},{7,0},{8,9},{9,10},{10,1... | collective-permute-start | bytes 196616 | tf_op jit(solution)/shard_map/ppermute | solution.py:301
  91.1 3.7 %collective-permute-start.3 = (f32[16,2,512]{2,1,0:T(2,128)S(1)}, f32[16,2,512]{2,1,0:T(2,128)S(1)}, u32[]{:S(2)}, u32[]{:S(2)}) collective-permute-start(f32[16,2,512]{2,1,0:T(2,128)S(1)} %get-tuple-element.24), channel_id=1, source_target_pairs={{1,0},{2,1},{3,2},{4,3},{5,4},{6,5},{7,6},{0,7},{9,8},{10,9},{11,1... | collective-permute-start | bytes 196616 | tf_op jit(solution)/shard_map/ppermute | solution.py:302

commit v3 on v2

v3 whole, which is shorter than its diff:
```python
import functools

import jax
import jax.numpy as jnp
from jax import lax
from jax.experimental import pallas as pl
from jax.experimental.pallas import tpu as pltpu
from jax.sharding import Mesh, PartitionSpec as P

STEPS = 2
FIELDS = 4
LEVELS = 4
ITEMS = FIELDS * LEVELS
ROWS = 16
WIDTH = 512
GROUPS = 4
MEMBERS = 16
PAIRS = MEMBERS // 2
LANES = 128
COLUMNS = WIDTH // LANES
TILE = (COLUMNS, 8, LANES)


def tendency(middle, half_x, half_y, spread):
    rows = middle.shape[0]
    eastern = pltpu.roll(middle, WIDTH - 1, 1)
    western = pltpu.roll(middle, 1, 1)
    north = pltpu.roll(middle, rows - 1, 0)
    south = pltpu.roll(middle, 1, 0)
    return spread * (eastern + western + north + south - 4.0 * middle) - (
        half_x * (eastern - western) + half_y * (north - south)
    )


def inner_pivots(rates):
    hold = 1.0 + rates[0]
    inverse = []
    for level in range(LEVELS - 1):
        once = 1.0 / (hold + rates[level + 1])
        inverse.append(once)
        hold = 1.0 + rates[level + 1] * hold * once
    return inverse


def solve_inner(source, rates, inverse):
    first = source[0]
    second = source[1] + rates[1] * inverse[0] * first
    third = (source[2] + rates[2] * inverse[1] * second) * inverse[2]
    second = (second + rates[2] * third) * inverse[1]
    first = (first + rates[1] * second) * inverse[0]
    return first, second, third


def pack_kernel(present_ref, vel_ref, low_ref, high_ref):
    low_ref[0:ITEMS] = present_ref[:, 0:2, :]
    high_ref[0:ITEMS] = present_ref[:, ROWS - 2 : ROWS, :]
    for item in range(2 * LEVELS):
        low_ref[ITEMS + item // 2, item % 2 : item % 2 + 1, :] = vel_ref[item, 0:1, :]
        high_ref[ITEMS + item // 2, item % 2 : item % 2 + 1, :] = vel_ref[item, ROWS - 1 : ROWS, :]


def places(tile, chunk, line):
    for column in range(COLUMNS):
        start = (tile * 8 * (chunk // 8) + line // 8) * COLUMNS * 8 + column * 8 + line % 8
        yield slice(column * LANES, column * LANES + LANES), pl.ds(start, 8, stride=COLUMNS * chunk)


def spread_rows(send_ref, tile, chunk, line, value):
    for lanes, lines in places(tile, chunk, line):
        send_ref[lines, :] = value[:, lanes]


def explicit_kernel(chunk, xy_ref, zs_ref, present_ref, south_ref, north_ref, vel_ref, vel_south_ref,
                    vel_north_ref, face_ref, explicit_ref, send_ref, tail_ref, vel_tail_ref):
    tail_ref[:, 0:2, :] = north_ref[0:ITEMS]
    tail_ref[:, 6:8, :] = south_ref[0:ITEMS]
    for item in range(2 * LEVELS):
        row = slice(item % 2, item % 2 + 1)
        vel_tail_ref[item, 0:1, :] = vel_north_ref[ITEMS + item // 2, row, :]
        vel_tail_ref[item, 7:8, :] = vel_south_ref[ITEMS + item // 2, row, :]
    for level in range(LEVELS):
        half_x = 0.5 * jnp.concatenate([vel_ref[level], vel_tail_ref[level]], 0)
        half_y = 0.5 * jnp.concatenate([vel_ref[LEVELS + level], vel_tail_ref[LEVELS + level]], 0)
        for field in range(FIELDS):
            item = field * LEVELS + level
            spread = xy_ref[field]
            middle = jnp.concatenate([present_ref[item], tail_ref[item]], 0)
            sectioned = middle + tendency(middle, half_x, half_y, spread)
            again = sectioned + tendency(sectioned, half_x, half_y, spread)
            explicit_ref[item] = (0.5 * middle + 0.5 * again)[:ROWS]
    for tile in range(ROWS // 8):
        rows = slice(tile * 8, tile * 8 + 8)
        for field in range(FIELDS):
            scale = zs_ref[field]
            rates = [scale * face_ref[level, rows, :] for level in range(LEVELS)]
            source = [explicit_ref[field * LEVELS + level, rows, :] for level in range(LEVELS)]
            first, _, third = solve_inner(source, rates, inner_pivots(rates))
            spread_rows(send_ref, tile, chunk, field, source[3] + rates[3] * third)
            spread_rows(send_ref, tile, chunk, FIELDS + field, rates[0] * first)
        if chunk > 8:
            for level in range(LEVELS):
                spread_rows(send_ref, tile, chunk, 8 + level, face_ref[level, rows, :])


def swap(value):
    return pltpu.roll(value, 4, 1)


def lower_half():
    return lax.broadcasted_iota(jnp.int32, TILE, 1) < 4


def pair_sources(got_ref, low):
    def side(block):
        return got_ref[block, 0] + swap(got_ref[block + 1, 0])

    return [jnp.where(low, side(step), swap(side(MEMBERS - 2 - step))) for step in range(PAIRS)]


def outer_source(got_ref, low):
    return jnp.where(low, swap(got_ref[0, 0]), swap(got_ref[MEMBERS - 1, 0]))


def eliminate(sources, gain_ref, center):
    value = sources[0]
    kept = [value]
    for step in range(1, PAIRS - 1):
        value = sources[step] + gain_ref[step - 1] * value
        kept.append(value)
    value = gain_ref[PAIRS - 2] * value
    return kept, (sources[PAIRS - 1] + value + swap(value)) * center


def reduce_kernel(first, zs_ref, got_ref, *refs):
    low = lower_half()
    if first:
        weight_ref, gain_ref, edge_ref, source_ref, send_ref = refs
        field = lax.rem(lax.broadcasted_iota(jnp.int32, TILE, 1), FIELDS)
        scale = jnp.full(TILE, zs_ref[0], jnp.float32)
        for other in range(1, FIELDS):
            scale = jnp.where(field == other, zs_ref[other], scale)
        couple, own, under = [], [], []
        for step in range(PAIRS):
            rates = [
                scale
                * jnp.where(
                    low,
                    jnp.broadcast_to(got_ref[step, 1, :, level : level + 1, :], TILE),
                    jnp.broadcast_to(got_ref[MEMBERS - 1 - step, 1, :, level : level + 1, :], TILE),
                )
                for level in range(LEVELS)
            ]
            inverse = inner_pivots(rates)
            one = jnp.ones(TILE, jnp.float32)
            bottom, _, third = solve_inner([one, one, one], rates, inverse)
            own.append(1.0 + rates[3] * third)
            under.append(rates[0] * bottom)
            couple.append(rates[0] * inverse[0] * rates[1] * inverse[1] * rates[2] * inverse[2] * rates[3])
        masses = [
            jnp.where(low, own[step] + under[step + 1], own[step + 1] + under[step]) for step in range(PAIRS - 1)
        ]
        last_own, last_under = own[PAIRS - 1], under[PAIRS - 1]
        masses.append(jnp.where(low, last_own + swap(last_under), swap(last_own) + last_under))
        hold = masses[0] + couple[0]
        through = couple[0]
        for step in range(PAIRS - 1):
            inward = couple[step + 1]
            weight = 1.0 / (hold + inward)
            gain = inward * weight
            weight_ref[step] = weight
            gain_ref[step] = gain
            through = through * gain
            hold = hold * gain + (masses[step + 1] if step + 2 < PAIRS else 0.0)
        center = 1.0 / (masses[PAIRS - 1] + hold + swap(hold))
        weight_ref[PAIRS - 1] = center
        edge_ref[...] = couple[0]
        kept, value = eliminate(masses, gain_ref, center)
        for step in reversed(range(PAIRS - 1)):
            value = weight_ref[step] * kept[step] + gain_ref[step] * value
        outer = jnp.where(low, under[0], own[0]) + couple[0] * value
        through = through * swap(through) * center
        for group in range(GROUPS):
            send_ref[group, 1] = outer
            send_ref[group, 2] = through
    else:
        weight_ref, gain_ref, edge_ref, source_ref, send_ref = refs
    sources = pair_sources(got_ref, low)
    for step in range(PAIRS):
        source_ref[step] = sources[step]
    kept, value = eliminate(sources, gain_ref, weight_ref[PAIRS - 1])
    for step in reversed(range(PAIRS - 1)):
        value = weight_ref[step] * kept[step] + gain_ref[step] * value
    outer = outer_source(got_ref, low) + edge_ref[...] * value
    for group in range(GROUPS):
        send_ref[group, 0] = outer


def across(parts, low):
    ends = jnp.where(low, swap(parts[0]) + parts[1], parts[3])
    middle = jnp.where(low, swap(parts[1]) + parts[2], parts[2] + swap(parts[3]))
    return ends, middle


def return_kernel(first, place_ref, got_ref, source_ref, weight_ref, gain_ref, edge_ref, *refs):
    low = lower_half()
    if first:
        top_ref, back_ref = refs
        ends, middle = across([got_ref[group, 1] for group in range(GROUPS)], low)
        through = [got_ref[group, 2] for group in range(GROUPS)]
        hold = ends + jnp.where(low, through[0], 0.0)
        inward = jnp.where(low, through[1], through[3])
        weight = 1.0 / (hold + inward)
        gain = inward * weight
        hold = middle + hold * gain
        other = swap(hold)
        inverse = 1.0 / (hold * other + through[2] * (hold + other))
        mine, cross = (other + through[2]) * inverse, through[2] * inverse
        for item, value in enumerate((weight, gain, mine, cross)):
            top_ref[item] = value
    else:
        top_ref, back_ref = refs
        weight, gain, mine, cross = (top_ref[item] for item in range(4))
    ends, middle = across([got_ref[group, 0] for group in range(GROUPS)], low)
    inner = middle + gain * ends
    inner = mine * inner + cross * swap(inner)
    ends = weight * ends + gain * inner
    turned = swap(ends)
    place = place_ref[0]
    value = jnp.where(
        place == 0,
        jnp.where(low, 0.0, turned),
        jnp.where(
            place == 1,
            jnp.where(low, ends, swap(inner)),
            jnp.where(place == 2, inner, jnp.where(low, swap(inner), ends)),
        ),
    )
    sources = [source_ref[step] for step in range(PAIRS)]
    sources[0] = sources[0] + edge_ref[...] * value
    kept, center = eliminate(sources, gain_ref, weight_ref[PAIRS - 1])
    solved = [center]
    for step in reversed(range(PAIRS - 1)):
        solved.insert(0, weight_ref[step] * kept[step] + gain_ref[step] * solved[0])
    outer = value
    for step in range(PAIRS):
        turned = swap(solved[step])
        back_ref[step] = jnp.where(low, outer, turned)
        back_ref[MEMBERS - 1 - step] = jnp.where(low, turned, outer)
        outer = solved[step]


def finish_kernel(edges, zs_ref, explicit_ref, face_ref, back_ref, present_ref, *edge_refs):
    for tile in range(ROWS // 8):
        rows = slice(tile * 8, tile * 8 + 8)
        for field in range(FIELDS):
            scale = zs_ref[field]
            rates = [scale * face_ref[level, rows, :] for level in range(LEVELS)]
            source = [explicit_ref[field * LEVELS + level, rows, :] for level in range(LEVELS - 1)]
            below = jnp.concatenate([back_ref[lines, :] for _, lines in places(tile, 8, field)], 1)
            top = jnp.concatenate([back_ref[lines, :] for _, lines in places(tile, 8, FIELDS + field)], 1)
            source[0] = source[0] + rates[0] * below
            source[2] = source[2] + rates[3] * top
            solved = solve_inner(source, rates, inner_pivots(rates)) + (top,)
            for level in range(LEVELS):
                item = field * LEVELS + level
                present_ref[item, rows, :] = solved[level]
                if edges and tile == 0:
                    edge_refs[0][item] = solved[level][0:2]
                if edges and tile == 1:
                    edge_refs[1][item] = solved[level][6:8]


VMEM = pl.BlockSpec(memory_space=pltpu.VMEM)
SMEM = pl.BlockSpec(memory_space=pltpu.SMEM)
PARAMS = pltpu.CompilerParams(vmem_limit_bytes=6 << 20)


def struct(*shape):
    return jax.ShapeDtypeStruct(shape, jnp.float32)


def pack_part(present, vel):
    shape = struct(ITEMS + LEVELS, 2, WIDTH)
    return pl.pallas_call(
        pack_kernel,
        out_shape=(shape, shape),
        in_specs=[VMEM, VMEM],
        out_specs=(VMEM, VMEM),
        compiler_params=PARAMS,
        name="pack_part",
    )(present, vel)


def explicit_part(chunk, *operands):
    return pl.pallas_call(
        functools.partial(explicit_kernel, chunk),
        out_shape=(struct(ITEMS, ROWS, WIDTH), struct(MEMBERS * COLUMNS * chunk, LANES)),
        in_specs=[SMEM, SMEM] + [VMEM] * 7,
        out_specs=(VMEM, VMEM),
        scratch_shapes=[
            pltpu.VMEM((ITEMS, 8, WIDTH), jnp.float32),
            pltpu.VMEM((2 * LEVELS, 8, WIDTH), jnp.float32),
        ],
        compiler_params=PARAMS,
        name="explicit_part",
    )(*operands)


def reduce_part(scale, got, factors=None):
    shapes = (struct(PAIRS, *TILE), struct(PAIRS - 1, *TILE), struct(*TILE))
    outs = (struct(PAIRS, *TILE), struct(GROUPS, 1 if factors else 3, *TILE))
    if not factors:
        outs = shapes + outs
    return pl.pallas_call(
        functools.partial(reduce_kernel, not factors),
        out_shape=outs,
        in_specs=[SMEM, VMEM] + [VMEM] * (3 if factors else 0),
        out_specs=(VMEM,) * len(outs),
        compiler_params=PARAMS,
        name="reduce_part",
    )(scale, got, *(factors or ()))


def return_part(place, got, sources, factors, top=None):
    outs = (struct(MEMBERS, *TILE),)
    if top is None:
        outs = (struct(4, *TILE),) + outs
    operands = (got, sources) + tuple(factors) + (() if top is None else (top,))
    return pl.pallas_call(
        functools.partial(return_kernel, top is None),
        out_shape=outs,
        in_specs=[SMEM] + [VMEM] * len(operands),
        out_specs=(VMEM,) * len(outs),
        compiler_params=PARAMS,
        name="return_part",
    )(place, *operands)


def finish_part(edges, *operands):
    shapes = [struct(ITEMS, ROWS, WIDTH)]
    if edges:
        shapes += [struct(ITEMS, 2, WIDTH)] * 2
    return pl.pallas_call(
        functools.partial(finish_kernel, edges),
        out_shape=tuple(shapes),
        in_specs=[SMEM] + [VMEM] * 3,
        out_specs=(VMEM,) * len(shapes),
        compiler_params=PARAMS,
        name="finish_part",
    )(*operands)


def on_device(fields, velocity, face_rate, xy_rate, z_scale):
    count = lax.axis_size("gy")
    up = [(i, (i + 1) % count) for i in range(count)]
    down = [(target, source) for source, target in up]
    present = fields.reshape(ITEMS, ROWS, WIDTH)
    vel = velocity.reshape(2 * LEVELS, ROWS, WIDTH)
    lowest, highest = pack_part(present, vel)
    south = lax.ppermute(highest, "gy", up)
    north = lax.ppermute(lowest, "gy", down)
    vel_south, vel_north = south, north

    place = lax.axis_index("zh").astype(jnp.int32).reshape(1)

    def near(chunks):
        return lax.all_to_all(chunks, "zi", 0, 0, tiled=True)

    def far(chunks):
        return lax.all_to_all(chunks, "zh", 0, 0, tiled=True)

    factors = top = None
    for step in range(STEPS):
        if step > 0:
            south = lax.ppermute(highest, "gy", up)
            north = lax.ppermute(lowest, "gy", down)
        chunk = 8 if factors else 16
        explicit, send = explicit_part(
            chunk, xy_rate, z_scale, present, south, north, vel, vel_south, vel_north, face_rate
        )
        got = near(send.reshape(MEMBERS, chunk // 8, *TILE))
        *made, sources, ports = reduce_part(z_scale, got, factors)
        factors = factors or tuple(made)
        *made, back = return_part(place, far(ports), sources, factors, top)
        top = made[0] if made else top
        present, *edges = finish_part(
            step + 1 < STEPS, z_scale, explicit, face_rate, near(back).reshape(MEMBERS * COLUMNS * 8, LANES)
        )
        if edges:
            lowest, highest = edges
    return present.reshape(fields.shape)


def solution(mesh):
    split = Mesh(mesh.devices.reshape(GROUPS, MEMBERS, -1), ("zh", "zi", "gy"))
    depth = ("zh", "zi")
    in_specs = (P(None, depth, "gy", None), P(None, depth, "gy", None), P(depth, "gy", None), P(), P())
    out_specs = P(None, depth, "gy", None)
    return jax.shard_map(
        on_device, mesh=split, in_specs=in_specs, out_specs=out_specs, check_vma=False
    )
```

time: 155 us -> 135 us (0.87)
  blocking collectives: 134 us -> 83.6 us
  waiting for transfers between devices: 6.65 us -> 22.4 us
  starting transfers between devices: 3.5 us -> 15.9 us
    all_to_all x4 -> x5, blocking collectives: 134 us -> 83.6 us  [the longest x4 67.4 us: near(): return lax.all_to_all(chunks, 'zi', 0, 0, tiled=True)]
    all_to_all x0 -> x1, waiting for transfers between devices: none -> 15.7 us  [far(): return lax.all_to_all(chunks, 'zh', 0, 0, tiled=True)]
    all_to_all x0 -> x1, starting transfers between devices: none -> 12.4 us  [far(): return lax.all_to_all(chunks, 'zh', 0, 0, tiled=True)]
  transfers between devices with their start and end apart: 4 -> 5, of which waited for: 3 -> 4; matrix products, arithmetic and copies ran while one was open for 0% -> 0% of each run, Pallas kernels for 0% -> 0%
where the time goes in v3:
time: 135 us; the launch traced here: 134 us
  blocking collectives  83.6 us (62%)
  waiting for transfers between devices  22.4 us (17%)
  starting transfers between devices  15.9 us (12%)
  Pallas kernels  9.9 us (7%)
  local copies, waits for them, and re-layouts  2.01 us (1%)
    all_to_all x4, blocking collectives, near(): return lax.all_to_all(chunks, 'zi', 0, 0, tiled=True)  67.4 us
    all_to_all x1, blocking collectives, far(): return lax.all_to_all(chunks, 'zh', 0, 0, tiled=True)  16.3 us
    all_to_all x1, waiting for transfers between devices, far(): return lax.all_to_all(chunks, 'zh', 0, 0, tiled=True)  15.7 us
    all_to_all x1, starting transfers between devices, far(): return lax.all_to_all(chunks, 'zh', 0, 0, tiled=True)  12.4 us
    pallas_call x2, Pallas kernels, explicit_part(): pl.pallas_call(functools.partial(explicit_kernel, chunk), out_shape=(stru...  5.16 us
    ppermute x2, waiting for transfers between devices, on_device(): south = lax.ppermute(highest, 'gy', up)  4.06 us
    ppermute x2, starting transfers between devices, on_device(): north = lax.ppermute(lowest, 'gy', down)  3.47 us
  transfers between devices with their start and end apart: 5, of which 4 were waited for; matrix products, arithmetic and copies ran while one was open for 0% of the time, Pallas kernels for 0%

profile of v3, /device:TPU:24, one launch (start us, length us, event | category | flops | bytes accessed | tf_op | source)
XLA Modules:
  0.0 133.9 jit_solution(5107076470353196657)
XLA Ops:
  0.0 0.0 copy-start
  0.0 0.9 copy-done
  1.0 1.0 copy-done.2
  2.0 0.0 copy-start.4
  2.0 0.0 copy-start.5
  2.1 0.0 collective-permute-start
  2.1 1.7 %collective-permute-start.1 = (f32[20,2,512]{2,1,0:T(2,128)S(1)}, f32[20,2,512]{2,1,0:T(2,128)S(1)}, u32[]{:S(2)}, u32[]{:S(2)}) collective-permute-start(f32[20,2,512]{2,1,0:T(2,128)S(1)} %get-tuple-element.24), channel_id=1, source_target_pairs={{1,0},{2,1},{3,2},{4,3},{5,4},{6,5},{7,6},{0,7},{9,8},{10,9},{11,1... | collective-permute-start | bytes 245768 | tf_op jit(solution)/shard_map/ppermute | solution.py:361
  3.8 2.1 %collective-permute-done.south_ref.vel_south_ref = f32[20,2,512]{2,1,0:T(2,128)S(1)} collective-permute-done((f32[20,2,512]{2,1,0:T(2,128)S(1)}, f32[20,2,512]{2,1,0:T(2,128)S(1)}, u32[]{:S(2)}, u32[]{:S(2)}) %collective-permute-start) | collective-permute-done | bytes 81952 | tf_op jit(solution)/shard_map/ppermute | solution.py:360
  5.9 2.6 %collective-permute-done.1.north_ref.vel_north_ref = f32[20,2,512]{2,1,0:T(2,128)S(1)} collective-permute-done((f32[20,2,512]{2,1,0:T(2,128)S(1)}, f32[20,2,512]{2,1,0:T(2,128)S(1)}, u32[]{:S(2)}, u32[]{:S(2)}) %collective-permute-start.1) | collective-permute-done | bytes 81952 | tf_op jit(solution)/shard_map/ppermute | solution.py:361
  8.5 0.0 copy-done.3
  8.5 0.0 copy-done.4
  8.5 0.0 copy-done.5
  8.5 2.6 %explicit_part.2 = (f32[16,16,512]{2,1,0:T(8,128)S(1)}, f32[1024,128]{1,0:T(8,128)S(1)}) custom-call(f32[4]{0:T(128)S(1)} %copy-done.5, f32[4]{0:T(128)S(1)} %copy-done.4, f32[16,16,512]{2,1,0:T(8,128)S(1)} %bitcast.12, f32[20,2,512]{2,1,0:T(2,128)S(1)} %collective-permute-done.south_ref.vel_south_ref, ...), custom_call_target="tpu_custom_call" | custom-call | tf_op jit(solution)/shard_map/explicit_part/pallas_call | solution.py:295
  11.1 21.9 %all_to_all.30.got_ref = f32[16,2,4,8,128]{4,3,2,1,0:T(8,128)S(1)} all-to-all(f32[16,2,4,8,128]{4,3,2,1,0:T(8,128)S(1)} %bitcast.15), channel_id=1, replica_groups=mesh['zh'=4,'zi'=16,'gy'=8] {'zi'}, dimensions={0} | all-to-all | bytes 1048576 | tf_op jit(solution)/shard_map/all_to_all | solution.py:367
  33.1 1.6 %reduce_part.2 = (f32[8,4,8,128]{3,2,1,0:T(8,128)S(1)}, f32[7,4,8,128]{3,2,1,0:T(8,128)S(1)}, f32[4,8,128]{2,1,0:T(8,128)S(1)}, f32[8,4,8,128]{3,2,1,0:T(8,128)S(1)}, f32[4,3,4,8,128]{4,3,2,1,0:T(8,128)}) custom-call(f32[4]{0:T(128)S(1)} %copy-done.4, f32[16,2,4,8,128]{4,3,2,1,0:T(8,128)S(1)} %all_to_all.30.got_ref), custom_call_target="tpu_custom_call" | custom-call | tf_op jit(solution)/shard_map/reduce_part/pallas_call | solution.py:314
  34.6 12.4 %all-to-all-start.1 = ((f32[4,3,4,8,128]{4,3,2,1,0:T(8,128)}), f32[4,3,4,8,128]{4,3,2,1,0:T(8,128)S(1)}, u32[]{:S(2)}, u32[]{:S(2)}) async-start(f32[4,3,4,8,128]{4,3,2,1,0:T(8,128)} %get-tuple-element.27), calls=%async_computation.1 | async-start | bytes 393216 | tf_op jit(solution)/shard_map/all_to_all | solution.py:370
  47.0 15.7 %all-to-all-done.1.got_ref = f32[4,3,4,8,128]{4,3,2,1,0:T(8,128)S(1)} async-done(((f32[4,3,4,8,128]{4,3,2,1,0:T(8,128)}), f32[4,3,4,8,128]{4,3,2,1,0:T(8,128)S(1)}, u32[]{:S(2)}, u32[]{:S(2)}) %all-to-all-start.1) | async-done | bytes 196640 | tf_op jit(solution)/shard_map/all_to_all | solution.py:370
  62.7 0.1 return_part.2
  62.8 16.4 %all_to_all.31 = f32[16,4,8,128]{3,2,1,0:T(8,128)S(1)} all-to-all(f32[16,4,8,128]{3,2,1,0:T(8,128)S(1)} %get-tuple-element.32), channel_id=1, replica_groups=mesh['zh'=4,'zi'=16,'gy'=8] {'zi'}, dimensions={0} | all-to-all | bytes 524288 | tf_op jit(solution)/shard_map/all_to_all | solution.py:367
  79.2 0.8 finish_part.2
  80.0 0.0 collective-permute-start.2
  80.0 1.7 %collective-permute-start.3 = (f32[16,2,512]{2,1,0:T(2,128)S(1)}, f32[16,2,512]{2,1,0:T(2,128)S(1)}, u32[]{:S(2)}, u32[]{:S(2)}) collective-permute-start(f32[16,2,512]{2,1,0:T(2,128)S(1)} %get-tuple-element.35), channel_id=1, source_target_pairs={{1,0},{2,1},{3,2},{4,3},{5,4},{6,5},{7,6},{0,7},{9,8},{10,9},{11,1... | collective-permute-start | bytes 196616 | tf_op jit(solution)/shard_map/ppermute | solution.py:376
  81.8 1.9 %collective-permute-done.2.south_ref = f32[16,2,512]{2,1,0:T(2,128)S(1)} collective-permute-done((f32[16,2,512]{2,1,0:T(2,128)S(1)}, f32[16,2,512]{2,1,0:T(2,128)S(1)}, u32[]{:S(2)}, u32[]{:S(2)}) %collective-permute-start.2) | collective-permute-done | bytes 65568 | tf_op jit(solution)/shard_map/ppermute | solution.py:375
  83.7 0.0 collective-permute-done.3.north_ref
  83.7 0.0 copy-done.1
  83.7 2.6 %explicit_part.3 = (f32[16,16,512]{2,1,0:T(8,128)S(1)}, f32[512,128]{1,0:T(8,128)S(1)}) custom-call(f32[4]{0:T(128)S(1)} %copy-done.5, f32[4]{0:T(128)S(1)} %copy-done.4, f32[16,16,512]{2,1,0:T(8,128)S(1)} %get-tuple-element.33.present_ref, f32[16,2,512]{2,1,0:T(2,128)S(1)} %collective-permute-done.2.south_ref, ...), custom_call_target="tpu_custom_call" | custom-call | tf_op jit(solution)/shard_map/explicit_part/pallas_call | solution.py:295
  86.3 15.5 %all_to_all.32.got_ref = f32[16,1,4,8,128]{4,3,2,1,0:T(8,128)S(1)} all-to-all(f32[16,1,4,8,128]{4,3,2,1,0:T(8,128)S(1)} %bitcast.16), channel_id=1, replica_groups=mesh['zh'=4,'zi'=16,'gy'=8] {'zi'}, dimensions={0} | all-to-all | bytes 524288 | tf_op jit(solution)/shard_map/all_to_all | solution.py:367
  101.7 0.6 reduce_part.3
  102.4 16.3 %all_to_all.33.got_ref = f32[4,1,4,8,128]{4,3,2,1,0:T(8,128)S(1)} all-to-all(f32[4,1,4,8,128]{4,3,2,1,0:T(8,128)S(1)} %get-tuple-element.38), channel_id=1, replica_groups=mesh['zh'=4,'zi'=16,'gy'=8] {'zh'}, dimensions={0} | all-to-all | bytes 131072 | tf_op jit(solution)/shard_map/all_to_all | solution.py:370
  118.6 0.1 return_part.3
  118.7 13.6 %all_to_all.34 = f32[16,4,8,128]{3,2,1,0:T(8,128)S(1)} all-to-all(f32[16,4,8,128]{3,2,1,0:T(8,128)S(1)} %return_part.3), channel_id=1, replica_groups=mesh['zh'=4,'zi'=16,'gy'=8] {'zi'}, dimensions={0} | all-to-all | bytes 524288 | tf_op jit(solution)/shard_map/all_to_all | solution.py:367
  132.3 1.6 %finish_part.3 = f32[16,16,512]{2,1,0:T(8,128)} custom-call(f32[4]{0:T(128)S(1)} %copy-done.4, f32[16,16,512]{2,1,0:T(8,128)S(1)} %get-tuple-element.36.explicit_ref, f32[4,16,512]{2,1,0:T(8,128)S(1)} %copy-done.3, f32[512,128]{1,0:T(8,128)S(1)} %bitcast.14), custom_call_target="tpu_custom_call" | custom-call | tf_op jit(solution)/shard_map/finish_part/pallas_call | solution.py:343
  (4 shorter events, 0.0 us)
Async XLA Ops:
  0.0 0.9 copy-start
  1.0 1.0 copy-start.2
  2.0 6.5 %copy-start.3 = (f32[4,16,512]{2,1,0:T(8,128)S(1)}, f32[4,16,512]{2,1,0:T(8,128)}, u32[]{:S(2)}) copy-start(f32[4,16,512]{2,1,0:T(8,128)} %face_ref.7) | copy-start | bytes 393220
  2.0 6.5 %copy-start.4 = (f32[4]{0:T(128)S(1)}, f32[4]{0:T(128)}, u32[]{:S(2)}) copy-start(f32[4]{0:T(128)} %zs_ref.11) | copy-start | bytes 52
  2.0 6.5 %copy-start.5 = (f32[4]{0:T(128)S(1)}, f32[4]{0:T(128)}, u32[]{:S(2)}) copy-start(f32[4]{0:T(128)} %xy_ref.3) | copy-start | bytes 52
  2.1 3.9 %collective-permute-start = (f32[20,2,512]{2,1,0:T(2,128)S(1)}, f32[20,2,512]{2,1,0:T(2,128)S(1)}, u32[]{:S(2)}, u32[]{:S(2)}) collective-permute-start(f32[20,2,512]{2,1,0:T(2,128)S(1)} %get-tuple-element.23), channel_id=1, source_target_pairs={{0,1},{1,2},{2,3},{3,4},{4,5},{5,6},{6,7},{7,0},{8,9},{9,10},{10,1... | collective-permute-start | bytes 245768 | tf_op jit(solution)/shard_map/ppermute | solution.py:360
  2.1 6.4 %collective-permute-start.1 = (f32[20,2,512]{2,1,0:T(2,128)S(1)}, f32[20,2,512]{2,1,0:T(2,128)S(1)}, u32[]{:S(2)}, u32[]{:S(2)}) collective-permute-start(f32[20,2,512]{2,1,0:T(2,128)S(1)} %get-tuple-element.24), channel_id=1, source_target_pairs={{1,0},{2,1},{3,2},{4,3},{5,4},{6,5},{7,6},{0,7},{9,8},{10,9},{11,1... | collective-permute-start | bytes 245768 | tf_op jit(solution)/shard_map/ppermute | solution.py:361
  34.6 28.1 %all-to-all-start.1 = ((f32[4,3,4,8,128]{4,3,2,1,0:T(8,128)}), f32[4,3,4,8,128]{4,3,2,1,0:T(8,128)S(1)}, u32[]{:S(2)}, u32[]{:S(2)}) async-start(f32[4,3,4,8,128]{4,3,2,1,0:T(8,128)} %get-tuple-element.27), calls=%async_computation.1 | async-start | bytes 393216 | tf_op jit(solution)/shard_map/all_to_all | solution.py:370
  79.2 4.5 %copy-start.1 = (f32[2,4,16,512]{3,2,1,0:T(8,128)S(1)}, f32[2,4,16,512]{3,2,1,0:T(8,128)}, u32[]{:S(2)}) copy-start(f32[2,4,16,512]{3,2,1,0:T(8,128)} %param.6) | copy-start | bytes 786436
  80.0 3.7 %collective-permute-start.2 = (f32[16,2,512]{2,1,0:T(2,128)S(1)}, f32[16,2,512]{2,1,0:T(2,128)S(1)}, u32[]{:S(2)}, u32[]{:S(2)}) collective-permute-start(f32[16,2,512]{2,1,0:T(2,128)S(1)} %get-tuple-element.34), channel_id=1, source_target_pairs={{0,1},{1,2},{2,3},{3,4},{4,5},{5,6},{6,7},{7,0},{8,9},{9,10},{10,1... | collective-permute-start | bytes 196616 | tf_op jit(solution)/shard_map/ppermute | solution.py:375
  80.0 3.7 %collective-permute-start.3 = (f32[16,2,512]{2,1,0:T(2,128)S(1)}, f32[16,2,512]{2,1,0:T(2,128)S(1)}, u32[]{:S(2)}, u32[]{:S(2)}) collective-permute-start(f32[16,2,512]{2,1,0:T(2,128)S(1)} %get-tuple-element.35), channel_id=1, source_target_pairs={{1,0},{2,1},{3,2},{4,3},{5,4},{6,5},{7,6},{0,7},{9,8},{10,9},{11,1... | collective-permute-start | bytes 196616 | tf_op jit(solution)/shard_map/ppermute | solution.py:376

commit v4 on v3

--- a/solution.py
+++ b/solution.py
@@ -16,20 +16,14 @@
 GROUPS = 4
 MEMBERS = 16
 PAIRS = MEMBERS // 2
+FACTORS = 7
 LANES = 128
 COLUMNS = WIDTH // LANES
 TILE = (COLUMNS, 8, LANES)
 
 
-def tendency(middle, half_x, half_y, spread):
-    rows = middle.shape[0]
-    eastern = pltpu.roll(middle, WIDTH - 1, 1)
-    western = pltpu.roll(middle, 1, 1)
-    north = pltpu.roll(middle, rows - 1, 0)
-    south = pltpu.roll(middle, 1, 0)
-    return spread * (eastern + western + north + south - 4.0 * middle) - (
-        half_x * (eastern - western) + half_y * (north - south)
-    )
+def columns():
+    return [slice(column * LANES, column * LANES + LANES) for column in range(COLUMNS)]
 
 
 def inner_pivots(rates):
@@ -42,13 +36,16 @@
     return inverse
 
 
-def solve_inner(source, rates, inverse):
-    first = source[0]
-    second = source[1] + rates[1] * inverse[0] * first
-    third = (source[2] + rates[2] * inverse[1] * second) * inverse[2]
-    second = (second + rates[2] * third) * inverse[1]
-    first = (first + rates[1] * second) * inverse[0]
-    return first, second, third
+def inner_factors(rates):
+    inverse = inner_pivots(rates)
+    return [*inverse, rates[1] * inverse[0], rates[2] * inverse[1], rates[0], rates[3]]
+
+
+def solve_inner(source, factors):
+    second = source[1] + factors[3] * source[0]
+    third = (source[2] + factors[4] * second) * factors[2]
+    second = second * factors[1] + factors[4] * third
+    return source[0] * factors[0] + factors[3] * second, second, third
 
 
 def pack_kernel(present_ref, vel_ref, low_ref, high_ref):
@@ -59,47 +56,101 @@
         high_ref[ITEMS + item // 2, item % 2 : item % 2 + 1, :] = vel_ref[item, ROWS - 1 : ROWS, :]
 
 
+def factor_kernel(scale_ref, face_ref, factor_ref):
+    for tile in range(ROWS // 8):
+        rows = slice(tile * 8, tile * 8 + 8)
+        for lanes in columns():
+            faces = [face_ref[level, rows, lanes] for level in range(LEVELS)]
+            for field in range(FIELDS):
+                scale = jnp.broadcast_to(scale_ref[field : field + 1, :], (8, LANES))
+                for item, value in enumerate(inner_factors([scale * face for face in faces])):
+                    factor_ref[item, field, rows, lanes] = value
+
+
 def places(tile, chunk, line):
     for column in range(COLUMNS):
         start = (tile * 8 * (chunk // 8) + line // 8) * COLUMNS * 8 + column * 8 + line % 8
-        yield slice(column * LANES, column * LANES + LANES), pl.ds(start, 8, stride=COLUMNS * chunk)
-
-
-def spread_rows(send_ref, tile, chunk, line, value):
-    for lanes, lines in places(tile, chunk, line):
-        send_ref[lines, :] = value[:, lanes]
-
-
-def explicit_kernel(chunk, xy_ref, zs_ref, present_ref, south_ref, north_ref, vel_ref, vel_south_ref,
-                    vel_north_ref, face_ref, explicit_ref, send_ref, tail_ref, vel_tail_ref):
-    tail_ref[:, 0:2, :] = north_ref[0:ITEMS]
-    tail_ref[:, 6:8, :] = south_ref[0:ITEMS]
-    for item in range(2 * LEVELS):
-        row = slice(item % 2, item % 2 + 1)
-        vel_tail_ref[item, 0:1, :] = vel_north_ref[ITEMS + item // 2, row, :]
-        vel_tail_ref[item, 7:8, :] = vel_south_ref[ITEMS + item // 2, row, :]
+        yield pl.ds(start, 8, stride=COLUMNS * chunk)
+
+
+def along_x(middle, last, begin):
+    ahead = [pltpu.roll(value, LANES - 1, 1) for value in middle]
+    behind = [pltpu.roll(value, 1, 1) for value in middle]
+    for column in range(COLUMNS):
+        eastern = jnp.where(last, ahead[(column + 1) % COLUMNS], ahead[column])
+        western = jnp.where(begin, behind[column - 1], behind[column])
+        yield eastern, western
+
+
+def tendency(middle, eastern, western, north, south, half_x, half_y, spread):
+    return spread * (eastern + western + north + south - 4.0 * middle) - (
+        half_x * (eastern - western) + half_y * (north - south)
+    )
+
+
+def explicit_kernel(chunk, scale_ref, factor_ref, present_ref, south_ref, north_ref, vel_ref, vel_south_ref,
+                    vel_north_ref, face_ref, explicit_ref, send_ref, wide_ref, vel_wide_ref, sectioned_ref):
+    for column, lanes in enumerate(columns()):
+        for item in range(2 * LEVELS):
+            row = slice(item % 2, item % 2 + 1)
+            vel_wide_ref[item, column, 8:24, :] = 0.5 * vel_ref[item, :, lanes]
+            vel_wide_ref[item, column, 7:8, :] = 0.5 * vel_south_ref[ITEMS + item // 2, row, lanes]
+            vel_wide_ref[item, column, 24:25, :] = 0.5 * vel_north_ref[ITEMS + item // 2, row, lanes]
+        for item in range(ITEMS):
+            wide_ref[item, column, 8:24, :] = present_ref[item, :, lanes]
+            wide_ref[item, column, 6:8, :] = south_ref[item, :, lanes]
+            wide_ref[item, column, 24:26, :] = north_ref[item, :, lanes]
+    lane = lax.broadcasted_iota(jnp.int32, (8, LANES), 1)
+    last, begin = lane == LANES - 1, lane == 0
     for level in range(LEVELS):
-        half_x = 0.5 * jnp.concatenate([vel_ref[level], vel_tail_ref[level]], 0)
-        half_y = 0.5 * jnp.concatenate([vel_ref[LEVELS + level], vel_tail_ref[LEVELS + level]], 0)
         for field in range(FIELDS):
             item = field * LEVELS + level
-            spread = xy_ref[field]
-            middle = jnp.concatenate([present_ref[item], tail_ref[item]], 0)
-            sectioned = middle + tendency(middle, half_x, half_y, spread)
-            again = sectioned + tendency(sectioned, half_x, half_y, spread)
-            explicit_ref[item] = (0.5 * middle + 0.5 * again)[:ROWS]
+            spread = jnp.broadcast_to(scale_ref[FIELDS + field : FIELDS + field + 1, :], (8, LANES))
+            for tile in range(3):
+                at = 7 + tile * 8
+                middle = [wide_ref[item, column, at : at + 8, :] for column in range(COLUMNS)]
+                for column, (eastern, western) in enumerate(along_x(middle, last, begin)):
+                    sectioned_ref[item, column, tile * 8 : tile * 8 + 8, :] = middle[column] + tendency(
+                        middle[column],
+                        eastern,
+                        western,
+                        wide_ref[item, column, at + 1 : at + 9, :],
+                        wide_ref[item, column, at - 1 : at + 7, :],
+                        vel_wide_ref[level, column, at : at + 8, :],
+                        vel_wide_ref[LEVELS + level, column, at : at + 8, :],
+                        spread,
+                    )
+            for tile in range(ROWS // 8):
+                at, row = tile * 8 + 1, tile * 8 + 8
+                middle = [sectioned_ref[item, column, at : at + 8, :] for column in range(COLUMNS)]
+                for column, (eastern, western) in enumerate(along_x(middle, last, begin)):
+                    change = tendency(
+                        middle[column],
+                        eastern,
+                        western,
+                        sectioned_ref[item, column, at + 1 : at + 9, :],
+                        sectioned_ref[item, column, at - 1 : at + 7, :],
+                        vel_wide_ref[level, column, row : row + 8, :],
+                        vel_wide_ref[LEVELS + level, column, row : row + 8, :],
+                        spread,
+                    )
+                    explicit_ref[item, tile * 8 : tile * 8 + 8, column * LANES : column * LANES + LANES] = 0.5 * (
+                        wide_ref[item, column, row : row + 8, :] + (middle[column] + change)
+                    )
     for tile in range(ROWS // 8):
         rows = slice(tile * 8, tile * 8 + 8)
         for field in range(FIELDS):
-            scale = zs_ref[field]
-            rates = [scale * face_ref[level, rows, :] for level in range(LEVELS)]
-            source = [explicit_ref[field * LEVELS + level, rows, :] for level in range(LEVELS)]
-            first, _, third = solve_inner(source, rates, inner_pivots(rates))
-            spread_rows(send_ref, tile, chunk, field, source[3] + rates[3] * third)
-            spread_rows(send_ref, tile, chunk, FIELDS + field, rates[0] * first)
+            lines = zip(columns(), places(tile, chunk, field), places(tile, chunk, FIELDS + field), strict=True)
+            for lanes, own, under in lines:
+                factors = [factor_ref[item, field, rows, lanes] for item in range(FACTORS)]
+                source = [explicit_ref[field * LEVELS + level, rows, lanes] for level in range(LEVELS)]
+                first, _, third = solve_inner(source, factors)
+                send_ref[own, :] = source[3] + factors[6] * third
+                send_ref[under, :] = factors[5] * first
         if chunk > 8:
             for level in range(LEVELS):
-                spread_rows(send_ref, tile, chunk, 8 + level, face_ref[level, rows, :])
+                for lanes, line in zip(columns(), places(tile, chunk, 8 + level), strict=True):
+                    send_ref[line, :] = face_ref[level, rows, lanes]
 
 
 def swap(value):
@@ -131,14 +182,11 @@
     return kept, (sources[PAIRS - 1] + value + swap(value)) * center
 
 
-def reduce_kernel(first, zs_ref, got_ref, *refs):
+def reduce_kernel(first, got_ref, *refs):
     low = lower_half()
     if first:
-        weight_ref, gain_ref, edge_ref, source_ref, send_ref = refs
-        field = lax.rem(lax.broadcasted_iota(jnp.int32, TILE, 1), FIELDS)
-        scale = jnp.full(TILE, zs_ref[0], jnp.float32)
-        for other in range(1, FIELDS):
-            scale = jnp.where(field == other, zs_ref[other], scale)
+        scale_ref, weight_ref, gain_ref, edge_ref, source_ref, send_ref = refs
+        scale = jnp.concatenate([scale_ref[0:FIELDS, :]] * 2, 0)[None]
         couple, own, under = [], [], []
         for step in range(PAIRS):
             rates = [
@@ -150,12 +198,12 @@
                 )
                 for level in range(LEVELS)
             ]
-            inverse = inner_pivots(rates)
+            part = inner_factors(rates)
             one = jnp.ones(TILE, jnp.float32)
-            bottom, _, third = solve_inner([one, one, one], rates, inverse)
+            bottom, _, third = solve_inner([one, one, one], part)
             own.append(1.0 + rates[3] * third)
             under.append(rates[0] * bottom)
-            couple.append(rates[0] * inverse[0] * rates[1] * inverse[1] * rates[2] * inverse[2] * rates[3])
+            couple.append(rates[0] * part[3] * part[4] * part[2] * rates[3])
         masses = [
             jnp.where(low, own[step] + under[step + 1], own[step + 1] + under[step]) for step in range(PAIRS - 1)
         ]
@@ -249,30 +297,30 @@
         outer = solved[step]
 
 
-def finish_kernel(edges, zs_ref, explicit_ref, face_ref, back_ref, present_ref, *edge_refs):
+def finish_kernel(edges, factor_ref, explicit_ref, back_ref, present_ref, *edge_refs):
     for tile in range(ROWS // 8):
         rows = slice(tile * 8, tile * 8 + 8)
         for field in range(FIELDS):
-            scale = zs_ref[field]
-            rates = [scale * face_ref[level, rows, :] for level in range(LEVELS)]
-            source = [explicit_ref[field * LEVELS + level, rows, :] for level in range(LEVELS - 1)]
-            below = jnp.concatenate([back_ref[lines, :] for _, lines in places(tile, 8, field)], 1)
-            top = jnp.concatenate([back_ref[lines, :] for _, lines in places(tile, 8, FIELDS + field)], 1)
-            source[0] = source[0] + rates[0] * below
-            source[2] = source[2] + rates[3] * top
-            solved = solve_inner(source, rates, inner_pivots(rates)) + (top,)
-            for level in range(LEVELS):
-                item = field * LEVELS + level
-                present_ref[item, rows, :] = solved[level]
-                if edges and tile == 0:
-                    edge_refs[0][item] = solved[level][0:2]
-                if edges and tile == 1:
-                    edge_refs[1][item] = solved[level][6:8]
+            lines = zip(columns(), places(tile, 8, field), places(tile, 8, FIELDS + field), strict=True)
+            for lanes, below, top in lines:
+                factors = [factor_ref[item, field, rows, lanes] for item in range(FACTORS)]
+                source = [explicit_ref[field * LEVELS + level, rows, lanes] for level in range(LEVELS - 1)]
+                top = back_ref[top, :]
+                source[0] = source[0] + factors[5] * back_ref[below, :]
+                source[2] = source[2] + factors[6] * top
+                solved = solve_inner(source, factors) + (top,)
+                for level in range(LEVELS):
+                    item = field * LEVELS + level
+                    present_ref[item, rows, lanes] = solved[level]
+                    if edges and tile == 0:
+                        edge_refs[0][item, :, lanes] = solved[level][0:2]
+                    if edges and tile == 1:
+                        edge_refs[1][item, :, lanes] = solved[level][6:8]
 
 
 VMEM = pl.BlockSpec(memory_space=pltpu.VMEM)
 SMEM = pl.BlockSpec(memory_space=pltpu.SMEM)
-PARAMS = pltpu.CompilerParams(vmem_limit_bytes=6 << 20)
+PARAMS = pltpu.CompilerParams(vmem_limit_bytes=8 << 20)
 
 
 def struct(*shape):
@@ -280,10 +328,10 @@
 
 
 def pack_part(present, vel):
-    shape = struct(ITEMS + LEVELS, 2, WIDTH)
+    edge = struct(ITEMS + LEVELS, 2, WIDTH)
     return pl.pallas_call(
         pack_kernel,
-        out_shape=(shape, shape),
+        out_shape=(edge, edge),
         in_specs=[VMEM, VMEM],
         out_specs=(VMEM, VMEM),
         compiler_params=PARAMS,
@@ -291,22 +339,34 @@
     )(present, vel)
 
 
+def factor_part(scale, faces):
+    return pl.pallas_call(
+        factor_kernel,
+        out_shape=struct(FACTORS, FIELDS, ROWS, WIDTH),
+        in_specs=[VMEM, VMEM],
+        out_specs=VMEM,
+        compiler_params=PARAMS,
+        name="factor_part",
+    )(scale, faces)
+
+
 def explicit_part(chunk, *operands):
     return pl.pallas_call(
         functools.partial(explicit_kernel, chunk),
         out_shape=(struct(ITEMS, ROWS, WIDTH), struct(MEMBERS * COLUMNS * chunk, LANES)),
-        in_specs=[SMEM, SMEM] + [VMEM] * 7,
+        in_specs=[VMEM] * 9,
         out_specs=(VMEM, VMEM),
         scratch_shapes=[
-            pltpu.VMEM((ITEMS, 8, WIDTH), jnp.float32),
-            pltpu.VMEM((2 * LEVELS, 8, WIDTH), jnp.float32),
+            pltpu.VMEM((ITEMS, COLUMNS, 32, LANES), jnp.float32),
+            pltpu.VMEM((2 * LEVELS, COLUMNS, 32, LANES), jnp.float32),
+            pltpu.VMEM((ITEMS, COLUMNS, 24, LANES), jnp.float32),
         ],
         compiler_params=PARAMS,
         name="explicit_part",
     )(*operands)
 
 
-def reduce_part(scale, got, factors=None):
+def reduce_part(got, factors=None, scale=None):
     shapes = (struct(PAIRS, *TILE), struct(PAIRS - 1, *TILE), struct(*TILE))
     outs = (struct(PAIRS, *TILE), struct(GROUPS, 1 if factors else 3, *TILE))
     if not factors:
@@ -314,11 +374,11 @@
     return pl.pallas_call(
         functools.partial(reduce_kernel, not factors),
         out_shape=outs,
-        in_specs=[SMEM, VMEM] + [VMEM] * (3 if factors else 0),
+        in_specs=[VMEM] * (4 if factors else 2),
         out_specs=(VMEM,) * len(outs),
         compiler_params=PARAMS,
         name="reduce_part",
-    )(scale, got, *(factors or ()))
+    )(got, *(factors or (scale,)))
 
 
 def return_part(place, got, sources, factors, top=None):
@@ -343,7 +403,7 @@
     return pl.pallas_call(
         functools.partial(finish_kernel, edges),
         out_shape=tuple(shapes),
-        in_specs=[SMEM] + [VMEM] * 3,
+        in_specs=[VMEM] * 3,
         out_specs=(VMEM,) * len(shapes),
         compiler_params=PARAMS,
         name="finish_part",
@@ -354,14 +414,17 @@
     count = lax.axis_size("gy")
     up = [(i, (i + 1) % count) for i in range(count)]
     down = [(target, source) for source, target in up]
+    scale = jnp.broadcast_to(jnp.concatenate([z_scale, xy_rate])[:, None], (2 * FIELDS, LANES))
+    place = lax.axis_index("zh").astype(jnp.int32).reshape(1)
+    scale, place = lax.optimization_barrier((scale, place))
+
     present = fields.reshape(ITEMS, ROWS, WIDTH)
     vel = velocity.reshape(2 * LEVELS, ROWS, WIDTH)
+    faces = face_rate
     lowest, highest = pack_part(present, vel)
-    south = lax.ppermute(highest, "gy", up)
-    north = lax.ppermute(lowest, "gy", down)
-    vel_south, vel_north = south, north
-
-    place = lax.axis_index("zh").astype(jnp.int32).reshape(1)
+    south = vel_south = lax.ppermute(highest, "gy", up)
+    north = vel_north = lax.ppermute(lowest, "gy", down)
+    inner = factor_part(scale, faces)
 
     def near(chunks):
         return lax.all_to_all(chunks, "zi", 0, 0, tiled=True)
@@ -376,15 +439,15 @@
             north = lax.ppermute(lowest, "gy", down)
         chunk = 8 if factors else 16
         explicit, send = explicit_part(
-            chunk, xy_rate, z_scale, present, south, north, vel, vel_south, vel_north, face_rate
+            chunk, scale, inner, present, south, north, vel, vel_south, vel_north, faces
         )
         got = near(send.reshape(MEMBERS, chunk // 8, *TILE))
-        *made, sources, ports = reduce_part(z_scale, got, factors)
+        *made, sources, ports = reduce_part(got, factors, scale)
         factors = factors or tuple(made)
         *made, back = return_part(place, far(ports), sources, factors, top)
         top = made[0] if made else top
         present, *edges = finish_part(
-            step + 1 < STEPS, z_scale, explicit, face_rate, near(back).reshape(MEMBERS * COLUMNS * 8, LANES)
+            step + 1 < STEPS, inner, explicit, near(back).reshape(MEMBERS * COLUMNS * 8, LANES)
         )
         if edges:
             lowest, highest = edges

time: 135 us -> 130 us (0.963)
  blocking collectives: 83.6 us -> 112 us
  waiting for transfers between devices: 22.4 us -> 5.73 us
  starting transfers between devices: 15.9 us -> 3.5 us
  Pallas kernels: 9.9 us -> 6.01 us
    all_to_all x1 -> x2, blocking collectives: 16.3 us -> 44.1 us  [far(): return lax.all_to_all(chunks, 'zh', 0, 0, tiled=True)]
    all_to_all x1 -> x0, waiting for transfers between devices: 15.7 us -> none  [far(): return lax.all_to_all(chunks, 'zh', 0, 0, tiled=True)]
    all_to_all x1 -> x0, starting transfers between devices: 12.4 us -> none  [far(): return lax.all_to_all(chunks, 'zh', 0, 0, tiled=True)]
    ppermute x0 -> x2, waiting for transfers between devices: none -> 3.78 us  [the longest x1 2.59 us: on_device(): north = vel_north = lax.ppermute(lowest, 'gy', down)]
    ppermute x2 -> x1, waiting for transfers between devices: 2.59 us -> 0.01 us  [on_device(): north = lax.ppermute(lowest, 'gy', down)]
    ppermute x2 -> x1, waiting for transfers between devices: 4.06 us -> 1.94 us  [on_device(): south = lax.ppermute(highest, 'gy', up)]
    ppermute x0 -> x2, starting transfers between devices: none -> 1.75 us  [the longest x1 1.73 us: on_device(): north = vel_north = lax.ppermute(lowest, 'gy', down)]
    pallas_call x2, Pallas kernels: 2.15 us -> 0.4 us  [reduce_part(): pl.pallas_call(functools.partial(reduce_kernel, not factors), out_shape=o...]
  transfers between devices with their start and end apart: 5 -> 4, of which waited for: 4 -> 3; matrix products, arithmetic and copies ran while one was open for 0% -> 0% of each run, Pallas kernels for 0% -> 0%
where the time goes in v4:
time: 130 us
  blocking collectives  112 us (86%)
  Pallas kernels  6.01 us (5%)
  waiting for transfers between devices  5.73 us (4%)
  starting transfers between devices  3.5 us (3%)
  local copies, waits for them, and re-layouts  2.74 us (2%)
    all_to_all x4, blocking collectives, near(): return lax.all_to_all(chunks, 'zi', 0, 0, tiled=True)  67.5 us
    all_to_all x2, blocking collectives, far(): return lax.all_to_all(chunks, 'zh', 0, 0, tiled=True)  44.1 us
    pallas_call x2, Pallas kernels, explicit_part(): pl.pallas_call(functools.partial(explicit_kernel, chunk), out_shape=(stru...  3.92 us
    unnamed x14, local copies, waits for them, and re-layouts  2.67 us
  transfers between devices with their start and end apart: 4, of which 3 were waited for; matrix products, arithmetic and copies ran while one was open for 0% of the time, Pallas kernels for 0%

profile of v4, /device:TPU:24, one launch (start us, length us, event | category | flops | bytes accessed | tf_op | source)
XLA Modules:
  0.0 129.8 jit_solution(5037001445128283457)
XLA Ops:
  0.0 0.9 copy-done
  1.0 1.0 copy-done.2
  2.0 0.0 collective-permute-start
  2.1 1.7 %collective-permute-start.1 = (f32[20,2,512]{2,1,0:T(2,128)S(1)}, f32[20,2,512]{2,1,0:T(2,128)S(1)}, u32[]{:S(2)}, u32[]{:S(2)}) collective-permute-start(f32[20,2,512]{2,1,0:T(2,128)S(1)} %get-tuple-element.27), channel_id=1, source_target_pairs={{1,0},{2,1},{3,2},{4,3},{5,4},{6,5},{7,6},{0,7},{9,8},{10,9},{11,1... | collective-permute-start | bytes 245768 | tf_op jit(solution)/shard_map/ppermute | solution.py:426
  3.8 0.7 copy-done.5
  4.4 0.0 copy-done.6
  4.5 0.1 pad_maximum_fusion
  4.5 0.1 broadcast_in_dim.2.scale_ref.refs_0_
  4.6 0.0 copy-done.4
  4.6 0.1 factor_part.1.factor_ref
  4.7 1.2 collective-permute-done.south_ref.vel_south_ref
  5.9 2.6 %collective-permute-done.1.north_ref.vel_north_ref = f32[20,2,512]{2,1,0:T(2,128)S(1)} collective-permute-done((f32[20,2,512]{2,1,0:T(2,128)S(1)}, f32[20,2,512]{2,1,0:T(2,128)S(1)}, u32[]{:S(2)}, u32[]{:S(2)}) %collective-permute-start.1) | collective-permute-done | bytes 81952 | tf_op jit(solution)/shard_map/ppermute | solution.py:426
  8.5 0.0 copy-done.1
  8.5 0.0 copy-done.3
  8.5 2.0 %explicit_part.2 = (f32[16,16,512]{2,1,0:T(8,128)S(1)}, f32[1024,128]{1,0:T(8,128)S(1)}) custom-call(f32[8,128]{1,0:T(8,128)S(1)} %broadcast_in_dim.2.scale_ref.refs_0_, f32[7,4,16,512]{3,2,1,0:T(8,128)S(1)} %factor_part.1.factor_ref, f32[16,16,512]{2,1,0:T(8,128)S(1)} %bitcast.12, f32[20,2,512]{2,1,0:T(2,128)S(1)} %collective-permute-done.south_ref.vel_south_ref, ...), custom_call_target="tpu_custom_call" | custom-call | tf_op jit(solution)/shard_map/explicit_part/pallas_call | solution.py:354
  10.5 21.9 %all_to_all.30.got_ref = f32[16,2,4,8,128]{4,3,2,1,0:T(8,128)S(1)} all-to-all(f32[16,2,4,8,128]{4,3,2,1,0:T(8,128)S(1)} %bitcast.15), channel_id=1, replica_groups=mesh['zh'=4,'zi'=16,'gy'=8] {'zi'}, dimensions={0} | all-to-all | bytes 1048576 | tf_op jit(solution)/shard_map/all_to_all | solution.py:430
  32.4 0.3 reduce_part.2
  32.8 28.2 %all_to_all.31.got_ref = f32[4,3,4,8,128]{4,3,2,1,0:T(8,128)S(1)} all-to-all(f32[4,3,4,8,128]{4,3,2,1,0:T(8,128)S(1)} %get-tuple-element.31), channel_id=1, replica_groups=mesh['zh'=4,'zi'=16,'gy'=8] {'zh'}, dimensions={0} | all-to-all | bytes 393216 | tf_op jit(solution)/shard_map/all_to_all | solution.py:433
  61.0 0.1 return_part.2
  61.1 16.5 %all_to_all.32 = f32[16,4,8,128]{3,2,1,0:T(8,128)S(1)} all-to-all(f32[16,4,8,128]{3,2,1,0:T(8,128)S(1)} %get-tuple-element.36), channel_id=1, replica_groups=mesh['zh'=4,'zi'=16,'gy'=8] {'zi'}, dimensions={0} | all-to-all | bytes 524288 | tf_op jit(solution)/shard_map/all_to_all | solution.py:430
  77.6 0.3 finish_part.2
  77.9 0.0 collective-permute-start.2
  78.0 1.7 %collective-permute-start.3 = (f32[16,2,512]{2,1,0:T(2,128)S(1)}, f32[16,2,512]{2,1,0:T(2,128)S(1)}, u32[]{:S(2)}, u32[]{:S(2)}) collective-permute-start(f32[16,2,512]{2,1,0:T(2,128)S(1)} %get-tuple-element.39), channel_id=1, source_target_pairs={{1,0},{2,1},{3,2},{4,3},{5,4},{6,5},{7,6},{0,7},{9,8},{10,9},{11,1... | collective-permute-start | bytes 196616 | tf_op jit(solution)/shard_map/ppermute | solution.py:439
  79.7 1.9 %collective-permute-done.2.south_ref = f32[16,2,512]{2,1,0:T(2,128)S(1)} collective-permute-done((f32[16,2,512]{2,1,0:T(2,128)S(1)}, f32[16,2,512]{2,1,0:T(2,128)S(1)}, u32[]{:S(2)}, u32[]{:S(2)}) %collective-permute-start.2) | collective-permute-done | bytes 65568 | tf_op jit(solution)/shard_map/ppermute | solution.py:438
  81.6 0.0 collective-permute-done.3.north_ref
  81.6 1.9 %explicit_part.3 = (f32[16,16,512]{2,1,0:T(8,128)S(1)}, f32[512,128]{1,0:T(8,128)S(1)}) custom-call(f32[8,128]{1,0:T(8,128)S(1)} %broadcast_in_dim.2.scale_ref.refs_0_, f32[7,4,16,512]{3,2,1,0:T(8,128)S(1)} %factor_part.1.factor_ref, f32[16,16,512]{2,1,0:T(8,128)S(1)} %get-tuple-element.37.present_ref, f32[16,2,512]{2,1,0:T(2,128)S(1)} %collective-permute-done.2.south_ref, ...), custom_call_target="tpu_custom_call" | custom-call | tf_op jit(solution)/shard_map/explicit_part/pallas_call | solution.py:354
  83.6 15.4 %all_to_all.33.got_ref = f32[16,1,4,8,128]{4,3,2,1,0:T(8,128)S(1)} all-to-all(f32[16,1,4,8,128]{4,3,2,1,0:T(8,128)S(1)} %bitcast.16), channel_id=1, replica_groups=mesh['zh'=4,'zi'=16,'gy'=8] {'zi'}, dimensions={0} | all-to-all | bytes 524288 | tf_op jit(solution)/shard_map/all_to_all | solution.py:430
  99.0 0.1 reduce_part.3
  99.0 15.9 %all_to_all.34.got_ref = f32[4,1,4,8,128]{4,3,2,1,0:T(8,128)S(1)} all-to-all(f32[4,1,4,8,128]{4,3,2,1,0:T(8,128)S(1)} %get-tuple-element.42), channel_id=1, replica_groups=mesh['zh'=4,'zi'=16,'gy'=8] {'zh'}, dimensions={0} | all-to-all | bytes 131072 | tf_op jit(solution)/shard_map/all_to_all | solution.py:433
  114.9 0.1 return_part.3
  115.0 13.7 %all_to_all.35 = f32[16,4,8,128]{3,2,1,0:T(8,128)S(1)} all-to-all(f32[16,4,8,128]{3,2,1,0:T(8,128)S(1)} %return_part.3), channel_id=1, replica_groups=mesh['zh'=4,'zi'=16,'gy'=8] {'zi'}, dimensions={0} | all-to-all | bytes 524288 | tf_op jit(solution)/shard_map/all_to_all | solution.py:430
  128.7 1.1 finish_part.3
  (8 shorter events, 0.0 us)
Async XLA Ops:
  0.0 0.9 copy-start
  1.0 1.0 copy-start.2
  2.0 2.6 %copy-start.4 = (f32[4,16,512]{2,1,0:T(8,128)S(1)}, f32[4,16,512]{2,1,0:T(8,128)}, u32[]{:S(2)}) copy-start(f32[4,16,512]{2,1,0:T(8,128)} %face_ref.5) | copy-start | bytes 393220
  2.0 3.9 %collective-permute-start = (f32[20,2,512]{2,1,0:T(2,128)S(1)}, f32[20,2,512]{2,1,0:T(2,128)S(1)}, u32[]{:S(2)}, u32[]{:S(2)}) collective-permute-start(f32[20,2,512]{2,1,0:T(2,128)S(1)} %get-tuple-element.26), channel_id=1, source_target_pairs={{0,1},{1,2},{2,3},{3,4},{4,5},{5,6},{6,7},{7,0},{8,9},{9,10},{10,1... | collective-permute-start | bytes 245768 | tf_op jit(solution)/shard_map/ppermute | solution.py:425
  2.1 6.4 %collective-permute-start.1 = (f32[20,2,512]{2,1,0:T(2,128)S(1)}, f32[20,2,512]{2,1,0:T(2,128)S(1)}, u32[]{:S(2)}, u32[]{:S(2)}) collective-permute-start(f32[20,2,512]{2,1,0:T(2,128)S(1)} %get-tuple-element.27), channel_id=1, source_target_pairs={{1,0},{2,1},{3,2},{4,3},{5,4},{6,5},{7,6},{0,7},{9,8},{10,9},{11,1... | collective-permute-start | bytes 245768 | tf_op jit(solution)/shard_map/ppermute | solution.py:426
  3.8 0.7 copy-start.5
  3.8 0.7 copy-start.6
  4.6 3.9 %copy-start.1 = (f32[2,4,16,512]{3,2,1,0:T(8,128)S(1)}, f32[2,4,16,512]{3,2,1,0:T(8,128)}, u32[]{:S(2)}) copy-start(f32[2,4,16,512]{3,2,1,0:T(8,128)} %param.6) | copy-start | bytes 786436
  4.6 3.9 %copy-start.3 = (f32[4,4,16,512]{3,2,1,0:T(8,128)S(1)}, f32[4,4,16,512]{3,2,1,0:T(8,128)}, u32[]{:S(2)}) copy-start(f32[4,4,16,512]{3,2,1,0:T(8,128)} %param.5) | copy-start | bytes 1572868
  77.9 3.7 %collective-permute-start.2 = (f32[16,2,512]{2,1,0:T(2,128)S(1)}, f32[16,2,512]{2,1,0:T(2,128)S(1)}, u32[]{:S(2)}, u32[]{:S(2)}) collective-permute-start(f32[16,2,512]{2,1,0:T(2,128)S(1)} %get-tuple-element.38), channel_id=1, source_target_pairs={{0,1},{1,2},{2,3},{3,4},{4,5},{5,6},{6,7},{7,0},{8,9},{9,10},{10,1... | collective-permute-start | bytes 196616 | tf_op jit(solution)/shard_map/ppermute | solution.py:438
  78.0 3.7 %collective-permute-start.3 = (f32[16,2,512]{2,1,0:T(2,128)S(1)}, f32[16,2,512]{2,1,0:T(2,128)S(1)}, u32[]{:S(2)}, u32[]{:S(2)}) collective-permute-start(f32[16,2,512]{2,1,0:T(2,128)S(1)} %get-tuple-element.39), channel_id=1, source_target_pairs={{1,0},{2,1},{3,2},{4,3},{5,4},{6,5},{7,6},{0,7},{9,8},{10,9},{11,1... | collective-permute-start | bytes 196616 | tf_op jit(solution)/shard_map/ppermute | solution.py:439

commit v5 on v4

--- a/solution.py
+++ b/solution.py
@@ -5,7 +5,7 @@
 from jax import lax
 from jax.experimental import pallas as pl
 from jax.experimental.pallas import tpu as pltpu
-from jax.sharding import Mesh, PartitionSpec as P
+from jax.sharding import PartitionSpec as P
 
 STEPS = 2
 FIELDS = 4
@@ -67,10 +67,18 @@
                     factor_ref[item, field, rows, lanes] = value
 
 
-def places(tile, chunk, line):
+def turned_tile(place_ref, tile):
+    return jnp.where(place_ref[0] >= GROUPS // 2, 1 - tile, tile)
+
+
+def places(tile, parts, line):
     for column in range(COLUMNS):
-        start = (tile * 8 * (chunk // 8) + line // 8) * COLUMNS * 8 + column * 8 + line % 8
-        yield pl.ds(start, 8, stride=COLUMNS * chunk)
+        start = column * 8 + line if line < 8 else face_line(column, line - 8)
+        yield pl.ds(tile * (64 * parts) + start, 8, stride=8 * parts)
+
+
+def face_line(column, level):
+    return (COLUMNS + column // 2) * 8 + column % 2 * LEVELS + level
 
 
 def along_x(middle, last, begin):
@@ -88,7 +96,7 @@
     )
 
 
-def explicit_kernel(chunk, scale_ref, factor_ref, present_ref, south_ref, north_ref, vel_ref, vel_south_ref,
+def explicit_kernel(parts, place_ref, scale_ref, factor_ref, present_ref, south_ref, north_ref, vel_ref, vel_south_ref,
                     vel_north_ref, face_ref, explicit_ref, send_ref, wide_ref, vel_wide_ref, sectioned_ref):
     for column, lanes in enumerate(columns()):
         for item in range(2 * LEVELS):
@@ -102,54 +110,65 @@
             wide_ref[item, column, 24:26, :] = north_ref[item, :, lanes]
     lane = lax.broadcasted_iota(jnp.int32, (8, LANES), 1)
     last, begin = lane == LANES - 1, lane == 0
-    for level in range(LEVELS):
-        for field in range(FIELDS):
-            item = field * LEVELS + level
-            spread = jnp.broadcast_to(scale_ref[FIELDS + field : FIELDS + field + 1, :], (8, LANES))
-            for tile in range(3):
-                at = 7 + tile * 8
-                middle = [wide_ref[item, column, at : at + 8, :] for column in range(COLUMNS)]
-                for column, (eastern, western) in enumerate(along_x(middle, last, begin)):
-                    sectioned_ref[item, column, tile * 8 : tile * 8 + 8, :] = middle[column] + tendency(
-                        middle[column],
-                        eastern,
-                        western,
-                        wide_ref[item, column, at + 1 : at + 9, :],
-                        wide_ref[item, column, at - 1 : at + 7, :],
-                        vel_wide_ref[level, column, at : at + 8, :],
-                        vel_wide_ref[LEVELS + level, column, at : at + 8, :],
-                        spread,
-                    )
-            for tile in range(ROWS // 8):
-                at, row = tile * 8 + 1, tile * 8 + 8
-                middle = [sectioned_ref[item, column, at : at + 8, :] for column in range(COLUMNS)]
-                for column, (eastern, western) in enumerate(along_x(middle, last, begin)):
-                    change = tendency(
-                        middle[column],
-                        eastern,
-                        western,
-                        sectioned_ref[item, column, at + 1 : at + 9, :],
-                        sectioned_ref[item, column, at - 1 : at + 7, :],
-                        vel_wide_ref[level, column, row : row + 8, :],
-                        vel_wide_ref[LEVELS + level, column, row : row + 8, :],
-                        spread,
-                    )
-                    explicit_ref[item, tile * 8 : tile * 8 + 8, column * LANES : column * LANES + LANES] = 0.5 * (
-                        wide_ref[item, column, row : row + 8, :] + (middle[column] + change)
-                    )
+
+    def section(item, tile):
+        field, level = divmod(item, LEVELS)
+        spread = jnp.broadcast_to(scale_ref[FIELDS + field : FIELDS + field + 1, :], (8, LANES))
+        at = 7 + tile * 8
+        middle = [wide_ref[item, column, at : at + 8, :] for column in range(COLUMNS)]
+        for column, (eastern, western) in enumerate(along_x(middle, last, begin)):
+            sectioned_ref[item, column, tile * 8 : tile * 8 + 8, :] = middle[column] + tendency(
+                middle[column],
+                eastern,
+                western,
+                wide_ref[item, column, at + 1 : at + 9, :],
+                wide_ref[item, column, at - 1 : at + 7, :],
+                vel_wide_ref[level, column, at : at + 8, :],
+                vel_wide_ref[LEVELS + level, column, at : at + 8, :],
+                spread,
+            )
+
+    def average(item, tile):
+        field, level = divmod(item, LEVELS)
+        spread = jnp.broadcast_to(scale_ref[FIELDS + field : FIELDS + field + 1, :], (8, LANES))
+        at, row = tile * 8 + 1, tile * 8 + 8
+        middle = [sectioned_ref[item, column, at : at + 8, :] for column in range(COLUMNS)]
+        for column, (eastern, western) in enumerate(along_x(middle, last, begin)):
+            change = tendency(
+                middle[column],
+                eastern,
+                western,
+                sectioned_ref[item, column, at + 1 : at + 9, :],
+                sectioned_ref[item, column, at - 1 : at + 7, :],
+                vel_wide_ref[level, column, row : row + 8, :],
+                vel_wide_ref[LEVELS + level, column, row : row + 8, :],
+                spread,
+            )
+            explicit_ref[item, tile * 8 : tile * 8 + 8, column * LANES : column * LANES + LANES] = 0.5 * (
+                wide_ref[item, column, row : row + 8, :] + (middle[column] + change)
+            )
+
+    order = [field * LEVELS + level for level in range(LEVELS) for field in range(FIELDS)]
+    for turn in range(ITEMS + 1):
+        for tile in range(3):
+            if turn < ITEMS:
+                section(order[turn], tile)
+            if turn > 0 and tile < ROWS // 8:
+                average(order[turn - 1], tile)
     for tile in range(ROWS // 8):
         rows = slice(tile * 8, tile * 8 + 8)
+        target = turned_tile(place_ref, tile)
         for field in range(FIELDS):
-            lines = zip(columns(), places(tile, chunk, field), places(tile, chunk, FIELDS + field), strict=True)
+            lines = zip(columns(), places(target, parts, field), places(target, parts, FIELDS + field), strict=True)
             for lanes, own, under in lines:
                 factors = [factor_ref[item, field, rows, lanes] for item in range(FACTORS)]
                 source = [explicit_ref[field * LEVELS + level, rows, lanes] for level in range(LEVELS)]
                 first, _, third = solve_inner(source, factors)
                 send_ref[own, :] = source[3] + factors[6] * third
                 send_ref[under, :] = factors[5] * first
-        if chunk > 8:
+        if parts > COLUMNS:
             for level in range(LEVELS):
-                for lanes, line in zip(columns(), places(tile, chunk, 8 + level), strict=True):
+                for lanes, line in zip(columns(), places(target, parts, 8 + level), strict=True):
                     send_ref[line, :] = face_ref[level, rows, lanes]
 
 
@@ -163,13 +182,13 @@
 
 def pair_sources(got_ref, low):
     def side(block):
-        return got_ref[block, 0] + swap(got_ref[block + 1, 0])
+        return got_ref[block, 0:COLUMNS] + swap(got_ref[block + 1, 0:COLUMNS])
 
     return [jnp.where(low, side(step), swap(side(MEMBERS - 2 - step))) for step in range(PAIRS)]
 
 
 def outer_source(got_ref, low):
-    return jnp.where(low, swap(got_ref[0, 0]), swap(got_ref[MEMBERS - 1, 0]))
+    return jnp.where(low, swap(got_ref[0, 0:COLUMNS]), swap(got_ref[MEMBERS - 1, 0:COLUMNS]))
 
 
 def eliminate(sources, gain_ref, center):
@@ -180,6 +199,14 @@
         kept.append(value)
     value = gain_ref[PAIRS - 2] * value
     return kept, (sources[PAIRS - 1] + value + swap(value)) * center
+
+
+def face_rows(got_ref, block, level):
+    rows = []
+    for column in range(COLUMNS):
+        tile, line = divmod(face_line(column, level), 8)
+        rows.append(jnp.broadcast_to(got_ref[block, tile, line : line + 1, :], (8, LANES)))
+    return jnp.stack(rows)
 
 
 def reduce_kernel(first, got_ref, *refs):
@@ -193,8 +220,8 @@
                 scale
                 * jnp.where(
                     low,
-                    jnp.broadcast_to(got_ref[step, 1, :, level : level + 1, :], TILE),
-                    jnp.broadcast_to(got_ref[MEMBERS - 1 - step, 1, :, level : level + 1, :], TILE),
+                    face_rows(got_ref, step, level),
+                    face_rows(got_ref, MEMBERS - 1 - step, level),
                 )
                 for level in range(LEVELS)
             ]
@@ -297,11 +324,12 @@
         outer = solved[step]
 
 
-def finish_kernel(edges, factor_ref, explicit_ref, back_ref, present_ref, *edge_refs):
+def finish_kernel(edges, place_ref, factor_ref, explicit_ref, back_ref, present_ref, *edge_refs):
     for tile in range(ROWS // 8):
         rows = slice(tile * 8, tile * 8 + 8)
+        target = turned_tile(place_ref, tile)
         for field in range(FIELDS):
-            lines = zip(columns(), places(tile, 8, field), places(tile, 8, FIELDS + field), strict=True)
+            lines = zip(columns(), places(target, COLUMNS, field), places(target, COLUMNS, FIELDS + field), strict=True)
             for lanes, below, top in lines:
                 factors = [factor_ref[item, field, rows, lanes] for item in range(FACTORS)]
                 source = [explicit_ref[field * LEVELS + level, rows, lanes] for level in range(LEVELS - 1)]
@@ -350,11 +378,11 @@
     )(scale, faces)
 
 
-def explicit_part(chunk, *operands):
-    return pl.pallas_call(
-        functools.partial(explicit_kernel, chunk),
-        out_shape=(struct(ITEMS, ROWS, WIDTH), struct(MEMBERS * COLUMNS * chunk, LANES)),
-        in_specs=[VMEM] * 9,
+def explicit_part(parts, *operands):
+    return pl.pallas_call(
+        functools.partial(explicit_kernel, parts),
+        out_shape=(struct(ITEMS, ROWS, WIDTH), struct(MEMBERS * parts * 8, LANES)),
+        in_specs=[SMEM] + [VMEM] * 9,
         out_specs=(VMEM, VMEM),
         scratch_shapes=[
             pltpu.VMEM((ITEMS, COLUMNS, 32, LANES), jnp.float32),
@@ -403,7 +431,7 @@
     return pl.pallas_call(
         functools.partial(finish_kernel, edges),
         out_shape=tuple(shapes),
-        in_specs=[VMEM] * 3,
+        in_specs=[SMEM] + [VMEM] * 3,
         out_specs=(VMEM,) * len(shapes),
         compiler_params=PARAMS,
         name="finish_part",
@@ -415,7 +443,7 @@
     up = [(i, (i + 1) % count) for i in range(count)]
     down = [(target, source) for source, target in up]
     scale = jnp.broadcast_to(jnp.concatenate([z_scale, xy_rate])[:, None], (2 * FIELDS, LANES))
-    place = lax.axis_index("zh").astype(jnp.int32).reshape(1)
+    place = (lax.axis_index("gz") // MEMBERS).astype(jnp.int32).reshape(1)
     scale, place = lax.optimization_barrier((scale, place))
 
     present = fields.reshape(ITEMS, ROWS, WIDTH)
@@ -426,28 +454,33 @@
     north = vel_north = lax.ppermute(lowest, "gy", down)
     inner = factor_part(scale, faces)
 
+    near_groups = [[group * MEMBERS + member for member in range(MEMBERS)] for group in range(GROUPS)]
+    far_groups = [
+        [group * MEMBERS + (row + group // 2 * 8) % MEMBERS for group in range(GROUPS)] for row in range(MEMBERS)
+    ]
+
     def near(chunks):
-        return lax.all_to_all(chunks, "zi", 0, 0, tiled=True)
+        return lax.all_to_all(chunks, "gz", 0, 0, tiled=True, axis_index_groups=near_groups)
 
     def far(chunks):
-        return lax.all_to_all(chunks, "zh", 0, 0, tiled=True)
+        return lax.all_to_all(chunks, "gz", 0, 0, tiled=True, axis_index_groups=far_groups)
 
     factors = top = None
     for step in range(STEPS):
         if step > 0:
             south = lax.ppermute(highest, "gy", up)
             north = lax.ppermute(lowest, "gy", down)
-        chunk = 8 if factors else 16
+        parts = COLUMNS if factors else COLUMNS + 2
         explicit, send = explicit_part(
-            chunk, scale, inner, present, south, north, vel, vel_south, vel_north, faces
+            parts, place, scale, inner, present, south, north, vel, vel_south, vel_north, faces
         )
-        got = near(send.reshape(MEMBERS, chunk // 8, *TILE))
+        got = near(send.reshape(MEMBERS, parts, 8, LANES))
         *made, sources, ports = reduce_part(got, factors, scale)
         factors = factors or tuple(made)
         *made, back = return_part(place, far(ports), sources, factors, top)
         top = made[0] if made else top
         present, *edges = finish_part(
-            step + 1 < STEPS, inner, explicit, near(back).reshape(MEMBERS * COLUMNS * 8, LANES)
+            step + 1 < STEPS, place, inner, explicit, near(back).reshape(MEMBERS * COLUMNS * 8, LANES)
         )
         if edges:
             lowest, highest = edges
@@ -455,10 +488,8 @@
 
 
 def solution(mesh):
-    split = Mesh(mesh.devices.reshape(GROUPS, MEMBERS, -1), ("zh", "zi", "gy"))
-    depth = ("zh", "zi")
-    in_specs = (P(None, depth, "gy", None), P(None, depth, "gy", None), P(depth, "gy", None), P(), P())
-    out_specs = P(None, depth, "gy", None)
+    in_specs = (P(None, "gz", "gy", None), P(None, "gz", "gy", None), P("gz", "gy", None), P(), P())
+    out_specs = P(None, "gz", "gy", None)
     return jax.shard_map(
-        on_device, mesh=split, in_specs=in_specs, out_specs=out_specs, check_vma=False
+        on_device, mesh=mesh, in_specs=in_specs, out_specs=out_specs, check_vma=False
     )

time: 130 us -> 124 us (0.954)
  blocking collectives: 112 us -> 106 us
    all_to_all x6, blocking collectives: 112 us -> 106 us  [the longest x4 64.7 us: near(): lax.all_to_all(chunks, 'gz', 0, 0, tiled=True, axis_index_groups=near_gro...]
where the time goes in v5:
time: 124 us
  blocking collectives  106 us (85%)
  waiting for transfers between devices  5.73 us (5%)
  Pallas kernels  5.36 us (4%)
  starting transfers between devices  3.5 us (3%)
  local copies, waits for them, and re-layouts  2.74 us (2%)
    all_to_all x4, blocking collectives, near(): lax.all_to_all(chunks, 'gz', 0, 0, tiled=True, axis_index_groups=near_gro...  64.7 us
    all_to_all x2, blocking collectives, far(): lax.all_to_all(chunks, 'gz', 0, 0, tiled=True, axis_index_groups=far_groups)  41.4 us
    pallas_call x2, Pallas kernels, explicit_part(): pl.pallas_call(functools.partial(explicit_kernel, parts), out_shape=(stru...  3.31 us
    unnamed x14, local copies, waits for them, and re-layouts  2.67 us
    ppermute x1, waiting for transfers between devices, on_device(): north = vel_north = lax.ppermute(lowest, 'gy', down)  2.59 us
  transfers between devices with their start and end apart: 4, of which 3 were waited for; matrix products, arithmetic and copies ran while one was open for 0% of the time, Pallas kernels for 0%

profile of v5, /device:TPU:24, one launch (start us, length us, event | category | flops | bytes accessed | tf_op | source)
XLA Modules:
  0.0 123.6 jit_solution(546031551587984353)
XLA Ops:
  0.0 0.9 copy-done
  1.0 1.0 copy-done.2
  2.0 0.0 collective-permute-start
  2.1 1.7 %collective-permute-start.1 = (f32[20,2,512]{2,1,0:T(2,128)S(1)}, f32[20,2,512]{2,1,0:T(2,128)S(1)}, u32[]{:S(2)}, u32[]{:S(2)}) collective-permute-start(f32[20,2,512]{2,1,0:T(2,128)S(1)} %get-tuple-element.28), channel_id=1, source_target_pairs={{1,0},{2,1},{3,2},{4,3},{5,4},{6,5},{7,6},{0,7},{9,8},{10,9},{11,1... | collective-permute-start | bytes 245768 | tf_op jit(solution)/shard_map/ppermute | solution.py:454
  3.8 0.7 copy-done.5
  4.4 0.0 copy-done.6
  4.5 0.1 pad_maximum_fusion
  4.5 0.1 broadcast_in_dim.2.scale_ref.refs_0_
  4.6 0.0 copy-done.4
  4.6 0.1 factor_part.1.factor_ref
  4.7 1.2 collective-permute-done.south_ref.vel_south_ref
  5.9 2.6 %collective-permute-done.1.north_ref.vel_north_ref = f32[20,2,512]{2,1,0:T(2,128)S(1)} collective-permute-done((f32[20,2,512]{2,1,0:T(2,128)S(1)}, f32[20,2,512]{2,1,0:T(2,128)S(1)}, u32[]{:S(2)}, u32[]{:S(2)}) %collective-permute-start.1) | collective-permute-done | bytes 81952 | tf_op jit(solution)/shard_map/ppermute | solution.py:454
  8.5 0.0 copy-done.1
  8.5 0.0 copy-done.3
  8.5 1.6 %explicit_part.2 = (f32[16,16,512]{2,1,0:T(8,128)S(1)}, f32[768,128]{1,0:T(8,128)S(1)}) custom-call(s32[1]{0:T(128)} %bitcast.place_ref, f32[8,128]{1,0:T(8,128)S(1)} %broadcast_in_dim.2.scale_ref.refs_0_, f32[7,4,16,512]{3,2,1,0:T(8,128)S(1)} %factor_part.1.factor_ref, f32[16,16,512]{2,1,0:T(8,128)S(1)} %bitcast.12, ...), custom_call_target="tpu_custom_call" | custom-call | tf_op jit(solution)/shard_map/explicit_part/pallas_call | solution.py:382
  10.1 19.7 %all_to_all.30.got_ref = f32[16,6,8,128]{3,2,1,0:T(8,128)S(1)} all-to-all(f32[16,6,8,128]{3,2,1,0:T(8,128)S(1)} %bitcast.15), channel_id=1, replica_groups={{0,8,16,24,32,40,48,56,64,72,80,88,96,104,112,120},{128,136,144,152,160..., dimensions={0} | all-to-all | bytes 786432 | tf_op jit(solution)/shard_map/all_to_all | solution.py:463
  29.8 0.3 reduce_part.2
  30.2 27.2 %all_to_all.31.got_ref = f32[4,3,4,8,128]{4,3,2,1,0:T(8,128)S(1)} all-to-all(f32[4,3,4,8,128]{4,3,2,1,0:T(8,128)S(1)} %get-tuple-element.31), channel_id=1, replica_groups={{0,128,320,448},{8,136,328,456},{16,144,336,464},{24,152,344,472},{32,1..., dimensions={0} | all-to-all | bytes 393216 | tf_op jit(solution)/shard_map/all_to_all | solution.py:466
  57.4 0.1 return_part.2
  57.5 15.3 %all_to_all.32 = f32[16,4,8,128]{3,2,1,0:T(8,128)S(1)} all-to-all(f32[16,4,8,128]{3,2,1,0:T(8,128)S(1)} %get-tuple-element.36), channel_id=1, replica_groups={{0,8,16,24,32,40,48,56,64,72,80,88,96,104,112,120},{128,136,144,152,160..., dimensions={0} | all-to-all | bytes 524288 | tf_op jit(solution)/shard_map/all_to_all | solution.py:463
  72.8 0.3 finish_part.2
  73.1 0.0 collective-permute-start.2
  73.2 1.7 %collective-permute-start.3 = (f32[16,2,512]{2,1,0:T(2,128)S(1)}, f32[16,2,512]{2,1,0:T(2,128)S(1)}, u32[]{:S(2)}, u32[]{:S(2)}) collective-permute-start(f32[16,2,512]{2,1,0:T(2,128)S(1)} %get-tuple-element.39), channel_id=1, source_target_pairs={{1,0},{2,1},{3,2},{4,3},{5,4},{6,5},{7,6},{0,7},{9,8},{10,9},{11,1... | collective-permute-start | bytes 196616 | tf_op jit(solution)/shard_map/ppermute | solution.py:472
  74.9 1.9 %collective-permute-done.2.south_ref = f32[16,2,512]{2,1,0:T(2,128)S(1)} collective-permute-done((f32[16,2,512]{2,1,0:T(2,128)S(1)}, f32[16,2,512]{2,1,0:T(2,128)S(1)}, u32[]{:S(2)}, u32[]{:S(2)}) %collective-permute-start.2) | collective-permute-done | bytes 65568 | tf_op jit(solution)/shard_map/ppermute | solution.py:471
  76.9 0.0 collective-permute-done.3.north_ref
  76.9 1.7 %explicit_part.3 = (f32[16,16,512]{2,1,0:T(8,128)S(1)}, f32[512,128]{1,0:T(8,128)S(1)}) custom-call(s32[1]{0:T(128)} %bitcast.place_ref, f32[8,128]{1,0:T(8,128)S(1)} %broadcast_in_dim.2.scale_ref.refs_0_, f32[7,4,16,512]{3,2,1,0:T(8,128)S(1)} %factor_part.1.factor_ref, f32[16,16,512]{2,1,0:T(8,128)S(1)} %get-tuple-element.37.present_ref, ...), custom_call_target="tpu_custom_call" | custom-call | tf_op jit(solution)/shard_map/explicit_part/pallas_call | solution.py:382
  78.5 14.8 %all_to_all.33.got_ref = f32[16,4,8,128]{3,2,1,0:T(8,128)S(1)} all-to-all(f32[16,4,8,128]{3,2,1,0:T(8,128)S(1)} %bitcast.16), channel_id=1, replica_groups={{0,8,16,24,32,40,48,56,64,72,80,88,96,104,112,120},{128,136,144,152,160..., dimensions={0} | all-to-all | bytes 524288 | tf_op jit(solution)/shard_map/all_to_all | solution.py:463
  93.3 0.1 reduce_part.3
  93.4 14.2 %all_to_all.34.got_ref = f32[4,1,4,8,128]{4,3,2,1,0:T(8,128)S(1)} all-to-all(f32[4,1,4,8,128]{4,3,2,1,0:T(8,128)S(1)} %get-tuple-element.42), channel_id=1, replica_groups={{0,128,320,448},{8,136,328,456},{16,144,336,464},{24,152,344,472},{32,1..., dimensions={0} | all-to-all | bytes 131072 | tf_op jit(solution)/shard_map/all_to_all | solution.py:466
  107.5 0.1 return_part.3
  107.6 14.9 %all_to_all.35 = f32[16,4,8,128]{3,2,1,0:T(8,128)S(1)} all-to-all(f32[16,4,8,128]{3,2,1,0:T(8,128)S(1)} %return_part.3), channel_id=1, replica_groups={{0,8,16,24,32,40,48,56,64,72,80,88,96,104,112,120},{128,136,144,152,160..., dimensions={0} | all-to-all | bytes 524288 | tf_op jit(solution)/shard_map/all_to_all | solution.py:463
  122.6 1.1 finish_part.3
  (8 shorter events, 0.0 us)
Async XLA Ops:
  0.0 0.9 copy-start
  1.0 1.0 copy-start.2
  2.0 2.6 %copy-start.4 = (f32[4,16,512]{2,1,0:T(8,128)S(1)}, f32[4,16,512]{2,1,0:T(8,128)}, u32[]{:S(2)}) copy-start(f32[4,16,512]{2,1,0:T(8,128)} %face_ref.5) | copy-start | bytes 393220
  2.0 3.9 %collective-permute-start = (f32[20,2,512]{2,1,0:T(2,128)S(1)}, f32[20,2,512]{2,1,0:T(2,128)S(1)}, u32[]{:S(2)}, u32[]{:S(2)}) collective-permute-start(f32[20,2,512]{2,1,0:T(2,128)S(1)} %get-tuple-element.27), channel_id=1, source_target_pairs={{0,1},{1,2},{2,3},{3,4},{4,5},{5,6},{6,7},{7,0},{8,9},{9,10},{10,1... | collective-permute-start | bytes 245768 | tf_op jit(solution)/shard_map/ppermute | solution.py:453
  2.1 6.4 %collective-permute-start.1 = (f32[20,2,512]{2,1,0:T(2,128)S(1)}, f32[20,2,512]{2,1,0:T(2,128)S(1)}, u32[]{:S(2)}, u32[]{:S(2)}) collective-permute-start(f32[20,2,512]{2,1,0:T(2,128)S(1)} %get-tuple-element.28), channel_id=1, source_target_pairs={{1,0},{2,1},{3,2},{4,3},{5,4},{6,5},{7,6},{0,7},{9,8},{10,9},{11,1... | collective-permute-start | bytes 245768 | tf_op jit(solution)/shard_map/ppermute | solution.py:454
  3.8 0.7 copy-start.5
  3.8 0.7 copy-start.6
  4.6 3.9 %copy-start.1 = (f32[2,4,16,512]{3,2,1,0:T(8,128)S(1)}, f32[2,4,16,512]{3,2,1,0:T(8,128)}, u32[]{:S(2)}) copy-start(f32[2,4,16,512]{3,2,1,0:T(8,128)} %param.6) | copy-start | bytes 786436
  4.6 3.9 %copy-start.3 = (f32[4,4,16,512]{3,2,1,0:T(8,128)S(1)}, f32[4,4,16,512]{3,2,1,0:T(8,128)}, u32[]{:S(2)}) copy-start(f32[4,4,16,512]{3,2,1,0:T(8,128)} %param.5) | copy-start | bytes 1572868
  73.1 3.7 %collective-permute-start.2 = (f32[16,2,512]{2,1,0:T(2,128)S(1)}, f32[16,2,512]{2,1,0:T(2,128)S(1)}, u32[]{:S(2)}, u32[]{:S(2)}) collective-permute-start(f32[16,2,512]{2,1,0:T(2,128)S(1)} %get-tuple-element.38), channel_id=1, source_target_pairs={{0,1},{1,2},{2,3},{3,4},{4,5},{5,6},{6,7},{7,0},{8,9},{9,10},{10,1... | collective-permute-start | bytes 196616 | tf_op jit(solution)/shard_map/ppermute | solution.py:471
  73.2 3.7 %collective-permute-start.3 = (f32[16,2,512]{2,1,0:T(2,128)S(1)}, f32[16,2,512]{2,1,0:T(2,128)S(1)}, u32[]{:S(2)}, u32[]{:S(2)}) collective-permute-start(f32[16,2,512]{2,1,0:T(2,128)S(1)} %get-tuple-element.39), channel_id=1, source_target_pairs={{1,0},{2,1},{3,2},{4,3},{5,4},{6,5},{7,6},{0,7},{9,8},{10,9},{11,1... | collective-permute-start | bytes 196616 | tf_op jit(solution)/shard_map/ppermute | solution.py:472

commit v6 on v5

--- a/solution.py
+++ b/solution.py
@@ -96,65 +96,136 @@
     )
 
 
-def explicit_kernel(parts, place_ref, scale_ref, factor_ref, present_ref, south_ref, north_ref, vel_ref, vel_south_ref,
-                    vel_north_ref, face_ref, explicit_ref, send_ref, wide_ref, vel_wide_ref, sectioned_ref):
-    for column, lanes in enumerate(columns()):
-        for item in range(2 * LEVELS):
-            row = slice(item % 2, item % 2 + 1)
-            vel_wide_ref[item, column, 8:24, :] = 0.5 * vel_ref[item, :, lanes]
-            vel_wide_ref[item, column, 7:8, :] = 0.5 * vel_south_ref[ITEMS + item // 2, row, lanes]
-            vel_wide_ref[item, column, 24:25, :] = 0.5 * vel_north_ref[ITEMS + item // 2, row, lanes]
-        for item in range(ITEMS):
-            wide_ref[item, column, 8:24, :] = present_ref[item, :, lanes]
-            wide_ref[item, column, 6:8, :] = south_ref[item, :, lanes]
-            wide_ref[item, column, 24:26, :] = north_ref[item, :, lanes]
+def edge_lanes():
     lane = lax.broadcasted_iota(jnp.int32, (8, LANES), 1)
-    last, begin = lane == LANES - 1, lane == 0
+    return lane == LANES - 1, lane == 0
+
+
+def spread_of(scale_ref, field):
+    return jnp.broadcast_to(scale_ref[FIELDS + field : FIELDS + field + 1, :], (8, LANES))
+
+
+ORDER = [field * LEVELS + level for level in range(LEVELS) for field in range(FIELDS)]
+
+
+def interior_kernel(scale_ref, present_ref, vel_ref, explicit_ref, wide_ref, sectioned_ref):
+    last, begin = edge_lanes()
 
     def section(item, tile):
         field, level = divmod(item, LEVELS)
-        spread = jnp.broadcast_to(scale_ref[FIELDS + field : FIELDS + field + 1, :], (8, LANES))
-        at = 7 + tile * 8
-        middle = [wide_ref[item, column, at : at + 8, :] for column in range(COLUMNS)]
+        rows, at = slice(tile * 8, tile * 8 + 8), tile * 8 + 8
+        middle = [present_ref[item, rows, lanes] for lanes in columns()]
         for column, (eastern, western) in enumerate(along_x(middle, last, begin)):
-            sectioned_ref[item, column, tile * 8 : tile * 8 + 8, :] = middle[column] + tendency(
+            lanes = slice(column * LANES, column * LANES + LANES)
+            sectioned_ref[item, column, at : at + 8, :] = middle[column] + tendency(
                 middle[column],
                 eastern,
                 western,
                 wide_ref[item, column, at + 1 : at + 9, :],
                 wide_ref[item, column, at - 1 : at + 7, :],
-                vel_wide_ref[level, column, at : at + 8, :],
-                vel_wide_ref[LEVELS + level, column, at : at + 8, :],
-                spread,
+                0.5 * vel_ref[level, rows, lanes],
+                0.5 * vel_ref[LEVELS + level, rows, lanes],
+                spread_of(scale_ref, field),
             )
 
     def average(item, tile):
         field, level = divmod(item, LEVELS)
-        spread = jnp.broadcast_to(scale_ref[FIELDS + field : FIELDS + field + 1, :], (8, LANES))
-        at, row = tile * 8 + 1, tile * 8 + 8
+        rows, at = slice(tile * 8, tile * 8 + 8), tile * 8 + 8
         middle = [sectioned_ref[item, column, at : at + 8, :] for column in range(COLUMNS)]
         for column, (eastern, western) in enumerate(along_x(middle, last, begin)):
+            lanes = slice(column * LANES, column * LANES + LANES)
             change = tendency(
                 middle[column],
                 eastern,
                 western,
                 sectioned_ref[item, column, at + 1 : at + 9, :],
                 sectioned_ref[item, column, at - 1 : at + 7, :],
-                vel_wide_ref[level, column, row : row + 8, :],
-                vel_wide_ref[LEVELS + level, column, row : row + 8, :],
-                spread,
+                0.5 * vel_ref[level, rows, lanes],
+                0.5 * vel_ref[LEVELS + level, rows, lanes],
+                spread_of(scale_ref, field),
             )
-            explicit_ref[item, tile * 8 : tile * 8 + 8, column * LANES : column * LANES + LANES] = 0.5 * (
-                wide_ref[item, column, row : row + 8, :] + (middle[column] + change)
+            explicit_ref[item, rows, lanes] = 0.5 * (present_ref[item, rows, lanes] + (middle[column] + change))
+
+    for item in range(ITEMS):
+        for column, lanes in enumerate(columns()):
+            wide_ref[item, column, 8:24, :] = present_ref[item, :, lanes]
+    for turn in range(ITEMS + 1):
+        for tile in range(ROWS // 8):
+            if turn < ITEMS:
+                section(ORDER[turn], tile)
+            if turn > 0:
+                average(ORDER[turn - 1], tile)
+
+
+def strip_tiles(strip_ref, item, column, low):
+    lines = [strip_ref[item, column, at : at + 8, :] for at in range(5)]
+    return [jnp.where(low, lines[at], lines[at + 2]) for at in range(3)]
+
+
+def explicit_kernel(parts, place_ref, scale_ref, factor_ref, inner_ref, present_ref, south_ref, north_ref, vel_ref,
+                    vel_south_ref, vel_north_ref, face_ref, explicit_ref, send_ref, strip_ref, vel_strip_ref,
+                    vel_tile_ref, sectioned_ref):
+    last, begin = edge_lanes()
+    low = lax.broadcasted_iota(jnp.int32, (8, LANES), 0) < 4
+    for column, lanes in enumerate(columns()):
+        for item in range(2 * LEVELS):
+            row = slice(item % 2, item % 2 + 1)
+            vel_strip_ref[item, column, 1:2, :] = 0.5 * vel_south_ref[ITEMS + item // 2, row, lanes]
+            vel_strip_ref[item, column, 2:6, :] = 0.5 * vel_ref[item, 0:4, lanes]
+            vel_strip_ref[item, column, 6:10, :] = 0.5 * vel_ref[item, ROWS - 4 : ROWS, lanes]
+            vel_strip_ref[item, column, 10:11, :] = 0.5 * vel_north_ref[ITEMS + item // 2, row, lanes]
+            _, near, far = strip_tiles(vel_strip_ref, item, column, low)
+            vel_tile_ref[0, item, column] = near
+            vel_tile_ref[1, item, column] = far
+        for item in range(ITEMS):
+            strip_ref[item, column, 0:2, :] = south_ref[item, :, lanes]
+            strip_ref[item, column, 2:6, :] = present_ref[item, 0:4, lanes]
+            strip_ref[item, column, 6:10, :] = present_ref[item, ROWS - 4 : ROWS, lanes]
+            strip_ref[item, column, 10:12, :] = north_ref[item, :, lanes]
+
+    def section(item):
+        field, level = divmod(item, LEVELS)
+        tiles = [strip_tiles(strip_ref, item, column, low) for column in range(COLUMNS)]
+        middle = [tile[1] for tile in tiles]
+        for column, (eastern, western) in enumerate(along_x(middle, last, begin)):
+            sectioned_ref[item, column, 0:8, :] = middle[column] + tendency(
+                middle[column],
+                eastern,
+                western,
+                tiles[column][2],
+                tiles[column][0],
+                vel_tile_ref[0, level, column],
+                vel_tile_ref[0, LEVELS + level, column],
+                spread_of(scale_ref, field),
             )
 
-    order = [field * LEVELS + level for level in range(LEVELS) for field in range(FIELDS)]
+    def average(item):
+        field, level = divmod(item, LEVELS)
+        middle = [sectioned_ref[item, column, 1:9, :] for column in range(COLUMNS)]
+        for column, (eastern, western) in enumerate(along_x(middle, last, begin)):
+            lanes = slice(column * LANES, column * LANES + LANES)
+            change = tendency(
+                middle[column],
+                eastern,
+                western,
+                sectioned_ref[item, column, 2:10, :],
+                sectioned_ref[item, column, 0:8, :],
+                vel_tile_ref[1, level, column],
+                vel_tile_ref[1, LEVELS + level, column],
+                spread_of(scale_ref, field),
+            )
+            here = jnp.where(low, strip_ref[item, column, 2:10, :], strip_ref[item, column, 4:12, :])
+            value = 0.5 * (here + (middle[column] + change))
+            explicit_ref[item, 0:2, lanes] = value[0:2]
+            explicit_ref[item, ROWS - 2 : ROWS, lanes] = value[4:6]
+
+    for item in range(ITEMS):
+        explicit_ref[item, 2 : ROWS - 2, :] = inner_ref[item, 2 : ROWS - 2, :]
     for turn in range(ITEMS + 1):
-        for tile in range(3):
-            if turn < ITEMS:
-                section(order[turn], tile)
-            if turn > 0 and tile < ROWS // 8:
-                average(order[turn - 1], tile)
+        if turn < ITEMS:
+            section(ORDER[turn])
+        if turn > 0:
+            average(ORDER[turn - 1])
     for tile in range(ROWS // 8):
         rows = slice(tile * 8, tile * 8 + 8)
         target = turned_tile(place_ref, tile)
@@ -361,7 +432,7 @@
         pack_kernel,
         out_shape=(edge, edge),
         in_specs=[VMEM, VMEM],
-        out_specs=(VMEM, VMEM),
+        out_specs=(VMEM,) * 2,
         compiler_params=PARAMS,
         name="pack_part",
     )(present, vel)
@@ -378,16 +449,30 @@
     )(scale, faces)
 
 
+def interior_part(scale, present, vel):
+    return pl.pallas_call(
+        interior_kernel,
+        out_shape=struct(ITEMS, ROWS, WIDTH),
+        in_specs=[VMEM] * 3,
+        out_specs=VMEM,
+        scratch_shapes=[pltpu.VMEM((ITEMS, COLUMNS, 32, LANES), jnp.float32)] * 2,
+        compiler_params=PARAMS,
+        cost_estimate=pl.CostEstimate(flops=8 << 20, bytes_accessed=3 << 20, transcendentals=0),
+        name="interior_part",
+    )(scale, present, vel)
+
+
 def explicit_part(parts, *operands):
     return pl.pallas_call(
         functools.partial(explicit_kernel, parts),
         out_shape=(struct(ITEMS, ROWS, WIDTH), struct(MEMBERS * parts * 8, LANES)),
-        in_specs=[SMEM] + [VMEM] * 9,
+        in_specs=[SMEM] + [VMEM] * 10,
         out_specs=(VMEM, VMEM),
         scratch_shapes=[
-            pltpu.VMEM((ITEMS, COLUMNS, 32, LANES), jnp.float32),
-            pltpu.VMEM((2 * LEVELS, COLUMNS, 32, LANES), jnp.float32),
-            pltpu.VMEM((ITEMS, COLUMNS, 24, LANES), jnp.float32),
+            pltpu.VMEM((ITEMS, COLUMNS, 16, LANES), jnp.float32),
+            pltpu.VMEM((2 * LEVELS, COLUMNS, 16, LANES), jnp.float32),
+            pltpu.VMEM((2, 2 * LEVELS, COLUMNS, 8, LANES), jnp.float32),
+            pltpu.VMEM((ITEMS, COLUMNS, 16, LANES), jnp.float32),
         ],
         compiler_params=PARAMS,
         name="explicit_part",
@@ -450,6 +535,7 @@
     vel = velocity.reshape(2 * LEVELS, ROWS, WIDTH)
     faces = face_rate
     lowest, highest = pack_part(present, vel)
+    half_vel = vel
     south = vel_south = lax.ppermute(highest, "gy", up)
     north = vel_north = lax.ppermute(lowest, "gy", down)
     inner = factor_part(scale, faces)
@@ -471,8 +557,9 @@
             south = lax.ppermute(highest, "gy", up)
             north = lax.ppermute(lowest, "gy", down)
         parts = COLUMNS if factors else COLUMNS + 2
+        interior = interior_part(scale, present, half_vel)
         explicit, send = explicit_part(
-            parts, place, scale, inner, present, south, north, vel, vel_south, vel_north, faces
+            parts, place, scale, inner, interior, present, south, north, half_vel, vel_south, vel_north, faces
         )
         got = near(send.reshape(MEMBERS, parts, 8, LANES))
         *made, sources, ports = reduce_part(got, factors, scale)

time: 124 us -> 122 us (0.984)
  waiting for transfers between devices: 5.73 us -> 2.6 us
    pallas_call x0 -> x2, Pallas kernels: none -> 2.08 us  [interior_part(): pl.pallas_call(interior_kernel, out_shape=struct(ITEMS, ROWS, WIDTH), in_...]
    pallas_call x2, Pallas kernels: 3.31 us -> 1.77 us  [explicit_part(): pl.pallas_call(functools.partial(explicit_kernel, parts), out_shape=(stru...]
  transfers between devices with their start and end apart: 4 -> 4, of which waited for: 3 -> 2; matrix products, arithmetic and copies ran while one was open for 0% -> 0% of each run, Pallas kernels for 0% -> 2%
where the time goes in v6:
time: 122 us
  blocking collectives  106 us (87%)
  Pallas kernels  5.92 us (5%)
  local copies, waits for them, and re-layouts  3.76 us (3%)
  starting transfers between devices  3.5 us (3%)
  waiting for transfers between devices  2.6 us (2%)
    all_to_all x4, blocking collectives, near(): lax.all_to_all(chunks, 'gz', 0, 0, tiled=True, axis_index_groups=near_gro...  64.7 us
    all_to_all x2, blocking collectives, far(): lax.all_to_all(chunks, 'gz', 0, 0, tiled=True, axis_index_groups=far_groups)  41 us
    unnamed x14, local copies, waits for them, and re-layouts  3.69 us
  transfers between devices with their start and end apart: 4, of which 2 were waited for; matrix products, arithmetic and copies ran while one was open for 0% of the time, Pallas kernels for 2%

profile of v6, /device:TPU:24, one launch (start us, length us, event | category | flops | bytes accessed | tf_op | source)
XLA Modules:
  0.0 121.7 jit_solution(5011097508282141965)
XLA Ops:
  0.0 0.9 copy-done
  1.0 1.0 copy-done.2
  2.0 0.0 collective-permute-start
  2.1 1.7 %collective-permute-start.1 = (f32[20,2,512]{2,1,0:T(2,128)S(1)}, f32[20,2,512]{2,1,0:T(2,128)S(1)}, u32[]{:S(2)}, u32[]{:S(2)}) collective-permute-start(f32[20,2,512]{2,1,0:T(2,128)S(1)} %get-tuple-element.28), channel_id=1, source_target_pairs={{1,0},{2,1},{3,2},{4,3},{5,4},{6,5},{7,6},{0,7},{9,8},{10,9},{11,1... | collective-permute-start | bytes 245768 | tf_op jit(solution)/shard_map/ppermute | solution.py:540
  3.8 0.7 copy-done.5
  4.4 0.0 copy-done.6
  4.5 0.1 pad_maximum_fusion
  4.5 0.1 broadcast_in_dim.2.scale_ref.refs_0_
  4.6 0.1 factor_part.1.factor_ref
  4.7 0.8 copy-done.1
  5.6 0.2 copy-done.3
  5.7 1.0 interior_part.2.inner_ref
  6.8 0.0 collective-permute-done.south_ref.vel_south_ref
  6.8 1.7 %collective-permute-done.1.north_ref.vel_north_ref = f32[20,2,512]{2,1,0:T(2,128)S(1)} collective-permute-done((f32[20,2,512]{2,1,0:T(2,128)S(1)}, f32[20,2,512]{2,1,0:T(2,128)S(1)}, u32[]{:S(2)}, u32[]{:S(2)}) %collective-permute-start.1) | collective-permute-done | bytes 81952 | tf_op jit(solution)/shard_map/ppermute | solution.py:540
  8.5 0.9 explicit_part.2
  9.4 20.3 %all_to_all.30.got_ref = f32[16,6,8,128]{3,2,1,0:T(8,128)S(1)} all-to-all(f32[16,6,8,128]{3,2,1,0:T(8,128)S(1)} %bitcast.18), channel_id=1, replica_groups={{0,8,16,24,32,40,48,56,64,72,80,88,96,104,112,120},{128,136,144,152,160..., dimensions={0} | all-to-all | bytes 786432 | tf_op jit(solution)/shard_map/all_to_all | solution.py:549
  29.7 0.3 reduce_part.2
  30.0 26.5 %all_to_all.31.got_ref = f32[4,3,4,8,128]{4,3,2,1,0:T(8,128)S(1)} all-to-all(f32[4,3,4,8,128]{4,3,2,1,0:T(8,128)S(1)} %get-tuple-element.31), channel_id=1, replica_groups={{0,128,320,448},{8,136,328,456},{16,144,336,464},{24,152,344,472},{32,1..., dimensions={0} | all-to-all | bytes 393216 | tf_op jit(solution)/shard_map/all_to_all | solution.py:552
  56.5 0.1 return_part.2
  56.6 14.7 %all_to_all.32 = f32[16,4,8,128]{3,2,1,0:T(8,128)S(1)} all-to-all(f32[16,4,8,128]{3,2,1,0:T(8,128)S(1)} %get-tuple-element.36), channel_id=1, replica_groups={{0,8,16,24,32,40,48,56,64,72,80,88,96,104,112,120},{128,136,144,152,160..., dimensions={0} | all-to-all | bytes 524288 | tf_op jit(solution)/shard_map/all_to_all | solution.py:549
  71.3 0.3 finish_part.2
  71.6 0.0 collective-permute-start.2
  71.6 1.7 %collective-permute-start.3 = (f32[16,2,512]{2,1,0:T(2,128)S(1)}, f32[16,2,512]{2,1,0:T(2,128)S(1)}, u32[]{:S(2)}, u32[]{:S(2)}) collective-permute-start(f32[16,2,512]{2,1,0:T(2,128)S(1)} %get-tuple-element.39), channel_id=1, source_target_pairs={{1,0},{2,1},{3,2},{4,3},{5,4},{6,5},{7,6},{0,7},{9,8},{10,9},{11,1... | collective-permute-start | bytes 196616 | tf_op jit(solution)/shard_map/ppermute | solution.py:558
  73.3 1.0 interior_part.3.inner_ref
  74.4 0.9 collective-permute-done.2.south_ref
  75.3 0.9 explicit_part.3
  76.2 14.6 %all_to_all.33.got_ref = f32[16,4,8,128]{3,2,1,0:T(8,128)S(1)} all-to-all(f32[16,4,8,128]{3,2,1,0:T(8,128)S(1)} %bitcast.19), channel_id=1, replica_groups={{0,8,16,24,32,40,48,56,64,72,80,88,96,104,112,120},{128,136,144,152,160..., dimensions={0} | all-to-all | bytes 524288 | tf_op jit(solution)/shard_map/all_to_all | solution.py:549
  90.8 0.1 reduce_part.3
  90.9 14.5 %all_to_all.34.got_ref = f32[4,1,4,8,128]{4,3,2,1,0:T(8,128)S(1)} all-to-all(f32[4,1,4,8,128]{4,3,2,1,0:T(8,128)S(1)} %get-tuple-element.42), channel_id=1, replica_groups={{0,128,320,448},{8,136,328,456},{16,144,336,464},{24,152,344,472},{32,1..., dimensions={0} | all-to-all | bytes 131072 | tf_op jit(solution)/shard_map/all_to_all | solution.py:552
  105.4 0.1 return_part.3
  105.5 15.0 %all_to_all.35 = f32[16,4,8,128]{3,2,1,0:T(8,128)S(1)} all-to-all(f32[16,4,8,128]{3,2,1,0:T(8,128)S(1)} %return_part.3), channel_id=1, replica_groups={{0,8,16,24,32,40,48,56,64,72,80,88,96,104,112,120},{128,136,144,152,160..., dimensions={0} | all-to-all | bytes 524288 | tf_op jit(solution)/shard_map/all_to_all | solution.py:549
  120.5 1.1 finish_part.3
  (10 shorter events, 0.1 us)
Async XLA Ops:
  0.0 0.9 copy-start
  1.0 1.0 copy-start.2
  2.0 2.6 %copy-start.4 = (f32[4,16,512]{2,1,0:T(8,128)S(1)}, f32[4,16,512]{2,1,0:T(8,128)}, u32[]{:S(2)}) copy-start(f32[4,16,512]{2,1,0:T(8,128)} %face_ref.5) | copy-start | bytes 393220
  2.0 4.8 %collective-permute-start = (f32[20,2,512]{2,1,0:T(2,128)S(1)}, f32[20,2,512]{2,1,0:T(2,128)S(1)}, u32[]{:S(2)}, u32[]{:S(2)}) collective-permute-start(f32[20,2,512]{2,1,0:T(2,128)S(1)} %get-tuple-element.27), channel_id=1, source_target_pairs={{0,1},{1,2},{2,3},{3,4},{4,5},{5,6},{6,7},{7,0},{8,9},{9,10},{10,1... | collective-permute-start | bytes 245768 | tf_op jit(solution)/shard_map/ppermute | solution.py:539
  2.1 6.4 %collective-permute-start.1 = (f32[20,2,512]{2,1,0:T(2,128)S(1)}, f32[20,2,512]{2,1,0:T(2,128)S(1)}, u32[]{:S(2)}, u32[]{:S(2)}) collective-permute-start(f32[20,2,512]{2,1,0:T(2,128)S(1)} %get-tuple-element.28), channel_id=1, source_target_pairs={{1,0},{2,1},{3,2},{4,3},{5,4},{6,5},{7,6},{0,7},{9,8},{10,9},{11,1... | collective-permute-start | bytes 245768 | tf_op jit(solution)/shard_map/ppermute | solution.py:540
  3.8 0.7 copy-start.5
  3.8 0.7 copy-start.6
  4.6 1.0 copy-start.1
  4.6 1.1 copy-start.3
  71.6 3.7 %collective-permute-start.2 = (f32[16,2,512]{2,1,0:T(2,128)S(1)}, f32[16,2,512]{2,1,0:T(2,128)S(1)}, u32[]{:S(2)}, u32[]{:S(2)}) collective-permute-start(f32[16,2,512]{2,1,0:T(2,128)S(1)} %get-tuple-element.38), channel_id=1, source_target_pairs={{0,1},{1,2},{2,3},{3,4},{4,5},{5,6},{6,7},{7,0},{8,9},{9,10},{10,1... | collective-permute-start | bytes 196616 | tf_op jit(solution)/shard_map/ppermute | solution.py:557
  71.6 3.7 %collective-permute-start.3 = (f32[16,2,512]{2,1,0:T(2,128)S(1)}, f32[16,2,512]{2,1,0:T(2,128)S(1)}, u32[]{:S(2)}, u32[]{:S(2)}) collective-permute-start(f32[16,2,512]{2,1,0:T(2,128)S(1)} %get-tuple-element.39), channel_id=1, source_target_pairs={{1,0},{2,1},{3,2},{4,3},{5,4},{6,5},{7,6},{0,7},{9,8},{10,9},{11,1... | collective-permute-start | bytes 196616 | tf_op jit(solution)/shard_map/ppermute | solution.py:558

commit v7 on v6

--- a/solution.py
+++ b/solution.py
@@ -326,8 +326,10 @@
         outer = jnp.where(low, under[0], own[0]) + couple[0] * value
         through = through * swap(through) * center
         for group in range(GROUPS):
-            send_ref[group, 1] = outer
-            send_ref[group, 2] = through
+            send_ref[group, COLUMNS : 2 * COLUMNS] = outer
+            for column in range(0, COLUMNS, 2):
+                pair = jnp.where(low[0], through[column], through[column + 1])
+                send_ref[group, 2 * COLUMNS + column // 2] = pair
     else:
         weight_ref, gain_ref, edge_ref, source_ref, send_ref = refs
     sources = pair_sources(got_ref, low)
@@ -338,7 +340,7 @@
         value = weight_ref[step] * kept[step] + gain_ref[step] * value
     outer = outer_source(got_ref, low) + edge_ref[...] * value
     for group in range(GROUPS):
-        send_ref[group, 0] = outer
+        send_ref[group, 0:COLUMNS] = outer
 
 
 def across(parts, low):
@@ -351,8 +353,13 @@
     low = lower_half()
     if first:
         top_ref, back_ref = refs
-        ends, middle = across([got_ref[group, 1] for group in range(GROUPS)], low)
-        through = [got_ref[group, 2] for group in range(GROUPS)]
+        ends, middle = across([got_ref[group, COLUMNS : 2 * COLUMNS] for group in range(GROUPS)], low)
+        through = []
+        for group in range(GROUPS):
+            pairs = got_ref[group, 2 * COLUMNS : 2 * COLUMNS + COLUMNS // 2]
+            turned = swap(pairs)
+            tiles = [jnp.where(low[0], one, other) for pair in zip(pairs, turned) for one, other in (pair, pair[::-1])]
+            through.append(jnp.stack(tiles))
         hold = ends + jnp.where(low, through[0], 0.0)
         inward = jnp.where(low, through[1], through[3])
         weight = 1.0 / (hold + inward)
@@ -366,7 +373,7 @@
     else:
         top_ref, back_ref = refs
         weight, gain, mine, cross = (top_ref[item] for item in range(4))
-    ends, middle = across([got_ref[group, 0] for group in range(GROUPS)], low)
+    ends, middle = across([got_ref[group, 0:COLUMNS] for group in range(GROUPS)], low)
     inner = middle + gain * ends
     inner = mine * inner + cross * swap(inner)
     ends = weight * ends + gain * inner
@@ -481,7 +488,7 @@
 
 def reduce_part(got, factors=None, scale=None):
     shapes = (struct(PAIRS, *TILE), struct(PAIRS - 1, *TILE), struct(*TILE))
-    outs = (struct(PAIRS, *TILE), struct(GROUPS, 1 if factors else 3, *TILE))
+    outs = (struct(PAIRS, *TILE), struct(GROUPS, COLUMNS if factors else 2 * COLUMNS + COLUMNS // 2, 8, LANES))
     if not factors:
         outs = shapes + outs
     return pl.pallas_call(

time: 122 us -> 121 us (level)
  blocking collectives: 106 us -> 104 us
where the time goes in v7:
time: 121 us; the launch traced here: 120 us
  blocking collectives  104 us (86%)
  Pallas kernels  5.92 us (5%)
  local copies, waits for them, and re-layouts  3.76 us (3%)
  starting transfers between devices  3.5 us (3%)
  waiting for transfers between devices  2.6 us (2%)
    all_to_all x4, blocking collectives, near(): lax.all_to_all(chunks, 'gz', 0, 0, tiled=True, axis_index_groups=near_gro...  64 us
    all_to_all x2, blocking collectives, far(): lax.all_to_all(chunks, 'gz', 0, 0, tiled=True, axis_index_groups=far_groups)  40.2 us
    unnamed x14, local copies, waits for them, and re-layouts  3.69 us
  transfers between devices with their start and end apart: 4, of which 2 were waited for; matrix products, arithmetic and copies ran while one was open for 0% of the time, Pallas kernels for 2%

profile of v7, /device:TPU:24, one launch (start us, length us, event | category | flops | bytes accessed | tf_op | source)
XLA Modules:
  0.0 120.2 jit_solution(748385935195051451)
XLA Ops:
  0.0 0.9 copy-done
  1.0 1.0 copy-done.2
  2.0 0.0 collective-permute-start
  2.1 1.7 %collective-permute-start.1 = (f32[20,2,512]{2,1,0:T(2,128)S(1)}, f32[20,2,512]{2,1,0:T(2,128)S(1)}, u32[]{:S(2)}, u32[]{:S(2)}) collective-permute-start(f32[20,2,512]{2,1,0:T(2,128)S(1)} %get-tuple-element.28), channel_id=1, source_target_pairs={{1,0},{2,1},{3,2},{4,3},{5,4},{6,5},{7,6},{0,7},{9,8},{10,9},{11,1... | collective-permute-start | bytes 245768 | tf_op jit(solution)/shard_map/ppermute | solution.py:547
  3.8 0.7 copy-done.5
  4.4 0.0 copy-done.6
  4.5 0.1 pad_maximum_fusion
  4.5 0.1 broadcast_in_dim.2.scale_ref.refs_0_
  4.6 0.1 factor_part.1.factor_ref
  4.7 0.8 copy-done.1
  5.6 0.2 copy-done.3
  5.7 1.0 interior_part.2.inner_ref
  6.8 0.0 collective-permute-done.south_ref.vel_south_ref
  6.8 1.7 %collective-permute-done.1.north_ref.vel_north_ref = f32[20,2,512]{2,1,0:T(2,128)S(1)} collective-permute-done((f32[20,2,512]{2,1,0:T(2,128)S(1)}, f32[20,2,512]{2,1,0:T(2,128)S(1)}, u32[]{:S(2)}, u32[]{:S(2)}) %collective-permute-start.1) | collective-permute-done | bytes 81952 | tf_op jit(solution)/shard_map/ppermute | solution.py:547
  8.5 0.9 explicit_part.2
  9.4 20.3 %all_to_all.30.got_ref = f32[16,6,8,128]{3,2,1,0:T(8,128)S(1)} all-to-all(f32[16,6,8,128]{3,2,1,0:T(8,128)S(1)} %bitcast.18), channel_id=1, replica_groups={{0,8,16,24,32,40,48,56,64,72,80,88,96,104,112,120},{128,136,144,152,160..., dimensions={0} | all-to-all | bytes 786432 | tf_op jit(solution)/shard_map/all_to_all | solution.py:556
  29.7 0.3 reduce_part.2
  30.0 25.5 %all_to_all.31.got_ref = f32[4,10,8,128]{3,2,1,0:T(8,128)S(1)} all-to-all(f32[4,10,8,128]{3,2,1,0:T(8,128)S(1)} %get-tuple-element.31), channel_id=1, replica_groups={{0,128,320,448},{8,136,328,456},{16,144,336,464},{24,152,344,472},{32,1..., dimensions={0} | all-to-all | bytes 327680 | tf_op jit(solution)/shard_map/all_to_all | solution.py:559
  55.5 0.1 return_part.2
  55.5 14.7 %all_to_all.32 = f32[16,4,8,128]{3,2,1,0:T(8,128)S(1)} all-to-all(f32[16,4,8,128]{3,2,1,0:T(8,128)S(1)} %get-tuple-element.36), channel_id=1, replica_groups={{0,8,16,24,32,40,48,56,64,72,80,88,96,104,112,120},{128,136,144,152,160..., dimensions={0} | all-to-all | bytes 524288 | tf_op jit(solution)/shard_map/all_to_all | solution.py:556
  70.2 0.3 finish_part.2
  70.5 0.0 collective-permute-start.2
  70.6 1.7 %collective-permute-start.3 = (f32[16,2,512]{2,1,0:T(2,128)S(1)}, f32[16,2,512]{2,1,0:T(2,128)S(1)}, u32[]{:S(2)}, u32[]{:S(2)}) collective-permute-start(f32[16,2,512]{2,1,0:T(2,128)S(1)} %get-tuple-element.39), channel_id=1, source_target_pairs={{1,0},{2,1},{3,2},{4,3},{5,4},{6,5},{7,6},{0,7},{9,8},{10,9},{11,1... | collective-permute-start | bytes 196616 | tf_op jit(solution)/shard_map/ppermute | solution.py:565
  72.3 1.0 interior_part.3.inner_ref
  73.3 0.9 collective-permute-done.2.south_ref
  74.2 0.9 explicit_part.3
  75.2 14.7 %all_to_all.33.got_ref = f32[16,4,8,128]{3,2,1,0:T(8,128)S(1)} all-to-all(f32[16,4,8,128]{3,2,1,0:T(8,128)S(1)} %bitcast.19), channel_id=1, replica_groups={{0,8,16,24,32,40,48,56,64,72,80,88,96,104,112,120},{128,136,144,152,160..., dimensions={0} | all-to-all | bytes 524288 | tf_op jit(solution)/shard_map/all_to_all | solution.py:556
  89.9 0.1 reduce_part.3
  90.0 14.8 %all_to_all.34.got_ref = f32[4,4,8,128]{3,2,1,0:T(8,128)S(1)} all-to-all(f32[4,4,8,128]{3,2,1,0:T(8,128)S(1)} %get-tuple-element.42), channel_id=1, replica_groups={{0,128,320,448},{8,136,328,456},{16,144,336,464},{24,152,344,472},{32,1..., dimensions={0} | all-to-all | bytes 131072 | tf_op jit(solution)/shard_map/all_to_all | solution.py:559
  104.7 0.1 return_part.3
  104.8 14.3 %all_to_all.35 = f32[16,4,8,128]{3,2,1,0:T(8,128)S(1)} all-to-all(f32[16,4,8,128]{3,2,1,0:T(8,128)S(1)} %return_part.3), channel_id=1, replica_groups={{0,8,16,24,32,40,48,56,64,72,80,88,96,104,112,120},{128,136,144,152,160..., dimensions={0} | all-to-all | bytes 524288 | tf_op jit(solution)/shard_map/all_to_all | solution.py:556
  119.1 1.1 finish_part.3
  (10 shorter events, 0.1 us)
Async XLA Ops:
  0.0 0.9 copy-start
  1.0 1.0 copy-start.2
  2.0 2.6 %copy-start.4 = (f32[4,16,512]{2,1,0:T(8,128)S(1)}, f32[4,16,512]{2,1,0:T(8,128)}, u32[]{:S(2)}) copy-start(f32[4,16,512]{2,1,0:T(8,128)} %face_ref.5) | copy-start | bytes 393220
  2.0 4.8 %collective-permute-start = (f32[20,2,512]{2,1,0:T(2,128)S(1)}, f32[20,2,512]{2,1,0:T(2,128)S(1)}, u32[]{:S(2)}, u32[]{:S(2)}) collective-permute-start(f32[20,2,512]{2,1,0:T(2,128)S(1)} %get-tuple-element.27), channel_id=1, source_target_pairs={{0,1},{1,2},{2,3},{3,4},{4,5},{5,6},{6,7},{7,0},{8,9},{9,10},{10,1... | collective-permute-start | bytes 245768 | tf_op jit(solution)/shard_map/ppermute | solution.py:546
  2.1 6.4 %collective-permute-start.1 = (f32[20,2,512]{2,1,0:T(2,128)S(1)}, f32[20,2,512]{2,1,0:T(2,128)S(1)}, u32[]{:S(2)}, u32[]{:S(2)}) collective-permute-start(f32[20,2,512]{2,1,0:T(2,128)S(1)} %get-tuple-element.28), channel_id=1, source_target_pairs={{1,0},{2,1},{3,2},{4,3},{5,4},{6,5},{7,6},{0,7},{9,8},{10,9},{11,1... | collective-permute-start | bytes 245768 | tf_op jit(solution)/shard_map/ppermute | solution.py:547
  3.8 0.7 copy-start.5
  3.8 0.7 copy-start.6
  4.6 1.0 copy-start.1
  4.6 1.1 copy-start.3
  70.5 3.7 %collective-permute-start.2 = (f32[16,2,512]{2,1,0:T(2,128)S(1)}, f32[16,2,512]{2,1,0:T(2,128)S(1)}, u32[]{:S(2)}, u32[]{:S(2)}) collective-permute-start(f32[16,2,512]{2,1,0:T(2,128)S(1)} %get-tuple-element.38), channel_id=1, source_target_pairs={{0,1},{1,2},{2,3},{3,4},{4,5},{5,6},{6,7},{7,0},{8,9},{9,10},{10,1... | collective-permute-start | bytes 196616 | tf_op jit(solution)/shard_map/ppermute | solution.py:564
  70.6 3.7 %collective-permute-start.3 = (f32[16,2,512]{2,1,0:T(2,128)S(1)}, f32[16,2,512]{2,1,0:T(2,128)S(1)}, u32[]{:S(2)}, u32[]{:S(2)}) collective-permute-start(f32[16,2,512]{2,1,0:T(2,128)S(1)} %get-tuple-element.39), channel_id=1, source_target_pairs={{1,0},{2,1},{3,2},{4,3},{5,4},{6,5},{7,6},{0,7},{9,8},{10,9},{11,1... | collective-permute-start | bytes 196616 | tf_op jit(solution)/shard_map/ppermute | solution.py:565

commit v8 on v6

--- a/solution.py
+++ b/solution.py
@@ -326,10 +326,11 @@
         outer = jnp.where(low, under[0], own[0]) + couple[0] * value
         through = through * swap(through) * center
         for group in range(GROUPS):
-            send_ref[group, 1] = outer
-            send_ref[group, 2] = through
+            send_ref[group, COLUMNS : 2 * COLUMNS] = outer
+            for item, pair in enumerate(pack_pairs(through, low)):
+                send_ref[group, 2 * COLUMNS + item] = pair
     else:
-        weight_ref, gain_ref, edge_ref, source_ref, send_ref = refs
+        weight_ref, gain_ref, edge_ref, top_ref, source_ref, send_ref, port_ref = refs
     sources = pair_sources(got_ref, low)
     for step in range(PAIRS):
         source_ref[step] = sources[step]
@@ -337,8 +338,69 @@
     for step in reversed(range(PAIRS - 1)):
         value = weight_ref[step] * kept[step] + gain_ref[step] * value
     outer = outer_source(got_ref, low) + edge_ref[...] * value
+    if first:
+        for group in range(GROUPS):
+            send_ref[group, 0:COLUMNS] = outer
+    else:
+        port_ref[...] = outer
+        for group in range(GROUPS):
+            part = outer * top_ref[group]
+            for item, pair in enumerate(pack_pairs(part + swap(part), low)):
+                send_ref[group, item] = pair
+
+
+def pack_pairs(value, low):
+    return [jnp.where(low[0], value[column], value[column + 1]) for column in range(0, COLUMNS, 2)]
+
+
+def unpack_pairs(pairs, low):
+    turned = swap(pairs)
+    tiles = [jnp.where(low[0], one, other) for pair in zip(pairs, turned) for one, other in (pair, pair[::-1])]
+    return jnp.stack(tiles)
+
+
+def port_weights(parts, through, place, low):
+    masses = []
     for group in range(GROUPS):
-        send_ref[group, 0] = outer
+        mass = jnp.where(low, swap(parts[group]), parts[group])
+        if group + 1 < GROUPS:
+            mass = mass + jnp.where(low, parts[group + 1], swap(parts[group + 1]))
+        masses.append(mass)
+    under, gain = [masses[0] + through[0]], []
+    for group in range(GROUPS - 1):
+        gain.append(through[group + 1] / (under[group] + through[group + 1]))
+        under.append(masses[group + 1] + under[group] * gain[group])
+    over, rise = [masses[GROUPS - 1]], []
+    for group in reversed(range(1, GROUPS)):
+        rise.insert(0, through[group] / (over[0] + through[group]))
+        over.insert(0, masses[group - 1] + over[0] * rise[0])
+    rise.insert(0, None)
+    one, zero = jnp.ones(TILE, jnp.float32), jnp.zeros(TILE, jnp.float32)
+    weights = [zero] * GROUPS
+    own = cross = zero
+    for mine in range(GROUPS):
+        here = place == mine
+        for group in range(GROUPS):
+            product = one
+            for between in range(mine, group - 1):
+                product = product * gain[between]
+            for between in range(group + 1, mine):
+                product = product * rise[between]
+            if group > mine:
+                tile = jnp.where(low, product * gain[mine - 1] if mine else zero, product)
+            elif group < mine:
+                tile = jnp.where(low, product, product * rise[mine])
+            else:
+                continue
+            weights[group] = jnp.where(here, tile, weights[group])
+        if mine:
+            low_hold, high_hold, link = under[mine - 1], over[mine], through[mine]
+            inverse = 1.0 / (low_hold * high_hold + link * (low_hold + high_hold))
+            own = jnp.where(here, (jnp.where(low, high_hold, low_hold) + link) * inverse, own)
+            cross = jnp.where(here, link * inverse, cross)
+        else:
+            own = jnp.where(here, jnp.where(low, zero, 1.0 / (over[0] + through[0])), own)
+    return *weights, own, cross
 
 
 def across(parts, low):
@@ -349,10 +411,16 @@
 
 def return_kernel(first, place_ref, got_ref, source_ref, weight_ref, gain_ref, edge_ref, *refs):
     low = lower_half()
+    place = place_ref[0]
     if first:
         top_ref, back_ref = refs
-        ends, middle = across([got_ref[group, 1] for group in range(GROUPS)], low)
-        through = [got_ref[group, 2] for group in range(GROUPS)]
+        parts = [got_ref[group, COLUMNS : 2 * COLUMNS] for group in range(GROUPS)]
+        through = [
+            unpack_pairs(got_ref[group, 2 * COLUMNS : 2 * COLUMNS + COLUMNS // 2], low) for group in range(GROUPS)
+        ]
+        for item, value in enumerate(port_weights(parts, through, place, low)):
+            top_ref[item] = value
+        ends, middle = across(parts, low)
         hold = ends + jnp.where(low, through[0], 0.0)
         inward = jnp.where(low, through[1], through[3])
         weight = 1.0 / (hold + inward)
@@ -361,26 +429,28 @@
         other = swap(hold)
         inverse = 1.0 / (hold * other + through[2] * (hold + other))
         mine, cross = (other + through[2]) * inverse, through[2] * inverse
-        for item, value in enumerate((weight, gain, mine, cross)):
-            top_ref[item] = value
+        ends, middle = across([got_ref[group, 0:COLUMNS] for group in range(GROUPS)], low)
+        inner = middle + gain * ends
+        inner = mine * inner + cross * swap(inner)
+        ends = weight * ends + gain * inner
+        turned = swap(ends)
+        value = jnp.where(
+            place == 0,
+            jnp.where(low, 0.0, turned),
+            jnp.where(
+                place == 1,
+                jnp.where(low, ends, swap(inner)),
+                jnp.where(place == 2, inner, jnp.where(low, swap(inner), ends)),
+            ),
+        )
     else:
-        top_ref, back_ref = refs
-        weight, gain, mine, cross = (top_ref[item] for item in range(4))
-    ends, middle = across([got_ref[group, 0] for group in range(GROUPS)], low)
-    inner = middle + gain * ends
-    inner = mine * inner + cross * swap(inner)
-    ends = weight * ends + gain * inner
-    turned = swap(ends)
-    place = place_ref[0]
-    value = jnp.where(
-        place == 0,
-        jnp.where(low, 0.0, turned),
-        jnp.where(
-            place == 1,
-            jnp.where(low, ends, swap(inner)),
-            jnp.where(place == 2, inner, jnp.where(low, swap(inner), ends)),
-        ),
-    )
+        port_ref, top_ref, back_ref = refs
+        ports = port_ref[...]
+        for group in range(GROUPS):
+            below = jnp.where(place > group, 1.0, 0.0)
+            above = jnp.where(place < group, 1.0, 0.0)
+            ports = ports + jnp.where(low, below, above) * unpack_pairs(got_ref[group], low)
+        value = top_ref[GROUPS] * ports + top_ref[GROUPS + 1] * swap(ports)
     sources = [source_ref[step] for step in range(PAIRS)]
     sources[0] = sources[0] + edge_ref[...] * value
     kept, center = eliminate(sources, gain_ref, weight_ref[PAIRS - 1])
@@ -479,28 +549,33 @@
     )(*operands)
 
 
-def reduce_part(got, factors=None, scale=None):
-    shapes = (struct(PAIRS, *TILE), struct(PAIRS - 1, *TILE), struct(*TILE))
-    outs = (struct(PAIRS, *TILE), struct(GROUPS, 1 if factors else 3, *TILE))
-    if not factors:
-        outs = shapes + outs
+def reduce_part(got, factors=None, top=None, scale=None):
+    first = not factors
+    tiles = 2 * COLUMNS + COLUMNS // 2 if first else COLUMNS // 2
+    outs = (struct(PAIRS, *TILE), struct(GROUPS, tiles, 8, LANES))
+    if first:
+        outs = (struct(PAIRS, *TILE), struct(PAIRS - 1, *TILE), struct(*TILE)) + outs
+    else:
+        outs += (struct(*TILE),)
+    operands = (got, scale) if first else (got, *factors, top)
     return pl.pallas_call(
-        functools.partial(reduce_kernel, not factors),
+        functools.partial(reduce_kernel, first),
         out_shape=outs,
-        in_specs=[VMEM] * (4 if factors else 2),
+        in_specs=[VMEM] * len(operands),
         out_specs=(VMEM,) * len(outs),
         compiler_params=PARAMS,
         name="reduce_part",
-    )(got, *(factors or (scale,)))
-
-
-def return_part(place, got, sources, factors, top=None):
+    )(*operands)
+
+
+def return_part(place, got, sources, factors, *more):
+    first = not more
     outs = (struct(MEMBERS, *TILE),)
-    if top is None:
-        outs = (struct(4, *TILE),) + outs
-    operands = (got, sources) + tuple(factors) + (() if top is None else (top,))
+    if first:
+        outs = (struct(GROUPS + 2, *TILE),) + outs
+    operands = (got, sources, *factors, *more)
     return pl.pallas_call(
-        functools.partial(return_kernel, top is None),
+        functools.partial(return_kernel, first),
         out_shape=outs,
         in_specs=[SMEM] + [VMEM] * len(operands),
         out_specs=(VMEM,) * len(outs),
@@ -562,10 +637,12 @@
             parts, place, scale, inner, interior, present, south, north, half_vel, vel_south, vel_north, faces
         )
         got = near(send.reshape(MEMBERS, parts, 8, LANES))
-        *made, sources, ports = reduce_part(got, factors, scale)
-        factors = factors or tuple(made)
-        *made, back = return_part(place, far(ports), sources, factors, top)
-        top = made[0] if made else top
+        if step == 0:
+            *factors, sources, send = reduce_part(got, scale=scale)
+            top, back = return_part(place, far(send), sources, factors)
+        else:
+            sources, send, ports = reduce_part(got, factors, top)
+            (back,) = return_part(place, far(send), sources, factors, ports, top)
         present, *edges = finish_part(
             step + 1 < STEPS, place, inner, explicit, near(back).reshape(MEMBERS * COLUMNS * 8, LANES)
         )

time: 122 us -> 120 us (0.984)
  blocking collectives: 106 us -> 104 us
    all_to_all x2, blocking collectives: 41 us -> 39.7 us  [far(): lax.all_to_all(chunks, 'gz', 0, 0, tiled=True, axis_index_groups=far_groups)]
where the time goes in v8:
time: 120 us
  blocking collectives  104 us (87%)
  Pallas kernels  5.98 us (5%)
  local copies, waits for them, and re-layouts  3.76 us (3%)
  starting transfers between devices  3.5 us (3%)
  waiting for transfers between devices  2.6 us (2%)
    all_to_all x4, blocking collectives, near(): lax.all_to_all(chunks, 'gz', 0, 0, tiled=True, axis_index_groups=near_gro...  63.9 us
    all_to_all x2, blocking collectives, far(): lax.all_to_all(chunks, 'gz', 0, 0, tiled=True, axis_index_groups=far_groups)  39.7 us
    unnamed x14, local copies, waits for them, and re-layouts  3.69 us
  transfers between devices with their start and end apart: 4, of which 2 were waited for; matrix products, arithmetic and copies ran while one was open for 0% of the time, Pallas kernels for 2%

profile of v8, /device:TPU:24, one launch (start us, length us, event | category | flops | bytes accessed | tf_op | source)
XLA Modules:
  0.0 119.5 jit_solution(16684966375901348783)
XLA Ops:
  0.0 0.9 copy-done
  1.0 1.0 copy-done.2
  2.0 0.0 collective-permute-start
  2.1 1.7 %collective-permute-start.1 = (f32[20,2,512]{2,1,0:T(2,128)S(1)}, f32[20,2,512]{2,1,0:T(2,128)S(1)}, u32[]{:S(2)}, u32[]{:S(2)}) collective-permute-start(f32[20,2,512]{2,1,0:T(2,128)S(1)} %get-tuple-element.29), channel_id=1, source_target_pairs={{1,0},{2,1},{3,2},{4,3},{5,4},{6,5},{7,6},{0,7},{9,8},{10,9},{11,1... | collective-permute-start | bytes 245768 | tf_op jit(solution)/shard_map/ppermute | solution.py:615
  3.8 0.7 copy-done.5
  4.4 0.0 copy-done.6
  4.5 0.1 pad_maximum_fusion
  4.5 0.1 broadcast_in_dim.2.scale_ref.refs_0_
  4.6 0.1 factor_part.1.factor_ref
  4.7 0.8 copy-done.1
  5.6 0.2 copy-done.3
  5.7 1.0 interior_part.2.inner_ref
  6.8 0.0 collective-permute-done.south_ref.vel_south_ref
  6.8 1.7 %collective-permute-done.1.north_ref.vel_north_ref = f32[20,2,512]{2,1,0:T(2,128)S(1)} collective-permute-done((f32[20,2,512]{2,1,0:T(2,128)S(1)}, f32[20,2,512]{2,1,0:T(2,128)S(1)}, u32[]{:S(2)}, u32[]{:S(2)}) %collective-permute-start.1) | collective-permute-done | bytes 81952 | tf_op jit(solution)/shard_map/ppermute | solution.py:615
  8.5 0.9 explicit_part.2
  9.4 20.3 %all_to_all.30.got_ref = f32[16,6,8,128]{3,2,1,0:T(8,128)S(1)} all-to-all(f32[16,6,8,128]{3,2,1,0:T(8,128)S(1)} %bitcast.18), channel_id=1, replica_groups={{0,8,16,24,32,40,48,56,64,72,80,88,96,104,112,120},{128,136,144,152,160..., dimensions={0} | all-to-all | bytes 786432 | tf_op jit(solution)/shard_map/all_to_all | solution.py:624
  29.7 0.3 reduce_part.2
  30.0 25.5 %all_to_all.31.got_ref = f32[4,10,8,128]{3,2,1,0:T(8,128)S(1)} all-to-all(f32[4,10,8,128]{3,2,1,0:T(8,128)S(1)} %get-tuple-element.32), channel_id=1, replica_groups={{0,128,320,448},{8,136,328,456},{16,144,336,464},{24,152,344,472},{32,1..., dimensions={0} | all-to-all | bytes 327680 | tf_op jit(solution)/shard_map/all_to_all | solution.py:627
  55.5 0.1 return_part.2
  55.6 14.7 %all_to_all.32 = f32[16,4,8,128]{3,2,1,0:T(8,128)S(1)} all-to-all(f32[16,4,8,128]{3,2,1,0:T(8,128)S(1)} %get-tuple-element.37), channel_id=1, replica_groups={{0,8,16,24,32,40,48,56,64,72,80,88,96,104,112,120},{128,136,144,152,160..., dimensions={0} | all-to-all | bytes 524288 | tf_op jit(solution)/shard_map/all_to_all | solution.py:624
  70.3 0.3 finish_part.2
  70.6 0.0 collective-permute-start.2
  70.6 1.7 %collective-permute-start.3 = (f32[16,2,512]{2,1,0:T(2,128)S(1)}, f32[16,2,512]{2,1,0:T(2,128)S(1)}, u32[]{:S(2)}, u32[]{:S(2)}) collective-permute-start(f32[16,2,512]{2,1,0:T(2,128)S(1)} %get-tuple-element.40), channel_id=1, source_target_pairs={{1,0},{2,1},{3,2},{4,3},{5,4},{6,5},{7,6},{0,7},{9,8},{10,9},{11,1... | collective-permute-start | bytes 196616 | tf_op jit(solution)/shard_map/ppermute | solution.py:633
  72.3 1.0 interior_part.3.inner_ref
  73.4 0.9 collective-permute-done.2.south_ref
  74.3 0.9 explicit_part.3
  75.2 14.7 %all_to_all.33.got_ref = f32[16,4,8,128]{3,2,1,0:T(8,128)S(1)} all-to-all(f32[16,4,8,128]{3,2,1,0:T(8,128)S(1)} %bitcast.19), channel_id=1, replica_groups={{0,8,16,24,32,40,48,56,64,72,80,88,96,104,112,120},{128,136,144,152,160..., dimensions={0} | all-to-all | bytes 524288 | tf_op jit(solution)/shard_map/all_to_all | solution.py:624
  90.0 0.1 reduce_part.3
  90.0 14.2 %all_to_all.34.got_ref = f32[4,2,8,128]{3,2,1,0:T(8,128)S(1)} all-to-all(f32[4,2,8,128]{3,2,1,0:T(8,128)S(1)} %get-tuple-element.44), channel_id=1, replica_groups={{0,128,320,448},{8,136,328,456},{16,144,336,464},{24,152,344,472},{32,1..., dimensions={0} | all-to-all | bytes 65536 | tf_op jit(solution)/shard_map/all_to_all | solution.py:627
  104.2 0.1 return_part.3
  104.3 14.1 %all_to_all.35 = f32[16,4,8,128]{3,2,1,0:T(8,128)S(1)} all-to-all(f32[16,4,8,128]{3,2,1,0:T(8,128)S(1)} %return_part.3), channel_id=1, replica_groups={{0,8,16,24,32,40,48,56,64,72,80,88,96,104,112,120},{128,136,144,152,160..., dimensions={0} | all-to-all | bytes 524288 | tf_op jit(solution)/shard_map/all_to_all | solution.py:624
  118.4 1.1 finish_part.3
  (10 shorter events, 0.1 us)
Async XLA Ops:
  0.0 0.9 copy-start
  1.0 1.0 copy-start.2
  2.0 2.6 %copy-start.4 = (f32[4,16,512]{2,1,0:T(8,128)S(1)}, f32[4,16,512]{2,1,0:T(8,128)}, u32[]{:S(2)}) copy-start(f32[4,16,512]{2,1,0:T(8,128)} %face_ref.5) | copy-start | bytes 393220
  2.0 4.8 %collective-permute-start = (f32[20,2,512]{2,1,0:T(2,128)S(1)}, f32[20,2,512]{2,1,0:T(2,128)S(1)}, u32[]{:S(2)}, u32[]{:S(2)}) collective-permute-start(f32[20,2,512]{2,1,0:T(2,128)S(1)} %get-tuple-element.28), channel_id=1, source_target_pairs={{0,1},{1,2},{2,3},{3,4},{4,5},{5,6},{6,7},{7,0},{8,9},{9,10},{10,1... | collective-permute-start | bytes 245768 | tf_op jit(solution)/shard_map/ppermute | solution.py:614
  2.1 6.4 %collective-permute-start.1 = (f32[20,2,512]{2,1,0:T(2,128)S(1)}, f32[20,2,512]{2,1,0:T(2,128)S(1)}, u32[]{:S(2)}, u32[]{:S(2)}) collective-permute-start(f32[20,2,512]{2,1,0:T(2,128)S(1)} %get-tuple-element.29), channel_id=1, source_target_pairs={{1,0},{2,1},{3,2},{4,3},{5,4},{6,5},{7,6},{0,7},{9,8},{10,9},{11,1... | collective-permute-start | bytes 245768 | tf_op jit(solution)/shard_map/ppermute | solution.py:615
  3.8 0.7 copy-start.5
  3.8 0.7 copy-start.6
  4.6 1.0 copy-start.1
  4.6 1.1 copy-start.3
  70.6 3.7 %collective-permute-start.2 = (f32[16,2,512]{2,1,0:T(2,128)S(1)}, f32[16,2,512]{2,1,0:T(2,128)S(1)}, u32[]{:S(2)}, u32[]{:S(2)}) collective-permute-start(f32[16,2,512]{2,1,0:T(2,128)S(1)} %get-tuple-element.39), channel_id=1, source_target_pairs={{0,1},{1,2},{2,3},{3,4},{4,5},{5,6},{6,7},{7,0},{8,9},{9,10},{10,1... | collective-permute-start | bytes 196616 | tf_op jit(solution)/shard_map/ppermute | solution.py:632
  70.6 3.7 %collective-permute-start.3 = (f32[16,2,512]{2,1,0:T(2,128)S(1)}, f32[16,2,512]{2,1,0:T(2,128)S(1)}, u32[]{:S(2)}, u32[]{:S(2)}) collective-permute-start(f32[16,2,512]{2,1,0:T(2,128)S(1)} %get-tuple-element.40), channel_id=1, source_target_pairs={{1,0},{2,1},{3,2},{4,3},{5,4},{6,5},{7,6},{0,7},{9,8},{10,9},{11,1... | collective-permute-start | bytes 196616 | tf_op jit(solution)/shard_map/ppermute | solution.py:633

commit v9 on v8

--- a/solution.py
+++ b/solution.py
@@ -465,26 +465,41 @@
         outer = solved[step]
 
 
-def finish_kernel(edges, place_ref, factor_ref, explicit_ref, back_ref, present_ref, *edge_refs):
+def finish_field(field, place_ref, factor_ref, explicit_ref, back_ref, present_ref, edge_refs=None):
     for tile in range(ROWS // 8):
         rows = slice(tile * 8, tile * 8 + 8)
         target = turned_tile(place_ref, tile)
-        for field in range(FIELDS):
-            lines = zip(columns(), places(target, COLUMNS, field), places(target, COLUMNS, FIELDS + field), strict=True)
-            for lanes, below, top in lines:
-                factors = [factor_ref[item, field, rows, lanes] for item in range(FACTORS)]
-                source = [explicit_ref[field * LEVELS + level, rows, lanes] for level in range(LEVELS - 1)]
-                top = back_ref[top, :]
-                source[0] = source[0] + factors[5] * back_ref[below, :]
-                source[2] = source[2] + factors[6] * top
-                solved = solve_inner(source, factors) + (top,)
-                for level in range(LEVELS):
-                    item = field * LEVELS + level
-                    present_ref[item, rows, lanes] = solved[level]
-                    if edges and tile == 0:
-                        edge_refs[0][item, :, lanes] = solved[level][0:2]
-                    if edges and tile == 1:
-                        edge_refs[1][item, :, lanes] = solved[level][6:8]
+        lines = zip(columns(), places(target, COLUMNS, field), places(target, COLUMNS, FIELDS + field), strict=True)
+        for lanes, below, top in lines:
+            factors = [factor_ref[item, field, rows, lanes] for item in range(FACTORS)]
+            source = [explicit_ref[field * LEVELS + level, rows, lanes] for level in range(LEVELS - 1)]
+            top = back_ref[top, :]
+            source[0] = source[0] + factors[5] * back_ref[below, :]
+            source[2] = source[2] + factors[6] * top
+            solved = solve_inner(source, factors) + (top,)
+            for level in range(LEVELS):
+                item = field * LEVELS + level
+                present_ref[item, rows, lanes] = solved[level]
+                if edge_refs and tile == 0:
+                    edge_refs[0][item, :, lanes] = solved[level][0:2]
+                if edge_refs and tile == 1:
+                    edge_refs[1][item, :, lanes] = solved[level][6:8]
+
+
+def finish_kernel(place_ref, factor_ref, explicit_ref, back_ref, present_ref, *edge_refs):
+    for field in range(FIELDS):
+        finish_field(field, place_ref, factor_ref, explicit_ref, back_ref, present_ref, edge_refs)
+
+
+def output_kernel(place_ref, factor_ref, explicit_ref, back_ref, out_ref, present_ref, sems):
+    copies = []
+    for field in range(FIELDS):
+        finish_field(field, place_ref, factor_ref, explicit_ref, back_ref, present_ref)
+        items = pl.ds(field * LEVELS, LEVELS)
+        copies.append(pltpu.make_async_copy(present_ref.at[items], out_ref.at[items], sems.at[field]))
+        copies[-1].start()
+    for copy in copies:
+        copy.wait()
 
 
 VMEM = pl.BlockSpec(memory_space=pltpu.VMEM)
@@ -584,17 +599,30 @@
     )(place, *operands)
 
 
-def finish_part(edges, *operands):
-    shapes = [struct(ITEMS, ROWS, WIDTH)]
-    if edges:
-        shapes += [struct(ITEMS, 2, WIDTH)] * 2
-    return pl.pallas_call(
-        functools.partial(finish_kernel, edges),
-        out_shape=tuple(shapes),
+def finish_part(*operands):
+    edge = struct(ITEMS, 2, WIDTH)
+    return pl.pallas_call(
+        finish_kernel,
+        out_shape=(struct(ITEMS, ROWS, WIDTH), edge, edge),
         in_specs=[SMEM] + [VMEM] * 3,
-        out_specs=(VMEM,) * len(shapes),
+        out_specs=(VMEM,) * 3,
         compiler_params=PARAMS,
         name="finish_part",
+    )(*operands)
+
+
+def output_part(*operands):
+    return pl.pallas_call(
+        output_kernel,
+        out_shape=struct(ITEMS, ROWS, WIDTH),
+        in_specs=[SMEM] + [VMEM] * 3,
+        out_specs=pl.BlockSpec(memory_space=pl.ANY),
+        scratch_shapes=[
+            pltpu.VMEM((ITEMS, ROWS, WIDTH), jnp.float32),
+            pltpu.SemaphoreType.DMA((FIELDS,)),
+        ],
+        compiler_params=PARAMS,
+        name="output_part",
     )(*operands)
 
 
@@ -643,11 +671,11 @@
         else:
             sources, send, ports = reduce_part(got, factors, top)
             (back,) = return_part(place, far(send), sources, factors, ports, top)
-        present, *edges = finish_part(
-            step + 1 < STEPS, place, inner, explicit, near(back).reshape(MEMBERS * COLUMNS * 8, LANES)
-        )
-        if edges:
-            lowest, highest = edges
+        operands = place, inner, explicit, near(back).reshape(MEMBERS * COLUMNS * 8, LANES)
+        if step + 1 < STEPS:
+            present, lowest, highest = finish_part(*operands)
+        else:
+            present = output_part(*operands)
     return present.reshape(fields.shape)
 
 

time: 120 us -> 120 us (level)
  no operation moved by 1% of the time
where the time goes in v9:
time: 120 us; the launch traced here: 119 us
  blocking collectives  104 us (87%)
  Pallas kernels  5.88 us (5%)
  local copies, waits for them, and re-layouts  3.76 us (3%)
  starting transfers between devices  3.5 us (3%)
  waiting for transfers between devices  2.6 us (2%)
    all_to_all x4, blocking collectives, near(): lax.all_to_all(chunks, 'gz', 0, 0, tiled=True, axis_index_groups=near_gro...  63.9 us
    all_to_all x2, blocking collectives, far(): lax.all_to_all(chunks, 'gz', 0, 0, tiled=True, axis_index_groups=far_groups)  39.7 us
    unnamed x14, local copies, waits for them, and re-layouts  3.69 us
  transfers between devices with their start and end apart: 4, of which 2 were waited for; matrix products, arithmetic and copies ran while one was open for 0% of the time, Pallas kernels for 2%

profile of v9, /device:TPU:24, one launch (start us, length us, event | category | flops | bytes accessed | tf_op | source)
XLA Modules:
  0.0 119.4 jit_solution(12311059216645649324)
XLA Ops:
  0.0 0.9 copy-done
  1.0 1.0 copy-done.2
  2.0 0.0 collective-permute-start
  2.1 1.7 %collective-permute-start.1 = (f32[20,2,512]{2,1,0:T(2,128)S(1)}, f32[20,2,512]{2,1,0:T(2,128)S(1)}, u32[]{:S(2)}, u32[]{:S(2)}) collective-permute-start(f32[20,2,512]{2,1,0:T(2,128)S(1)} %get-tuple-element.29), channel_id=1, source_target_pairs={{1,0},{2,1},{3,2},{4,3},{5,4},{6,5},{7,6},{0,7},{9,8},{10,9},{11,1... | collective-permute-start | bytes 245768 | tf_op jit(solution)/shard_map/ppermute | solution.py:643
  3.8 0.7 copy-done.5
  4.4 0.0 copy-done.6
  4.5 0.1 pad_maximum_fusion
  4.5 0.1 broadcast_in_dim.2.scale_ref.refs_0_
  4.6 0.1 factor_part.1.factor_ref
  4.7 0.8 copy-done.1
  5.6 0.2 copy-done.3
  5.7 1.0 interior_part.2.inner_ref
  6.8 0.0 collective-permute-done.south_ref.vel_south_ref
  6.8 1.7 %collective-permute-done.1.north_ref.vel_north_ref = f32[20,2,512]{2,1,0:T(2,128)S(1)} collective-permute-done((f32[20,2,512]{2,1,0:T(2,128)S(1)}, f32[20,2,512]{2,1,0:T(2,128)S(1)}, u32[]{:S(2)}, u32[]{:S(2)}) %collective-permute-start.1) | collective-permute-done | bytes 81952 | tf_op jit(solution)/shard_map/ppermute | solution.py:643
  8.5 0.9 explicit_part.2
  9.4 20.3 %all_to_all.30.got_ref = f32[16,6,8,128]{3,2,1,0:T(8,128)S(1)} all-to-all(f32[16,6,8,128]{3,2,1,0:T(8,128)S(1)} %bitcast.18), channel_id=1, replica_groups={{0,8,16,24,32,40,48,56,64,72,80,88,96,104,112,120},{128,136,144,152,160..., dimensions={0} | all-to-all | bytes 786432 | tf_op jit(solution)/shard_map/all_to_all | solution.py:652
  29.7 0.3 reduce_part.2
  30.0 25.5 %all_to_all.31.got_ref = f32[4,10,8,128]{3,2,1,0:T(8,128)S(1)} all-to-all(f32[4,10,8,128]{3,2,1,0:T(8,128)S(1)} %get-tuple-element.32), channel_id=1, replica_groups={{0,128,320,448},{8,136,328,456},{16,144,336,464},{24,152,344,472},{32,1..., dimensions={0} | all-to-all | bytes 327680 | tf_op jit(solution)/shard_map/all_to_all | solution.py:655
  55.5 0.1 return_part.2
  55.6 14.7 %all_to_all.32 = f32[16,4,8,128]{3,2,1,0:T(8,128)S(1)} all-to-all(f32[16,4,8,128]{3,2,1,0:T(8,128)S(1)} %get-tuple-element.37), channel_id=1, replica_groups={{0,8,16,24,32,40,48,56,64,72,80,88,96,104,112,120},{128,136,144,152,160..., dimensions={0} | all-to-all | bytes 524288 | tf_op jit(solution)/shard_map/all_to_all | solution.py:652
  70.3 0.3 finish_part.1
  70.6 0.0 collective-permute-start.2
  70.6 1.7 %collective-permute-start.3 = (f32[16,2,512]{2,1,0:T(2,128)S(1)}, f32[16,2,512]{2,1,0:T(2,128)S(1)}, u32[]{:S(2)}, u32[]{:S(2)}) collective-permute-start(f32[16,2,512]{2,1,0:T(2,128)S(1)} %get-tuple-element.40), channel_id=1, source_target_pairs={{1,0},{2,1},{3,2},{4,3},{5,4},{6,5},{7,6},{0,7},{9,8},{10,9},{11,1... | collective-permute-start | bytes 196616 | tf_op jit(solution)/shard_map/ppermute | solution.py:661
  72.4 1.0 interior_part.3.inner_ref
  73.4 0.9 collective-permute-done.2.south_ref
  74.3 0.9 explicit_part.3
  75.2 14.7 %all_to_all.33.got_ref = f32[16,4,8,128]{3,2,1,0:T(8,128)S(1)} all-to-all(f32[16,4,8,128]{3,2,1,0:T(8,128)S(1)} %bitcast.19), channel_id=1, replica_groups={{0,8,16,24,32,40,48,56,64,72,80,88,96,104,112,120},{128,136,144,152,160..., dimensions={0} | all-to-all | bytes 524288 | tf_op jit(solution)/shard_map/all_to_all | solution.py:652
  90.0 0.1 reduce_part.3
  90.0 14.2 %all_to_all.34.got_ref = f32[4,2,8,128]{3,2,1,0:T(8,128)S(1)} all-to-all(f32[4,2,8,128]{3,2,1,0:T(8,128)S(1)} %get-tuple-element.44), channel_id=1, replica_groups={{0,128,320,448},{8,136,328,456},{16,144,336,464},{24,152,344,472},{32,1..., dimensions={0} | all-to-all | bytes 65536 | tf_op jit(solution)/shard_map/all_to_all | solution.py:655
  104.2 0.1 return_part.3
  104.3 14.1 %all_to_all.35 = f32[16,4,8,128]{3,2,1,0:T(8,128)S(1)} all-to-all(f32[16,4,8,128]{3,2,1,0:T(8,128)S(1)} %return_part.3), channel_id=1, replica_groups={{0,8,16,24,32,40,48,56,64,72,80,88,96,104,112,120},{128,136,144,152,160..., dimensions={0} | all-to-all | bytes 524288 | tf_op jit(solution)/shard_map/all_to_all | solution.py:652
  118.4 1.0 output_part.1
  (10 shorter events, 0.0 us)
Async XLA Ops:
  0.0 0.9 copy-start
  1.0 1.0 copy-start.2
  2.0 2.6 %copy-start.4 = (f32[4,16,512]{2,1,0:T(8,128)S(1)}, f32[4,16,512]{2,1,0:T(8,128)}, u32[]{:S(2)}) copy-start(f32[4,16,512]{2,1,0:T(8,128)} %face_ref.5) | copy-start | bytes 393220
  2.0 4.8 %collective-permute-start = (f32[20,2,512]{2,1,0:T(2,128)S(1)}, f32[20,2,512]{2,1,0:T(2,128)S(1)}, u32[]{:S(2)}, u32[]{:S(2)}) collective-permute-start(f32[20,2,512]{2,1,0:T(2,128)S(1)} %get-tuple-element.28), channel_id=1, source_target_pairs={{0,1},{1,2},{2,3},{3,4},{4,5},{5,6},{6,7},{7,0},{8,9},{9,10},{10,1... | collective-permute-start | bytes 245768 | tf_op jit(solution)/shard_map/ppermute | solution.py:642
  2.1 6.4 %collective-permute-start.1 = (f32[20,2,512]{2,1,0:T(2,128)S(1)}, f32[20,2,512]{2,1,0:T(2,128)S(1)}, u32[]{:S(2)}, u32[]{:S(2)}) collective-permute-start(f32[20,2,512]{2,1,0:T(2,128)S(1)} %get-tuple-element.29), channel_id=1, source_target_pairs={{1,0},{2,1},{3,2},{4,3},{5,4},{6,5},{7,6},{0,7},{9,8},{10,9},{11,1... | collective-permute-start | bytes 245768 | tf_op jit(solution)/shard_map/ppermute | solution.py:643
  3.8 0.7 copy-start.5
  3.8 0.7 copy-start.6
  4.6 1.0 copy-start.1
  4.6 1.1 copy-start.3
  70.6 3.7 %collective-permute-start.2 = (f32[16,2,512]{2,1,0:T(2,128)S(1)}, f32[16,2,512]{2,1,0:T(2,128)S(1)}, u32[]{:S(2)}, u32[]{:S(2)}) collective-permute-start(f32[16,2,512]{2,1,0:T(2,128)S(1)} %get-tuple-element.39), channel_id=1, source_target_pairs={{0,1},{1,2},{2,3},{3,4},{4,5},{5,6},{6,7},{7,0},{8,9},{9,10},{10,1... | collective-permute-start | bytes 196616 | tf_op jit(solution)/shard_map/ppermute | solution.py:660
  70.6 3.7 %collective-permute-start.3 = (f32[16,2,512]{2,1,0:T(2,128)S(1)}, f32[16,2,512]{2,1,0:T(2,128)S(1)}, u32[]{:S(2)}, u32[]{:S(2)}) collective-permute-start(f32[16,2,512]{2,1,0:T(2,128)S(1)} %get-tuple-element.40), channel_id=1, source_target_pairs={{1,0},{2,1},{3,2},{4,3},{5,4},{6,5},{7,6},{0,7},{9,8},{10,9},{11,1... | collective-permute-start | bytes 196616 | tf_op jit(solution)/shard_map/ppermute | solution.py:661

commit v10 on v9

--- a/solution.py
+++ b/solution.py
@@ -201,6 +201,7 @@
 
     def average(item):
         field, level = divmod(item, LEVELS)
+        explicit_ref[item] = inner_ref[item]
         middle = [sectioned_ref[item, column, 1:9, :] for column in range(COLUMNS)]
         for column, (eastern, western) in enumerate(along_x(middle, last, begin)):
             lanes = slice(column * LANES, column * LANES + LANES)
@@ -219,8 +220,6 @@
             explicit_ref[item, 0:2, lanes] = value[0:2]
             explicit_ref[item, ROWS - 2 : ROWS, lanes] = value[4:6]
 
-    for item in range(ITEMS):
-        explicit_ref[item, 2 : ROWS - 2, :] = inner_ref[item, 2 : ROWS - 2, :]
     for turn in range(ITEMS + 1):
         if turn < ITEMS:
             section(ORDER[turn])
@@ -631,7 +630,7 @@
     up = [(i, (i + 1) % count) for i in range(count)]
     down = [(target, source) for source, target in up]
     scale = jnp.broadcast_to(jnp.concatenate([z_scale, xy_rate])[:, None], (2 * FIELDS, LANES))
-    place = (lax.axis_index("gz") // MEMBERS).astype(jnp.int32).reshape(1)
+    place = lax.shift_right_logical(lax.axis_index("gz"), MEMBERS.bit_length() - 1).astype(jnp.int32).reshape(1)
     scale, place = lax.optimization_barrier((scale, place))
 
     present = fields.reshape(ITEMS, ROWS, WIDTH)

time: 120 us -> 120 us (level)
  no operation moved by 1% of the time
where the time goes in v10:
time: 120 us; the launch traced here: 119 us
  blocking collectives  104 us (87%)
  Pallas kernels  5.88 us (5%)
  local copies, waits for them, and re-layouts  3.76 us (3%)
  starting transfers between devices  3.5 us (3%)
  waiting for transfers between devices  2.6 us (2%)
    all_to_all x4, blocking collectives, near(): lax.all_to_all(chunks, 'gz', 0, 0, tiled=True, axis_index_groups=near_gro...  63.9 us
    all_to_all x2, blocking collectives, far(): lax.all_to_all(chunks, 'gz', 0, 0, tiled=True, axis_index_groups=far_groups)  39.7 us
    unnamed x14, local copies, waits for them, and re-layouts  3.69 us
  transfers between devices with their start and end apart: 4, of which 2 were waited for; matrix products, arithmetic and copies ran while one was open for 0% of the time, Pallas kernels for 2%

profile of v10, /device:TPU:24, one launch (start us, length us, event | category | flops | bytes accessed | tf_op | source)
XLA Modules:
  0.0 119.4 jit_solution(5641560415398552687)
XLA Ops:
  0.0 0.9 copy-done
  1.0 1.0 copy-done.2
  2.0 0.0 collective-permute-start
  2.1 1.7 %collective-permute-start.1 = (f32[20,2,512]{2,1,0:T(2,128)S(1)}, f32[20,2,512]{2,1,0:T(2,128)S(1)}, u32[]{:S(2)}, u32[]{:S(2)}) collective-permute-start(f32[20,2,512]{2,1,0:T(2,128)S(1)} %get-tuple-element.29), channel_id=1, source_target_pairs={{1,0},{2,1},{3,2},{4,3},{5,4},{6,5},{7,6},{0,7},{9,8},{10,9},{11,1... | collective-permute-start | bytes 245768 | tf_op jit(solution)/shard_map/ppermute | solution.py:642
  3.8 0.7 copy-done.5
  4.4 0.0 copy-done.6
  4.5 0.1 pad_maximum_fusion
  4.5 0.1 broadcast_in_dim.2.scale_ref.refs_0_
  4.6 0.1 factor_part.1.factor_ref
  4.7 0.8 copy-done.1
  5.6 0.2 copy-done.3
  5.7 1.0 interior_part.2.inner_ref
  6.8 0.0 collective-permute-done.south_ref.vel_south_ref
  6.8 1.7 %collective-permute-done.1.north_ref.vel_north_ref = f32[20,2,512]{2,1,0:T(2,128)S(1)} collective-permute-done((f32[20,2,512]{2,1,0:T(2,128)S(1)}, f32[20,2,512]{2,1,0:T(2,128)S(1)}, u32[]{:S(2)}, u32[]{:S(2)}) %collective-permute-start.1) | collective-permute-done | bytes 81952 | tf_op jit(solution)/shard_map/ppermute | solution.py:642
  8.5 0.9 explicit_part.2
  9.4 20.3 %all_to_all.30.got_ref = f32[16,6,8,128]{3,2,1,0:T(8,128)S(1)} all-to-all(f32[16,6,8,128]{3,2,1,0:T(8,128)S(1)} %bitcast.18), channel_id=1, replica_groups={{0,8,16,24,32,40,48,56,64,72,80,88,96,104,112,120},{128,136,144,152,160..., dimensions={0} | all-to-all | bytes 786432 | tf_op jit(solution)/shard_map/all_to_all | solution.py:651
  29.7 0.3 reduce_part.2
  30.0 25.5 %all_to_all.31.got_ref = f32[4,10,8,128]{3,2,1,0:T(8,128)S(1)} all-to-all(f32[4,10,8,128]{3,2,1,0:T(8,128)S(1)} %get-tuple-element.32), channel_id=1, replica_groups={{0,128,320,448},{8,136,328,456},{16,144,336,464},{24,152,344,472},{32,1..., dimensions={0} | all-to-all | bytes 327680 | tf_op jit(solution)/shard_map/all_to_all | solution.py:654
  55.5 0.1 return_part.2
  55.6 14.7 %all_to_all.32 = f32[16,4,8,128]{3,2,1,0:T(8,128)S(1)} all-to-all(f32[16,4,8,128]{3,2,1,0:T(8,128)S(1)} %get-tuple-element.37), channel_id=1, replica_groups={{0,8,16,24,32,40,48,56,64,72,80,88,96,104,112,120},{128,136,144,152,160..., dimensions={0} | all-to-all | bytes 524288 | tf_op jit(solution)/shard_map/all_to_all | solution.py:651
  70.3 0.3 finish_part.1
  70.6 0.0 collective-permute-start.2
  70.6 1.7 %collective-permute-start.3 = (f32[16,2,512]{2,1,0:T(2,128)S(1)}, f32[16,2,512]{2,1,0:T(2,128)S(1)}, u32[]{:S(2)}, u32[]{:S(2)}) collective-permute-start(f32[16,2,512]{2,1,0:T(2,128)S(1)} %get-tuple-element.40), channel_id=1, source_target_pairs={{1,0},{2,1},{3,2},{4,3},{5,4},{6,5},{7,6},{0,7},{9,8},{10,9},{11,1... | collective-permute-start | bytes 196616 | tf_op jit(solution)/shard_map/ppermute | solution.py:660
  72.3 1.0 interior_part.3.inner_ref
  73.4 0.9 collective-permute-done.2.south_ref
  74.3 0.9 explicit_part.3
  75.2 14.7 %all_to_all.33.got_ref = f32[16,4,8,128]{3,2,1,0:T(8,128)S(1)} all-to-all(f32[16,4,8,128]{3,2,1,0:T(8,128)S(1)} %bitcast.19), channel_id=1, replica_groups={{0,8,16,24,32,40,48,56,64,72,80,88,96,104,112,120},{128,136,144,152,160..., dimensions={0} | all-to-all | bytes 524288 | tf_op jit(solution)/shard_map/all_to_all | solution.py:651
  90.0 0.1 reduce_part.3
  90.0 14.2 %all_to_all.34.got_ref = f32[4,2,8,128]{3,2,1,0:T(8,128)S(1)} all-to-all(f32[4,2,8,128]{3,2,1,0:T(8,128)S(1)} %get-tuple-element.44), channel_id=1, replica_groups={{0,128,320,448},{8,136,328,456},{16,144,336,464},{24,152,344,472},{32,1..., dimensions={0} | all-to-all | bytes 65536 | tf_op jit(solution)/shard_map/all_to_all | solution.py:654
  104.2 0.1 return_part.3
  104.3 14.1 %all_to_all.35 = f32[16,4,8,128]{3,2,1,0:T(8,128)S(1)} all-to-all(f32[16,4,8,128]{3,2,1,0:T(8,128)S(1)} %return_part.3), channel_id=1, replica_groups={{0,8,16,24,32,40,48,56,64,72,80,88,96,104,112,120},{128,136,144,152,160..., dimensions={0} | all-to-all | bytes 524288 | tf_op jit(solution)/shard_map/all_to_all | solution.py:651
  118.4 1.0 output_part.1
  (10 shorter events, 0.0 us)
Async XLA Ops:
  0.0 0.9 copy-start
  1.0 1.0 copy-start.2
  2.0 2.6 %copy-start.4 = (f32[4,16,512]{2,1,0:T(8,128)S(1)}, f32[4,16,512]{2,1,0:T(8,128)}, u32[]{:S(2)}) copy-start(f32[4,16,512]{2,1,0:T(8,128)} %face_ref.5) | copy-start | bytes 393220
  2.0 4.8 %collective-permute-start = (f32[20,2,512]{2,1,0:T(2,128)S(1)}, f32[20,2,512]{2,1,0:T(2,128)S(1)}, u32[]{:S(2)}, u32[]{:S(2)}) collective-permute-start(f32[20,2,512]{2,1,0:T(2,128)S(1)} %get-tuple-element.28), channel_id=1, source_target_pairs={{0,1},{1,2},{2,3},{3,4},{4,5},{5,6},{6,7},{7,0},{8,9},{9,10},{10,1... | collective-permute-start | bytes 245768 | tf_op jit(solution)/shard_map/ppermute | solution.py:641
  2.1 6.4 %collective-permute-start.1 = (f32[20,2,512]{2,1,0:T(2,128)S(1)}, f32[20,2,512]{2,1,0:T(2,128)S(1)}, u32[]{:S(2)}, u32[]{:S(2)}) collective-permute-start(f32[20,2,512]{2,1,0:T(2,128)S(1)} %get-tuple-element.29), channel_id=1, source_target_pairs={{1,0},{2,1},{3,2},{4,3},{5,4},{6,5},{7,6},{0,7},{9,8},{10,9},{11,1... | collective-permute-start | bytes 245768 | tf_op jit(solution)/shard_map/ppermute | solution.py:642
  3.8 0.7 copy-start.5
  3.8 0.7 copy-start.6
  4.6 1.0 copy-start.1
  4.6 1.1 copy-start.3
  70.6 3.7 %collective-permute-start.2 = (f32[16,2,512]{2,1,0:T(2,128)S(1)}, f32[16,2,512]{2,1,0:T(2,128)S(1)}, u32[]{:S(2)}, u32[]{:S(2)}) collective-permute-start(f32[16,2,512]{2,1,0:T(2,128)S(1)} %get-tuple-element.39), channel_id=1, source_target_pairs={{0,1},{1,2},{2,3},{3,4},{4,5},{5,6},{6,7},{7,0},{8,9},{9,10},{10,1... | collective-permute-start | bytes 196616 | tf_op jit(solution)/shard_map/ppermute | solution.py:659
  70.6 3.7 %collective-permute-start.3 = (f32[16,2,512]{2,1,0:T(2,128)S(1)}, f32[16,2,512]{2,1,0:T(2,128)S(1)}, u32[]{:S(2)}, u32[]{:S(2)}) collective-permute-start(f32[16,2,512]{2,1,0:T(2,128)S(1)} %get-tuple-element.40), channel_id=1, source_target_pairs={{1,0},{2,1},{3,2},{4,3},{5,4},{6,5},{7,6},{0,7},{9,8},{10,9},{11,1... | collective-permute-start | bytes 196616 | tf_op jit(solution)/shard_map/ppermute | solution.py:660
